TPU v7x, 32 devices: a whole 2x2x4 slice. The times are simulated.
32 devices in a mesh: dp: 2 (over core), expert: 16 (over z, y, x).
Axes of the slice: x: 2, y: 2, z: 4, core: 2. Of those that a mesh axis runs over, the one named last changes fastest.
Arguments:
- tokens: bfloat16 [4096, 1152], P(('dp', 'expert')), may hold values from -6 to 6
- out_grad: bfloat16 [4096, 1152], P(('dp', 'expert')), may hold values from -6 to 6
- gates: float32 [4096, 2], P(('dp', 'expert')), may hold values from 0.05 to 1
- expert_ids: int32 [4096, 2], P(('dp', 'expert')), may hold values from 0 to 15, all different within a row; in each aligned block of 128 rows (0 to 127, 128 to 255, ...) at most 24 rows name the same one
- swap_list: int32 [16], replicated, may hold values from 0 to 15, as said below
- w_in: bfloat16 [16, 1152, 3072], P('expert', None, 'dp'), may hold values from -0.1875 to 0.1875
- w_out: bfloat16 [16, 3072, 1152], P('expert', 'dp'), may hold values from -0.109375 to 0.109375
- first_moment: float32 [16, 1152, 3072], P('expert', None, 'dp'), may hold values from -12 to 12
- second_moment: float32 [16, 1152, 3072], P('expert', None, 'dp'), may hold values from 1 to 100
Outputs:
- x_grad: bfloat16 [4096, 1152], P(('dp', 'expert'))
- adam_out: bfloat16 [16, 1152, 3072], P('expert', None, 'dp')
Inputs may be any that keep to these rules, and one draw needn't show every extreme that they name: `expert_ids`: among the 128 tokens of one device no expert is named by more than 24 rows; a token's two experts differ. swap_list[e] is e or e XOR 16/2, and swap_list[swap_list[e]] = e; swap_list[0] = 8 and swap_list[15] = 7.
All inputs are finite; a program needn't handle non-finite values.
Results may differ from a plain program's by a relative error of at most 0.015.
Values may be sent and summed in bfloat16 or wider, within the bound.
No kernel may reach another device: no remote copies, remote signals or barrier semaphores. Data moves between devices by JAX's collectives and lax.ppermute only.
A program may use at most 128 MiB of HBM per device.

v0:
```python
import functools
import itertools
import math

import jax
import jax.numpy as jnp
from jax import lax
from jax.experimental import pallas as pl
from jax.experimental.pallas import tpu as pltpu
from jax.sharding import PartitionSpec as P

ADAM_STEP = 100


coef_c = 0.7978845608028654
coef_a = 0.044715
beta_one = 0.9
beta_two = 0.999
adam_eps = 1e-08


VMEM_LIMIT = 60 * 1024 * 1024

f32 = jnp.float32
bf16 = jnp.bfloat16
NN = (((1,), (0,)), ((), ()))
NT = (((1,), (1,)), ((), ()))
TN = (((0,), (0,)), ((), ()))


def mxu(a, b, dims):
    return lax.dot_general(a, b, dims, preferred_element_type=f32)


def gelu_slope(pre_act):
    inner_arg = coef_c * (pre_act + coef_a * pre_act * pre_act * pre_act)
    tanh_val = jnp.tanh(inner_arg)
    return 0.5 * (1.0 + tanh_val) + 0.5 * pre_act * (1.0 - tanh_val * tanh_val) * coef_c * (
        1.0 + 3.0 * coef_a * pre_act * pre_act
    )


def adam_step(weight_grad, first_moment, second_moment):
    first_new = beta_one * first_moment + (1.0 - beta_one) * weight_grad
    second_new = beta_two * second_moment + (1.0 - beta_two) * weight_grad * weight_grad
    return (
        first_new
        / (1.0 - beta_one**ADAM_STEP)
        / (jnp.sqrt(second_new / (1.0 - beta_two**ADAM_STEP)) + adam_eps)
    ).astype(bf16)


def pack_kernel(expert_count, capacity, ids_ref, gates_ref, x_ref, g_ref, rows_ref, where_ref):
    tok_count, width = x_ref.shape
    slots = expert_count * capacity
    first = ids_ref[0:1, :]
    second = ids_ref[1:2, :]
    experts = lax.broadcasted_iota(jnp.int32, (expert_count, tok_count), 0)
    hit_first = experts == first
    hit_second = experts == second
    hits = jnp.where(hit_first | hit_second, 1.0, 0.0).astype(bf16)
    earlier = lax.broadcasted_iota(jnp.int32, (tok_count, tok_count), 0)
    later = lax.broadcasted_iota(jnp.int32, (tok_count, tok_count), 1)
    upper = jnp.where(earlier < later, 1.0, 0.0).astype(bf16)
    before = mxu(hits, upper, NN)
    slot_first = jnp.sum(jnp.where(hit_first, before, 0.0), axis=0, keepdims=True)
    slot_second = jnp.sum(jnp.where(hit_second, before, 0.0), axis=0, keepdims=True)
    pos_first = first * capacity + slot_first.astype(jnp.int32)
    pos_second = second * capacity + slot_second.astype(jnp.int32)
    where_ref[0:1, :] = pos_first
    where_ref[1:2, :] = pos_second
    row = lax.broadcasted_iota(jnp.int32, (slots, tok_count), 0)
    at_first = row == pos_first
    at_second = row == pos_second
    pick = jnp.where(at_first | at_second, 1.0, 0.0).astype(bf16)
    gate = jnp.sum(
        jnp.where(at_first, gates_ref[0:1, :], 0.0) + jnp.where(at_second, gates_ref[1:2, :], 0.0),
        axis=1,
        keepdims=True,
    )
    rows_ref[:, :width] = mxu(pick, x_ref[...], NN).astype(bf16)
    rows_ref[:, width:] = (gate * mxu(pick, g_ref[...], NN)).astype(bf16)


def pack_rows(id_rows, gate_rows, tokens, out_grad, expert_count, capacity):
    tok_count, width = tokens.shape
    slots = expert_count * capacity
    return pl.pallas_call(
        functools.partial(pack_kernel, expert_count, capacity),
        out_shape=(
            jax.ShapeDtypeStruct((slots, 2 * width), bf16),
            jax.ShapeDtypeStruct((2, tok_count), jnp.int32),
        ),
        name="pack_rows",
    )(id_rows, gate_rows, tokens, out_grad)


def pre_tile(rows, w_in, w_out, pre_ref):
    per, width = rows[0].shape[0], rows[0].shape[1] // 2
    for b, block in enumerate(rows):
        pre_act = mxu(block[:, :width], w_in, NN)
        act_grad = mxu(block[:, width:], w_out, NT)
        pre_ref[b * per : (b + 1) * per, :] = (act_grad * gelu_slope(pre_act)).astype(bf16)


def first_kernel(blocks, *refs):
    rows = refs[:blocks]
    w_in_ref, w_out_ref, m_ref, v_ref, adam_ref, pre_ref, xt_ref = refs[blocks:]
    width, per = m_ref.shape[0], rows[0].shape[0]
    for b in range(blocks):
        xt_ref[:, b * per : (b + 1) * per] = rows[b][:, :width].T
    pre_tile(rows, w_in_ref[...], w_out_ref[...], pre_ref)
    weight_grad = mxu(xt_ref[...], pre_ref[...], NN)
    adam_ref[...] = adam_step(weight_grad, m_ref[...], v_ref[...])


def first_step(rows, w_in, w_out, first_moment, second_moment, tile):
    per, width = rows[0].shape[0], rows[0].shape[1] // 2
    total = len(rows) * per
    corner = lambda i: (0, 0)
    columns = pl.BlockSpec((width, tile), corner)
    return pl.pallas_call(
        functools.partial(first_kernel, len(rows)),
        grid=(1,),
        in_specs=[pl.BlockSpec(r.shape, corner) for r in rows]
        + [columns, pl.BlockSpec((tile, width), corner), columns, columns],
        out_specs=[
            columns,
            pl.BlockSpec((total, tile), corner),
            pl.BlockSpec((width, total), corner),
        ],
        out_shape=[
            jax.ShapeDtypeStruct((width, tile), bf16),
            jax.ShapeDtypeStruct((total, tile), bf16),
            jax.ShapeDtypeStruct((width, total), bf16),
        ],
        compiler_params=pltpu.CompilerParams(vmem_limit_bytes=VMEM_LIMIT),
        cost_estimate=pl.CostEstimate(
            flops=6 * total * width * tile, bytes_accessed=14 * tile * width, transcendentals=0
        ),
        name="first_step",
    )(*rows, w_in, w_out, first_moment, second_moment)


def rest_kernel(blocks, *refs):
    rows = refs[:blocks]
    first_ref, w_first_ref, w_in_ref, w_out_ref, pre_ref = refs[blocks : blocks + 5]
    parts = refs[blocks + 5 : -1]
    total_ref = refs[-1]
    per = rows[0].shape[0]
    step = pl.program_id(0)

    @pl.when(step == 0)
    def _():
        total_ref[...] = mxu(first_ref[...], w_first_ref[...], NT)

    pre_tile(rows, w_in_ref[...], w_out_ref[...], pre_ref)
    total_ref[...] += mxu(pre_ref[...], w_in_ref[...], NT)

    @pl.when(step == pl.num_programs(0) - 1)
    def _():
        for b in range(blocks):
            parts[b][...] = total_ref[b * per : (b + 1) * per, :].astype(bf16)


def rest_step(rows, pre_first, w_in, w_out, tile):
    per, width = rows[0].shape[0], rows[0].shape[1] // 2
    total = len(rows) * per
    tiles = w_in.shape[1] // tile - 1
    corner = lambda j: (0, 0)
    return pl.pallas_call(
        functools.partial(rest_kernel, len(rows)),
        grid=(tiles,),
        in_specs=[pl.BlockSpec(r.shape, corner) for r in rows]
        + [
            pl.BlockSpec((total, tile), corner),
            pl.BlockSpec((width, tile), corner),
            pl.BlockSpec((width, tile), lambda j: (0, j + 1)),
            pl.BlockSpec((tile, width), lambda j: (j + 1, 0)),
        ],
        out_specs=[pl.BlockSpec((total, tile), lambda j: (0, j))]
        + [pl.BlockSpec((per, width), corner) for _ in rows],
        out_shape=[jax.ShapeDtypeStruct((total, tiles * tile), bf16)]
        + [jax.ShapeDtypeStruct((per, width), bf16) for _ in rows],
        scratch_shapes=[pltpu.VMEM((total, width), f32)],
        compiler_params=pltpu.CompilerParams(vmem_limit_bytes=VMEM_LIMIT),
        cost_estimate=pl.CostEstimate(
            flops=6 * total * width * tile * tiles,
            bytes_accessed=4 * tile * width * tiles,
            transcendentals=0,
        ),
        name="rest_step",
    )(*rows, pre_first, w_in, w_in, w_out)


def adam_kernel(xt_ref, pre_ref, m_ref, v_ref, *outs):
    weight_grad = mxu(xt_ref[...], pre_ref[...], NN)
    step = adam_step(weight_grad, m_ref[...], v_ref[...])
    at = 0
    for out in outs:
        out[...] = step[at : at + out.shape[0], :]
        at += out.shape[0]


def adam_columns(x_t, pre_rest, first_moment, second_moment, start, tiles, tile, pieces):
    width, total = x_t.shape
    rows = width // pieces
    columns = pl.BlockSpec((width, tile), lambda j: (0, start + j))
    return pl.pallas_call(
        adam_kernel,
        grid=(tiles,),
        in_specs=[
            pl.BlockSpec((width, total), lambda j: (0, 0)),
            pl.BlockSpec((total, tile), lambda j: (0, start - 1 + j)),
            columns,
            columns,
        ],
        out_specs=[pl.BlockSpec((rows, tile), lambda j: (0, j)) for _ in range(pieces)],
        out_shape=[jax.ShapeDtypeStruct((rows, tiles * tile), bf16) for _ in range(pieces)],
        compiler_params=pltpu.CompilerParams(vmem_limit_bytes=VMEM_LIMIT),
        cost_estimate=pl.CostEstimate(
            flops=2 * total * width * tile * tiles,
            bytes_accessed=10 * tile * width * tiles,
            transcendentals=0,
        ),
        name="adam_columns",
    )(x_t, pre_rest, first_moment, second_moment)


def place_kernel(boxes, rows, moved_ref, *refs):
    out_ref = refs[-1]
    step = pl.program_id(0)
    for n, (row, col, high, wide) in enumerate(boxes):
        inside = (step >= row // rows) & (step < (row + high) // rows)

        @pl.when(inside & (moved_ref[0] == 0))
        def _(n=n, col=col, wide=wide):
            out_ref[:, col : col + wide] = refs[2 * n][...]

        @pl.when(inside & (moved_ref[0] != 0))
        def _(n=n, col=col, wide=wide):
            out_ref[:, col : col + wide] = refs[2 * n + 1][...]


def place(moved, pieces, width, inner, rows):
    boxes = [piece[:4] for piece in pieces]
    in_specs, args = [], []

    def spec(row, high, wide, wanted):
        def block(i, moved_ref):
            near = jnp.clip(i - row // rows, 0, high // rows - 1)
            return (jnp.where(moved_ref[0] == wanted, near, 0), 0)

        return pl.BlockSpec((rows, wide), block)

    for row, col, high, wide, kept, got in pieces:
        in_specs += [spec(row, high, wide, 0), spec(row, high, wide, 1)]
        args += [kept, got]
    return pl.pallas_call(
        functools.partial(place_kernel, boxes, rows),
        grid_spec=pltpu.PrefetchScalarGridSpec(
            num_scalar_prefetch=1,
            grid=(width // rows,),
            in_specs=in_specs,
            out_specs=pl.BlockSpec((rows, inner), lambda i, moved_ref: (i, 0)),
        ),
        out_shape=jax.ShapeDtypeStruct((width, inner), bf16),
        name="place",
    )(moved, *args)


def swap_plans(half):
    line = half >> 1
    groups = {}
    for e in range(half):
        groups.setdefault(e & ~(line | 1), []).append(e)
    groups = list(groups.values())
    forced = {0, half - 1}
    size = len(groups[0])

    def sets(members, k):
        must = forced & set(members)
        return [set(s) for s in itertools.combinations(members, k) if must <= set(s)]

    choices = [[sets(g, k) for g in groups] for k in range(1, size + 1)]
    if half < 4 or sum(math.prod(len(c) for c in by_k) for by_k in choices) > 32:
        return None, None
    plans = [set().union(*picked) for by_k in choices for picked in itertools.product(*by_k)]
    table = []
    for mask in range(1 << half):
        moved = forced | {e for e in range(half) if mask >> e & 1}
        table.append(next(n for n, plan in enumerate(plans) if moved <= plan))
    return plans, table


def combine_kernel(where_ref, back_ref, out_ref):
    slots, tok_count = back_ref.shape[0], out_ref.shape[0]
    row = lax.broadcasted_iota(jnp.int32, (slots, tok_count), 0)
    pick = (row == where_ref[0:1, :]) | (row == where_ref[1:2, :])
    pick = jnp.where(pick, 1.0, 0.0).astype(bf16)
    out_ref[...] = mxu(pick, back_ref[...], TN).astype(bf16)


def combine_rows(where_to, returned, tok_count):
    return pl.pallas_call(
        combine_kernel,
        out_shape=jax.ShapeDtypeStruct((tok_count, returned.shape[1]), bf16),
        name="combine_rows",
    )(where_to, returned)


def dp_shift(block, apart):
    count = lax.axis_size("dp")
    return lax.ppermute(block, "dp", [(i, i ^ apart) for i in range(count)])


def shards(
    tokens, out_grad, gates, expert_ids, swap_list, w_in, w_out, first_moment, second_moment
):
    expert_count = lax.axis_size("expert")
    dp_count = lax.axis_size("dp")
    half = 1 << (expert_count.bit_length() - 2)
    own_index = lax.axis_index("expert")
    lane_ids = jnp.arange(expert_count, dtype=jnp.int32)
    partner_me = jnp.sum(jnp.where(lane_ids == own_index, swap_list, 0))
    is_moved = (partner_me != own_index).astype(jnp.int32).reshape(1)
    moved_bits = jnp.where((swap_list != lane_ids) & (lane_ids < half), 1 << lane_ids, 0)
    moved_mask = jnp.sum(moved_bits)
    tok_count, width = tokens.shape
    capacity = 3 * tok_count // expert_count
    slots = expert_count * capacity

    rows, where_to = pack_rows(expert_ids.T, gates.T, tokens, out_grad, expert_count, capacity)
    own = lax.all_to_all(
        rows.reshape(expert_count, capacity, 2 * width),
        "expert",
        split_axis=0,
        concat_axis=0,
        tiled=True,
    ).reshape(slots, 2 * width)
    all_rows = [own] + [dp_shift(own, d) for d in range(1, dp_count)]

    inner = w_in.shape[2]
    tile = 256 if inner % 256 == 0 else 128
    tiles = inner // tile
    plans, table = swap_plans(half)
    route = [(e, e ^ half) for e in range(expert_count)]
    across = [(e, e ^ 1) for e in range(expert_count)]

    first, pre_first, x_t = first_step(
        all_rows, w_in[0], w_out[0], first_moment[0], second_moment[0], tile
    )
    first_got = lax.ppermute(first, "expert", route)
    pieces = [(0, 0, width, tile, first, first_got)]

    pre_rest, *parts = rest_step(all_rows, pre_first, w_in[0], w_out[0], tile)
    total = parts[0].astype(f32)
    for d in range(1, dp_count):
        total = total + dp_shift(parts[d], d).astype(f32)
    returned = lax.all_to_all(
        total.astype(bf16).reshape(expert_count, capacity, width),
        "expert",
        split_axis=0,
        concat_axis=0,
        tiled=True,
    ).reshape(slots, width)

    chunks = [n for n in (2 * (tiles - 1) // 5, tiles - 1 - 2 * (tiles - 1) // 5) if n > 0]
    at = 1
    near, far, boxes = [], [], []
    for n in chunks:
        done = adam_columns(
            x_t, pre_rest, first_moment[0], second_moment[0], at, n, tile, 2 if plans else 1
        )
        if plans:
            near.append(done[0])
            far.append(done[1])
            boxes.append((at * tile, n * tile))
        else:
            got = lax.ppermute(done[0], "expert", route)
            pieces.append((0, at * tile, width, n * tile, done[0], got))
        at += n
    if plans:
        lent = [lax.ppermute(f, "expert", across) for f in far]

        def branch(plan):
            pairs = [(e, e ^ half) for p in plan for e in (p, p ^ half)]
            skew = [(e ^ 1, f) for e, f in pairs]

            def run(near, lent):
                return (
                    [lax.ppermute(a, "expert", pairs) for a in near],
                    [lax.ppermute(b, "expert", skew) for b in lent],
                )

            return run

        choice = jnp.asarray(table, jnp.int32)[moved_mask]
        near_got, far_got = lax.switch(choice, [branch(p) for p in plans], near, lent)
        for n, (col, wide) in enumerate(boxes):
            pieces.append((0, col, width // 2, wide, near[n], near_got[n]))
            pieces.append((width // 2, col, width // 2, wide, far[n], far_got[n]))

    x_grad = combine_rows(where_to, returned, tok_count)
    adam_out = place(is_moved, pieces, width, inner, width // 8)
    return (x_grad, adam_out[None])


def solution(mesh):
    in_specs = (
        P(("dp", "expert"), None),
        P(("dp", "expert"), None),
        P(("dp", "expert"), None),
        P(("dp", "expert"), None),
        P(),
        P("expert", None, "dp"),
        P("expert", "dp", None),
        P("expert", None, "dp"),
        P("expert", None, "dp"),
    )
    out_specs = (P(("dp", "expert"), None), P("expert", None, "dp"))
    return jax.shard_map(shards, mesh=mesh, in_specs=in_specs, out_specs=out_specs, check_vma=False)
```

profile of v0, /device:TPU:0, one launch (start us, length us, event | category | flops | bytes accessed | tf_op | source)
XLA Modules:
  0.0 224.3 jit_solution(13731863318672537914)
XLA Ops:
  0.6 3.1 %pack_rows.1 = (bf16[384,2304]{1,0:T(8,128)(2,1)}, s32[2,128]{1,0:T(2,128)}) custom-call(s32[2,128]{1,0:T(2,128)} %bitcast.30, f32[2,128]{1,0:T(2,128)} %bitcast.31, bf16[128,1152]{1,0:T(8,128)(2,1)} %x_ref.1, bf16[128,1152]{1,0:T(8,128)(2,1)} %g_ref.1), custom_call_target="tpu_custom_call" | custom-call | tf_op jit(solution)/shard_map/pack_rows/pallas_call | solution.py:88
  3.7 50.8 %all_to_all.10 = bf16[16,24,2304]{2,1,0:T(8,128)(2,1)S(1)} all-to-all(bf16[16,24,2304]{2,1,0:T(8,128)(2,1)} %bitcast.29), channel_id=1, replica_groups=mesh['dp'=2,'expert'=16] {'expert'}, dimensions={0} | all-to-all | bytes 3538944 | tf_op jit(solution)/shard_map/all_to_all | solution.py:334
  54.5 0.0 collective-permute-start.80
  54.5 3.7 %collective-permute-done.80.refs_1_ = bf16[384,2304]{1,0:T(8,128)(2,1)S(1)} collective-permute-done((bf16[384,2304]{1,0:T(8,128)(2,1)S(1)}, bf16[384,2304]{1,0:T(8,128)(2,1)S(1)}, u32[]{:S(2)}, u32[]{:S(2)}) %collective-permute-start.80) | collective-permute-done | bytes 1769504 | tf_op jit(solution)/shard_map/ppermute | solution.py:314
  58.2 1.3 copy-done.2
  59.5 6.6 %first_step.1 = (bf16[1152,256]{1,0:T(8,128)(2,1)}, bf16[768,256]{1,0:T(8,128)(2,1)}, bf16[1152,768]{1,0:T(8,128)(2,1)}) custom-call(bf16[384,2304]{1,0:T(8,128)(2,1)} %bitcast.20, bf16[384,2304]{1,0:T(8,128)(2,1)} %copy-done.2, bf16[1152,1536]{1,0:T(8,128)(2,1)} %bitcast.22, bf16[1536,1152]{1,0:T(8,128)(2,1)} %bitcast.25, f32[1152,1536]{1,0:T(8,128)} %bitcast.13, ...), custom_call_target="tpu_custom_call" | custom-call | flops 1358954496 | bytes 4128768 | tf_op jit(solution)/shard_map/first_step/pallas_call | solution.py:122
  66.1 14.6 %rest_step.1 = (bf16[768,1280]{1,0:T(8,128)(2,1)}, bf16[384,1152]{1,0:T(8,128)(2,1)}, bf16[384,1152]{1,0:T(8,128)(2,1)}) custom-call(bf16[384,2304]{1,0:T(8,128)(2,1)} %bitcast.21, bf16[384,2304]{1,0:T(8,128)(2,1)} %copy-done.2, bf16[768,256]{1,0:T(8,128)(2,1)} %get-tuple-element.260.refs_2_, bf16[1152,1536]{1,0:T(8,128)(2,1)} %bitcast.23, ...), custom_call_target="tpu_custom_call" | custom-call | flops 6794772480 | bytes 5898240 | tf_op jit(solution)/shard_map/rest_step/pallas_call | solution.py:171
  80.7 0.1 collective-permute-start.81
  80.8 2.5 %collective-permute-done.81 = bf16[384,1152]{1,0:T(8,128)(2,1)S(1)} collective-permute-done((bf16[384,1152]{1,0:T(8,128)(2,1)}, bf16[384,1152]{1,0:T(8,128)(2,1)S(1)}, u32[]{:S(2)}, u32[]{:S(2)}) %collective-permute-start.81) | collective-permute-done | bytes 884768 | tf_op jit(solution)/shard_map/ppermute | solution.py:314
  83.3 2.3 %add_convert_fusion = bf16[384,1152]{1,0:T(8,128)(2,1)} fusion(bf16[384,1152]{1,0:T(8,128)(2,1)S(1)} %collective-permute-done.81, bf16[384,1152]{1,0:T(8,128)(2,1)} %get-tuple-element.261), kind=kLoop, calls=%fused_computation | loop fusion | flops 1769472 | bytes 2654208 | tf_op jit(solution)/shard_map/convert_element_type | solution.py:361
  85.7 3.6 %all-to-all-start.1 = ((bf16[16,24,1152]{2,1,0:T(8,128)(2,1)}), bf16[16,24,1152]{2,1,0:T(8,128)(2,1)S(1)}, u32[]{:S(2)}, u32[]{:S(2)}) async-start(bf16[16,24,1152]{2,1,0:T(8,128)(2,1)} %bitcast.8), calls=%async_computation.1 | async-start | bytes 1769472 | tf_op jit(solution)/shard_map/all_to_all | solution.py:360
  89.3 7.8 %adam_columns.3 = (bf16[576,768]{1,0:T(8,128)(2,1)S(1)}, bf16[576,768]{1,0:T(8,128)(2,1)}) custom-call(bf16[1152,768]{1,0:T(8,128)(2,1)} %get-tuple-element.264.xt_ref, bf16[768,1280]{1,0:T(8,128)(2,1)} %get-tuple-element.265.pre_ref, f32[1152,1536]{1,0:T(8,128)} %bitcast.14, f32[1152,1536]{1,0:T(8,128)} %bitcast.17), custom_call_target="tpu_custom_call" | custom-call | flops 1358954496 | bytes 8847360 | tf_op jit(solution)/shard_map/adam_columns/pallas_call | solution.py:209
  97.1 5.7 %collective-permute-start.84 = (bf16[576,768]{1,0:T(8,128)(2,1)}, bf16[576,768]{1,0:T(8,128)(2,1)}, u32[]{:S(2)}, u32[]{:S(2)}) collective-permute-start(bf16[576,768]{1,0:T(8,128)(2,1)} %get-tuple-element.269.refs_8_), channel_id=1, source_target_pairs={{0,1},{1,0},{2,3},{3,2},{4,5},{5,4},{6,7},{7,6},{8,9},{9,8},{10,11... | collective-permute-start | bytes 2654216 | tf_op jit(solution)/shard_map/ppermute | solution.py:384
  102.8 5.9 %adam_columns.2 = (bf16[576,512]{1,0:T(8,128)(2,1)S(1)}, bf16[576,512]{1,0:T(8,128)(2,1)}) custom-call(bf16[1152,768]{1,0:T(8,128)(2,1)} %get-tuple-element.264.xt_ref, bf16[768,1280]{1,0:T(8,128)(2,1)} %get-tuple-element.265.pre_ref, f32[1152,1536]{1,0:T(8,128)} %bitcast.15, f32[1152,1536]{1,0:T(8,128)} %bitcast.18), custom_call_target="tpu_custom_call" | custom-call | flops 905969664 | bytes 5898240 | tf_op jit(solution)/shard_map/adam_columns/pallas_call | solution.py:209
  108.8 5.7 %collective-permute-start.83 = (bf16[576,512]{1,0:T(8,128)(2,1)}, bf16[576,512]{1,0:T(8,128)(2,1)}, u32[]{:S(2)}, u32[]{:S(2)}) collective-permute-start(bf16[576,512]{1,0:T(8,128)(2,1)} %get-tuple-element.268.refs_4_), channel_id=1, source_target_pairs={{0,1},{1,0},{2,3},{3,2},{4,5},{5,4},{6,7},{7,6},{8,9},{9,8},{10,11... | collective-permute-start | bytes 1769480 | tf_op jit(solution)/shard_map/ppermute | solution.py:384
  114.5 5.7 %collective-permute-start.82 = (bf16[1152,256]{1,0:T(8,128)(2,1)S(1)}, bf16[1152,256]{1,0:T(8,128)(2,1)S(1)}, u32[]{:S(2)}, u32[]{:S(2)}) collective-permute-start(bf16[1152,256]{1,0:T(8,128)(2,1)S(1)} %copy-done.3), channel_id=1, source_target_pairs={{0,8},{1,9},{2,10},{3,11},{4,12},{5,13},{6,14},{7,15},{8,0},{9,1},... | collective-permute-start | bytes 1769480 | tf_op jit(solution)/shard_map/ppermute | solution.py:353
  120.2 0.6 fusion.1
  123.4 0.6 dynamic_slice.3
  124.7 15.3 %collective-permute-done.83 = bf16[576,512]{1,0:T(8,128)(2,1)} collective-permute-done((bf16[576,512]{1,0:T(8,128)(2,1)}, bf16[576,512]{1,0:T(8,128)(2,1)}, u32[]{:S(2)}, u32[]{:S(2)}) %collective-permute-start.83) | collective-permute-done | bytes 589856 | tf_op jit(solution)/shard_map/ppermute | solution.py:384
  140.0 73.5 %conditional.1 = (bf16[576,512]{1,0:T(8,128)(2,1)}, bf16[576,768]{1,0:T(8,128)(2,1)}, bf16[576,512]{1,0:T(8,128)(2,1)}, bf16[576,768]{1,0:T(8,128)(2,1)}) conditional(s32[]{:T(128)} %bitcast.11, (bf16[576,512]{1,0:T(8,128)(2,1)S(1)}, bf16[576,768]{1,0:T(8,128)(2,1)S(1)}, bf16[576,512]{1,0:T(8,128)(2,1)}, ...), branch_computations={%region_2.3_spmd, %region_3.4_spmd, %region_4.5_spmd, %region_5.6_... | conditional | bytes 11796672 | solution.py:399
  140.0 5.2 %collective-permute-start.9 = (bf16[576,768]{1,0:T(8,128)(2,1)S(1)}, bf16[576,768]{1,0:T(8,128)(2,1)}, u32[]{:S(2)}, u32[]{:S(2)}) collective-permute-start(bf16[576,768]{1,0:T(8,128)(2,1)S(1)} %get-tuple-element.169), channel_id=1, source_target_pairs={{0,8},{8,0},{1,9},{9,1},{3,11},{11,3},{7,15},{15,7},{16,24},{24,16... | collective-permute-start | bytes 2654216 | tf_op jit(solution)/shard_map/cond/branch_2_fun/ppermute | solution.py:392
  145.2 2.0 collective-permute-start.11
  147.2 4.8 %collective-permute-start.8 = (bf16[576,512]{1,0:T(8,128)(2,1)S(1)}, bf16[576,512]{1,0:T(8,128)(2,1)}, u32[]{:S(2)}, u32[]{:S(2)}) collective-permute-start(bf16[576,512]{1,0:T(8,128)(2,1)S(1)} %get-tuple-element.168), channel_id=1, source_target_pairs={{0,8},{8,0},{1,9},{9,1},{3,11},{11,3},{7,15},{15,7},{16,24},{24,16... | collective-permute-start | bytes 1769480 | tf_op jit(solution)/shard_map/cond/branch_2_fun/ppermute | solution.py:392
  152.1 2.7 %collective-permute-start.10 = (bf16[576,512]{1,0:T(8,128)(2,1)}, bf16[576,512]{1,0:T(8,128)(2,1)}, u32[]{:S(2)}, u32[]{:S(2)}) collective-permute-start(bf16[576,512]{1,0:T(8,128)(2,1)} %get-tuple-element.170), channel_id=1, source_target_pairs={{1,8},{9,0},{0,9},{8,1},{2,11},{10,3},{6,15},{14,7},{17,24},{25,16... | collective-permute-start | bytes 1769480 | tf_op jit(solution)/shard_map/cond/branch_2_fun/ppermute | solution.py:393
  154.8 45.7 %collective-permute-done.8 = bf16[576,512]{1,0:T(8,128)(2,1)} collective-permute-done((bf16[576,512]{1,0:T(8,128)(2,1)S(1)}, bf16[576,512]{1,0:T(8,128)(2,1)}, u32[]{:S(2)}, u32[]{:S(2)}) %collective-permute-start.8) | collective-permute-done | bytes 589856 | tf_op jit(solution)/shard_map/cond/branch_2_fun/ppermute | solution.py:392
  200.5 13.0 %collective-permute-done.10 = bf16[576,512]{1,0:T(8,128)(2,1)} collective-permute-done((bf16[576,512]{1,0:T(8,128)(2,1)}, bf16[576,512]{1,0:T(8,128)(2,1)}, u32[]{:S(2)}, u32[]{:S(2)}) %collective-permute-start.10) | collective-permute-done | bytes 589856 | tf_op jit(solution)/shard_map/cond/branch_2_fun/ppermute | solution.py:393
  213.4 0.0 collective-permute-done.82.refs_1_
  213.5 0.8 copy-done.4
  214.3 6.9 %place.1 = bf16[1152,1536]{1,0:T(8,128)(2,1)} custom-call(s32[1]{0:T(128)} %bitcast.10.moved_ref, bf16[1152,256]{1,0:T(8,128)(2,1)} %get-tuple-element.263.refs_0_, bf16[1152,256]{1,0:T(8,128)(2,1)} %copy-done.4, bf16[576,512]{1,0:T(8,128)(2,1)S(1)} %get-tuple-element.266.refs_2_, bf16[576,512]{1,0:T(8,128)(2,1)} %get-tuple-element.270.refs_3_, ...), custom_call_target="tpu_custom_call" | custom-call | tf_op jit(solution)/shard_map/place/pallas_call | solution.py:259
  221.2 0.0 all-to-all-done.1
  221.2 0.9 copy-done.1
  222.1 2.3 %combine_rows.1 = bf16[128,1152]{1,0:T(8,128)(2,1)} custom-call(s32[2,128]{1,0:T(2,128)} %get-tuple-element.258.where_ref, bf16[384,1152]{1,0:T(8,128)(2,1)} %bitcast.27), custom_call_target="tpu_custom_call" | custom-call | tf_op jit(solution)/shard_map/combine_rows/pallas_call | solution.py:305
  (14 shorter events, 0.0 us)
Async XLA Ops:
  54.5 3.7 %copy-start = (bf16[16,24,2304]{2,1,0:T(8,128)(2,1)}, bf16[16,24,2304]{2,1,0:T(8,128)(2,1)S(1)}, u32[]{:S(2)}) copy-start(bf16[16,24,2304]{2,1,0:T(8,128)(2,1)S(1)} %all_to_all.10) | copy-start | bytes 5308420
  54.5 3.7 %collective-permute-start.80 = (bf16[384,2304]{1,0:T(8,128)(2,1)S(1)}, bf16[384,2304]{1,0:T(8,128)(2,1)S(1)}, u32[]{:S(2)}, u32[]{:S(2)}) collective-permute-start(bf16[384,2304]{1,0:T(8,128)(2,1)S(1)} %bitcast.19), channel_id=1, source_target_pairs={{0,16},{16,0},{1,17},{17,1},{2,18},{18,2},{3,19},{19,3},{4,20},{20... | collective-permute-start | bytes 5308424 | tf_op jit(solution)/shard_map/ppermute | solution.py:314
  58.2 1.3 copy-start.2
  80.7 2.6 %collective-permute-start.81 = (bf16[384,1152]{1,0:T(8,128)(2,1)}, bf16[384,1152]{1,0:T(8,128)(2,1)S(1)}, u32[]{:S(2)}, u32[]{:S(2)}) collective-permute-start(bf16[384,1152]{1,0:T(8,128)(2,1)} %get-tuple-element.262), channel_id=1, source_target_pairs={{0,16},{16,0},{1,17},{17,1},{2,18},{18,2},{3,19},{19,3},{4,20},{20... | collective-permute-start | bytes 2654216 | tf_op jit(solution)/shard_map/ppermute | solution.py:314
  85.7 135.5 %all-to-all-start.1 = ((bf16[16,24,1152]{2,1,0:T(8,128)(2,1)}), bf16[16,24,1152]{2,1,0:T(8,128)(2,1)S(1)}, u32[]{:S(2)}, u32[]{:S(2)}) async-start(bf16[16,24,1152]{2,1,0:T(8,128)(2,1)} %bitcast.8), calls=%async_computation.1 | async-start | bytes 1769472 | tf_op jit(solution)/shard_map/all_to_all | solution.py:360
  97.1 17.3 %copy-start.3 = (bf16[1152,256]{1,0:T(8,128)(2,1)S(1)}, bf16[1152,256]{1,0:T(8,128)(2,1)}, u32[]{:S(2)}) copy-start(bf16[1152,256]{1,0:T(8,128)(2,1)} %get-tuple-element.263.refs_0_) | copy-start | bytes 1769476
  97.1 23.1 %copy-start.5 = (s32[16]{0:T(128)S(1)}, s32[16]{0:T(128)}, u32[]{:S(2)}) copy-start(s32[16]{0:T(128)} %param.34) | copy-start | bytes 196
  97.1 26.3 %copy-start.6 = (s32[256]{0:T(256)S(1)}, s32[256]{0:T(256)}, u32[]{:S(2)}) copy-start(s32[256]{0:T(256)} %constant.19.clone) | copy-start | bytes 3076
  97.1 42.8 %collective-permute-start.84 = (bf16[576,768]{1,0:T(8,128)(2,1)}, bf16[576,768]{1,0:T(8,128)(2,1)}, u32[]{:S(2)}, u32[]{:S(2)}) collective-permute-start(bf16[576,768]{1,0:T(8,128)(2,1)} %get-tuple-element.269.refs_8_), channel_id=1, source_target_pairs={{0,1},{1,0},{2,3},{3,2},{4,5},{5,4},{6,7},{7,6},{8,9},{9,8},{10,11... | collective-permute-start | bytes 2654216 | tf_op jit(solution)/shard_map/ppermute | solution.py:384
  108.8 31.2 %collective-permute-start.83 = (bf16[576,512]{1,0:T(8,128)(2,1)}, bf16[576,512]{1,0:T(8,128)(2,1)}, u32[]{:S(2)}, u32[]{:S(2)}) collective-permute-start(bf16[576,512]{1,0:T(8,128)(2,1)} %get-tuple-element.268.refs_4_), channel_id=1, source_target_pairs={{0,1},{1,0},{2,3},{3,2},{4,5},{5,4},{6,7},{7,6},{8,9},{9,8},{10,11... | collective-permute-start | bytes 1769480 | tf_op jit(solution)/shard_map/ppermute | solution.py:384
  114.5 99.0 %collective-permute-start.82 = (bf16[1152,256]{1,0:T(8,128)(2,1)S(1)}, bf16[1152,256]{1,0:T(8,128)(2,1)S(1)}, u32[]{:S(2)}, u32[]{:S(2)}) collective-permute-start(bf16[1152,256]{1,0:T(8,128)(2,1)S(1)} %copy-done.3), channel_id=1, source_target_pairs={{0,8},{1,9},{2,10},{3,11},{4,12},{5,13},{6,14},{7,15},{8,0},{9,1},... | collective-permute-start | bytes 1769480 | tf_op jit(solution)/shard_map/ppermute | solution.py:353
  140.0 73.5 %collective-permute-start.9 = (bf16[576,768]{1,0:T(8,128)(2,1)S(1)}, bf16[576,768]{1,0:T(8,128)(2,1)}, u32[]{:S(2)}, u32[]{:S(2)}) collective-permute-start(bf16[576,768]{1,0:T(8,128)(2,1)S(1)} %get-tuple-element.169), channel_id=1, source_target_pairs={{0,8},{8,0},{1,9},{9,1},{3,11},{11,3},{7,15},{15,7},{16,24},{24,16... | collective-permute-start | bytes 2654216 | tf_op jit(solution)/shard_map/cond/branch_2_fun/ppermute | solution.py:392
  145.2 68.2 %collective-permute-start.11 = (bf16[576,768]{1,0:T(8,128)(2,1)}, bf16[576,768]{1,0:T(8,128)(2,1)}, u32[]{:S(2)}, u32[]{:S(2)}) collective-permute-start(bf16[576,768]{1,0:T(8,128)(2,1)} %get-tuple-element.171), channel_id=1, source_target_pairs={{1,8},{9,0},{0,9},{8,1},{2,11},{10,3},{6,15},{14,7},{17,24},{25,16... | collective-permute-start | bytes 2654216 | tf_op jit(solution)/shard_map/cond/branch_2_fun/ppermute | solution.py:393
  147.2 53.2 %collective-permute-start.8 = (bf16[576,512]{1,0:T(8,128)(2,1)S(1)}, bf16[576,512]{1,0:T(8,128)(2,1)}, u32[]{:S(2)}, u32[]{:S(2)}) collective-permute-start(bf16[576,512]{1,0:T(8,128)(2,1)S(1)} %get-tuple-element.168), channel_id=1, source_target_pairs={{0,8},{8,0},{1,9},{9,1},{3,11},{11,3},{7,15},{15,7},{16,24},{24,16... | collective-permute-start | bytes 1769480 | tf_op jit(solution)/shard_map/cond/branch_2_fun/ppermute | solution.py:392
  152.1 61.4 %collective-permute-start.10 = (bf16[576,512]{1,0:T(8,128)(2,1)}, bf16[576,512]{1,0:T(8,128)(2,1)}, u32[]{:S(2)}, u32[]{:S(2)}) collective-permute-start(bf16[576,512]{1,0:T(8,128)(2,1)} %get-tuple-element.170), channel_id=1, source_target_pairs={{1,8},{9,0},{0,9},{8,1},{2,11},{10,3},{6,15},{14,7},{17,24},{25,16... | collective-permute-start | bytes 1769480 | tf_op jit(solution)/shard_map/cond/branch_2_fun/ppermute | solution.py:393
  213.5 0.8 copy-start.4
  221.2 0.9 copy-start.1
where the time goes:
time: 225 us; the launch traced here: 224 us
  waiting for transfers between devices  80.1 us (36%)
  blocking collectives  50.8 us (23%)
  Pallas kernels  47.2 us (21%)
  starting transfers between devices  35.6 us (16%)
  between operations  3.98 us (2%)
  local copies, waits for them, and re-layouts  3.61 us (2%)
  other arithmetic  2.94 us (1%)
    all_to_all x1, blocking collectives, shards(): lax.all_to_all(rows.reshape(expert_count, capacity, 2 * width), 'expert',...  50.8 us
    ppermute x2, waiting for transfers between devices, run(): lax.ppermute(a, 'expert', pairs)  45.7 us
    ppermute x2, waiting for transfers between devices, shards(): lent = [lax.ppermute(f, 'expert', across) for f in far]  15.3 us
    pallas_call x1, Pallas kernels, rest_step(): pl.pallas_call(functools.partial(rest_kernel, len(rows)), grid=(tiles,),...  14.6 us
    pallas_call x2, Pallas kernels, adam_columns(): pl.pallas_call(adam_kernel, grid=(tiles,), in_specs=[pl.BlockSpec((width,...  13.8 us
    ppermute x2, waiting for transfers between devices, run(): lax.ppermute(b, 'expert', skew)  13 us
    ppermute x2, starting transfers between devices, shards(): lent = [lax.ppermute(f, 'expert', across) for f in far]  11.4 us
    ppermute x2, starting transfers between devices, run(): lax.ppermute(a, 'expert', pairs)  10.1 us
  transfers between devices with their start and end apart: 10, of which 5 were waited for; matrix products, arithmetic and copies ran while one was open for 1% of the time, Pallas kernels for 9%

commit v1 on v0

--- a/solution.py
+++ b/solution.py
@@ -1,6 +1,5 @@
 import functools
 import itertools
-import math
 
 import jax
 import jax.numpy as jnp
@@ -8,6 +7,7 @@
 from jax.experimental import pallas as pl
 from jax.experimental.pallas import tpu as pltpu
 from jax.sharding import PartitionSpec as P
+
 
 ADAM_STEP = 100
 
@@ -193,80 +193,81 @@
     )(*rows, pre_first, w_in, w_in, w_out)
 
 
-def adam_kernel(xt_ref, pre_ref, m_ref, v_ref, *outs):
+def adam_kernel(xt_ref, pre_ref, m_ref, v_ref, out_ref):
     weight_grad = mxu(xt_ref[...], pre_ref[...], NN)
-    step = adam_step(weight_grad, m_ref[...], v_ref[...])
-    at = 0
-    for out in outs:
-        out[...] = step[at : at + out.shape[0], :]
-        at += out.shape[0]
-
-
-def adam_columns(x_t, pre_rest, first_moment, second_moment, start, tiles, tile, pieces):
+    out_ref[...] = adam_step(weight_grad, m_ref[...], v_ref[...])
+
+
+def adam_block(x_t, pre_rest, first_moment, second_moment, start, tiles, tile, part, parts):
     width, total = x_t.shape
-    rows = width // pieces
-    columns = pl.BlockSpec((width, tile), lambda j: (0, start + j))
+    rows = width // parts
+    block = pl.BlockSpec((rows, tile), lambda j: (part, start + j))
     return pl.pallas_call(
         adam_kernel,
         grid=(tiles,),
         in_specs=[
-            pl.BlockSpec((width, total), lambda j: (0, 0)),
+            pl.BlockSpec((rows, total), lambda j: (part, 0)),
             pl.BlockSpec((total, tile), lambda j: (0, start - 1 + j)),
-            columns,
-            columns,
+            block,
+            block,
         ],
-        out_specs=[pl.BlockSpec((rows, tile), lambda j: (0, j)) for _ in range(pieces)],
-        out_shape=[jax.ShapeDtypeStruct((rows, tiles * tile), bf16) for _ in range(pieces)],
+        out_specs=pl.BlockSpec((rows, tile), lambda j: (0, j)),
+        out_shape=jax.ShapeDtypeStruct((rows, tiles * tile), bf16),
         compiler_params=pltpu.CompilerParams(vmem_limit_bytes=VMEM_LIMIT),
         cost_estimate=pl.CostEstimate(
-            flops=2 * total * width * tile * tiles,
-            bytes_accessed=10 * tile * width * tiles,
+            flops=2 * total * rows * tile * tiles,
+            bytes_accessed=10 * tile * rows * tiles,
             transcendentals=0,
         ),
-        name="adam_columns",
     )(x_t, pre_rest, first_moment, second_moment)
 
 
-def place_kernel(boxes, rows, moved_ref, *refs):
-    out_ref = refs[-1]
-    step = pl.program_id(0)
-    for n, (row, col, high, wide) in enumerate(boxes):
-        inside = (step >= row // rows) & (step < (row + high) // rows)
-
-        @pl.when(inside & (moved_ref[0] == 0))
-        def _(n=n, col=col, wide=wide):
-            out_ref[:, col : col + wide] = refs[2 * n][...]
-
-        @pl.when(inside & (moved_ref[0] != 0))
-        def _(n=n, col=col, wide=wide):
-            out_ref[:, col : col + wide] = refs[2 * n + 1][...]
-
-
-def place(moved, pieces, width, inner, rows):
-    boxes = [piece[:4] for piece in pieces]
-    in_specs, args = [], []
-
-    def spec(row, high, wide, wanted):
-        def block(i, moved_ref):
-            near = jnp.clip(i - row // rows, 0, high // rows - 1)
-            return (jnp.where(moved_ref[0] == wanted, near, 0), 0)
-
-        return pl.BlockSpec((rows, wide), block)
-
-    for row, col, high, wide, kept, got in pieces:
-        in_specs += [spec(row, high, wide, 0), spec(row, high, wide, 1)]
-        args += [kept, got]
-    return pl.pallas_call(
-        functools.partial(place_kernel, boxes, rows),
-        grid_spec=pltpu.PrefetchScalarGridSpec(
-            num_scalar_prefetch=1,
-            grid=(width // rows,),
-            in_specs=in_specs,
-            out_specs=pl.BlockSpec((rows, inner), lambda i, moved_ref: (i, 0)),
+def place_kernel(boxes, source_ref, *refs):
+    sources, at = [], 0
+    for box in boxes:
+        sources.append(refs[at : at + box[4]])
+        at += box[4]
+    out_ref = refs[at]
+    bufs = refs[at + 1 : at + 1 + len(boxes)]
+    in_sem, out_sem = refs[at + 1 + len(boxes) :]
+    for n, arrays in enumerate(sources):
+        for k, array in enumerate(arrays):
+            last = k == len(arrays) - 1
+            wanted = source_ref[0] >= k if last else source_ref[0] == k
+
+            @pl.when(wanted)
+            def _(n=n, array=array):
+                pltpu.make_async_copy(array, bufs[n], in_sem.at[n]).start()
+
+    puts = []
+    for n, (row, col, high, wide, _) in enumerate(boxes):
+        pltpu.make_async_copy(sources[n][0], bufs[n], in_sem.at[n]).wait()
+        put = pltpu.make_async_copy(
+            bufs[n], out_ref.at[pl.ds(row, high), pl.ds(col, wide)], out_sem.at[n]
+        )
+        put.start()
+        puts.append(put)
+    for put in puts:
+        put.wait()
+
+
+def place(source, pieces, width, inner):
+    boxes = [piece[:4] + (len(piece[4]),) for piece in pieces]
+    args = [array for piece in pieces for array in piece[4]]
+    return pl.pallas_call(
+        functools.partial(place_kernel, boxes),
+        in_specs=[pl.BlockSpec(memory_space=pltpu.SMEM)]
+        + [pl.BlockSpec(memory_space=pl.ANY) for _ in args],
+        out_specs=pl.BlockSpec(memory_space=pl.ANY),
+        out_shape=jax.ShapeDtypeStruct((width, inner), bf16),
+        scratch_shapes=[pltpu.VMEM((box[2], box[3]), bf16) for box in boxes]
+        + [pltpu.SemaphoreType.DMA((len(boxes),)), pltpu.SemaphoreType.DMA((len(boxes),))],
+        compiler_params=pltpu.CompilerParams(vmem_limit_bytes=VMEM_LIMIT),
+        cost_estimate=pl.CostEstimate(
+            flops=0, bytes_accessed=4 * width * inner, transcendentals=0
         ),
-        out_shape=jax.ShapeDtypeStruct((width, inner), bf16),
         name="place",
-    )(moved, *args)
+    )(source, *args)
 
 
 def swap_plans(half):
@@ -275,22 +276,24 @@
     for e in range(half):
         groups.setdefault(e & ~(line | 1), []).append(e)
     groups = list(groups.values())
+    if half < 4 or len(groups) > 2:
+        return []
     forced = {0, half - 1}
-    size = len(groups[0])
-
-    def sets(members, k):
+    switches = []
+    for members in groups:
         must = forced & set(members)
-        return [set(s) for s in itertools.combinations(members, k) if must <= set(s)]
-
-    choices = [[sets(g, k) for g in groups] for k in range(1, size + 1)]
-    if half < 4 or sum(math.prod(len(c) for c in by_k) for by_k in choices) > 32:
-        return None, None
-    plans = [set().union(*picked) for by_k in choices for picked in itertools.product(*by_k)]
-    table = []
-    for mask in range(1 << half):
-        moved = forced | {e for e in range(half) if mask >> e & 1}
-        table.append(next(n for n, plan in enumerate(plans) if moved <= plan))
-    return plans, table
+        plans = [
+            set(s)
+            for k in range(2, len(members) + 1)
+            for s in itertools.combinations(members, k)
+            if must <= set(s)
+        ]
+        table = []
+        for mask in range(1 << half):
+            moved = must | {e for e in members if mask >> e & 1}
+            table.append(next(n for n, plan in enumerate(plans) if moved <= plan))
+        switches.append((plans, table))
+    return switches
 
 
 def combine_kernel(where_ref, back_ref, out_ref):
@@ -323,7 +326,7 @@
     own_index = lax.axis_index("expert")
     lane_ids = jnp.arange(expert_count, dtype=jnp.int32)
     partner_me = jnp.sum(jnp.where(lane_ids == own_index, swap_list, 0))
-    is_moved = (partner_me != own_index).astype(jnp.int32).reshape(1)
+    is_moved = (partner_me != own_index).astype(jnp.int32)
     moved_bits = jnp.where((swap_list != lane_ids) & (lane_ids < half), 1 << lane_ids, 0)
     moved_mask = jnp.sum(moved_bits)
     tok_count, width = tokens.shape
@@ -343,7 +346,6 @@
     inner = w_in.shape[2]
     tile = 256 if inner % 256 == 0 else 128
     tiles = inner // tile
-    plans, table = swap_plans(half)
     route = [(e, e ^ half) for e in range(expert_count)]
     across = [(e, e ^ 1) for e in range(expert_count)]
 
@@ -351,7 +353,7 @@
         all_rows, w_in[0], w_out[0], first_moment[0], second_moment[0], tile
     )
     first_got = lax.ppermute(first, "expert", route)
-    pieces = [(0, 0, width, tile, first, first_got)]
+    pieces = [(0, 0, width, tile, [first, first_got])]
 
     pre_rest, *parts = rest_step(all_rows, pre_first, w_in[0], w_out[0], tile)
     total = parts[0].astype(f32)
@@ -365,23 +367,19 @@
         tiled=True,
     ).reshape(slots, width)
 
-    chunks = [n for n in (2 * (tiles - 1) // 5, tiles - 1 - 2 * (tiles - 1) // 5) if n > 0]
-    at = 1
-    near, far, boxes = [], [], []
-    for n in chunks:
-        done = adam_columns(
-            x_t, pre_rest, first_moment[0], second_moment[0], at, n, tile, 2 if plans else 1
-        )
-        if plans:
-            near.append(done[0])
-            far.append(done[1])
-            boxes.append((at * tile, n * tile))
-        else:
-            got = lax.ppermute(done[0], "expert", route)
-            pieces.append((0, at * tile, width, n * tile, done[0], got))
-        at += n
-    if plans:
-        lent = [lax.ppermute(f, "expert", across) for f in far]
+    switches = swap_plans(half) if tiles > 2 else []
+    direct = 1 if switches else tiles - 1
+    moments = (first_moment[0], second_moment[0])
+    second = adam_block(x_t, pre_rest, *moments, 1, direct, tile, 0, 1)
+    second_got = lax.ppermute(second, "expert", route)
+    pieces.append((0, tile, width, direct * tile, [second, second_got]))
+    group = jnp.zeros((), jnp.int32)
+
+    if switches:
+        at, left = 1 + direct, tiles - 1 - direct
+        far = adam_block(x_t, pre_rest, *moments, at, left, tile, 1, 2)
+        lent = lax.ppermute(far, "expert", across)
+        near = adam_block(x_t, pre_rest, *moments, at, left, tile, 0, 2)
 
         def branch(plan):
             pairs = [(e, e ^ half) for p in plan for e in (p, p ^ half)]
@@ -389,20 +387,28 @@
 
             def run(near, lent):
                 return (
-                    [lax.ppermute(a, "expert", pairs) for a in near],
-                    [lax.ppermute(b, "expert", skew) for b in lent],
+                    lax.ppermute(near, "expert", pairs),
+                    lax.ppermute(lent, "expert", skew),
                 )
 
             return run
 
-        choice = jnp.asarray(table, jnp.int32)[moved_mask]
-        near_got, far_got = lax.switch(choice, [branch(p) for p in plans], near, lent)
-        for n, (col, wide) in enumerate(boxes):
-            pieces.append((0, col, width // 2, wide, near[n], near_got[n]))
-            pieces.append((width // 2, col, width // 2, wide, far[n], far_got[n]))
+        near_all, far_all = [near], [far]
+        for n, (plans, table) in enumerate(switches):
+            choice = jnp.asarray(table, jnp.int32)[moved_mask]
+            near_got, far_got = lax.switch(choice, [branch(p) for p in plans], near, lent)
+            near_all.append(near_got)
+            far_all.append(far_got)
+            members = {e for plan in plans for p in plan for e in (p, p ^ half)}
+            here = jnp.asarray([e in members for e in range(expert_count)])
+            group += jnp.sum(jnp.where(here & (lane_ids == own_index), n, 0))
+        wide = left * tile
+        pieces.append((0, at * tile, width // 2, wide, near_all))
+        pieces.append((width // 2, at * tile, width // 2, wide, far_all))
 
     x_grad = combine_rows(where_to, returned, tok_count)
-    adam_out = place(is_moved, pieces, width, inner, width // 8)
+    source = (is_moved * (1 + group)).reshape(1)
+    adam_out = place(source, pieces, width, inner)
     return (x_grad, adam_out[None])
 
 
@@ -419,4 +425,5 @@
         P("expert", None, "dp"),
     )
     out_specs = (P(("dp", "expert"), None), P("expert", None, "dp"))
+
     return jax.shard_map(shards, mesh=mesh, in_specs=in_specs, out_specs=out_specs, check_vma=False)

time: 225 us -> 223 us (level)
  the two profiles are of different devices: /device:TPU:0 before, /device:TPU:6 now
where the time goes in v1:
time: 223 us; the launch traced here: 222 us
  waiting for transfers between devices  96.6 us (43%)
  blocking collectives  47.6 us (21%)
  Pallas kernels  45.8 us (21%)
  starting transfers between devices  19.6 us (9%)
  between operations  5.26 us (2%)
  local copies, waits for them, and re-layouts  4.18 us (2%)
  other arithmetic  3.03 us (1%)
    ppermute x2, waiting for transfers between devices, run(): lax.ppermute(near, 'expert', pairs)  77.6 us
    all_to_all x1, blocking collectives, shards(): lax.all_to_all(rows.reshape(expert_count, capacity, 2 * width), 'expert',...  47.6 us
    pallas_call x3, Pallas kernels, adam_block(): pl.pallas_call(adam_kernel, grid=(tiles,), in_specs=[pl.BlockSpec((rows,...  16.2 us
    pallas_call x1, Pallas kernels, rest_step(): pl.pallas_call(functools.partial(rest_kernel, len(rows)), grid=(tiles,),...  14.6 us
    ppermute x1, waiting for transfers between devices, shards(): lent = lax.ppermute(far, 'expert', across)  12.8 us
    ppermute x2, starting transfers between devices, run(): lax.ppermute(near, 'expert', pairs)  7.32 us
    pallas_call x1, Pallas kernels, first_step(): pl.pallas_call(functools.partial(first_kernel, len(rows)), grid=(1,), in_...  6.52 us
    ppermute x2, waiting for transfers between devices, dp_shift(): return lax.ppermute(block, 'dp', [(i, i ^ apart) for i in range(count)])  6.2 us
  transfers between devices with their start and end apart: 10, of which 4 were waited for; matrix products, arithmetic and copies ran while one was open for 1% of the time, Pallas kernels for 9%

profile of v1, /device:TPU:6, one launch (start us, length us, event | category | flops | bytes accessed | tf_op | source)
XLA Modules:
  0.0 222.1 jit_solution(6647422955122533434)
XLA Ops:
  0.6 3.1 %pack_rows.1 = (bf16[384,2304]{1,0:T(8,128)(2,1)}, s32[2,128]{1,0:T(2,128)}) custom-call(s32[2,128]{1,0:T(2,128)} %bitcast.33, f32[2,128]{1,0:T(2,128)} %bitcast.34, bf16[128,1152]{1,0:T(8,128)(2,1)} %x_ref.1, bf16[128,1152]{1,0:T(8,128)(2,1)} %g_ref.1), custom_call_target="tpu_custom_call" | custom-call | tf_op jit(solution)/shard_map/pack_rows/pallas_call | solution.py:88
  3.7 47.6 %all_to_all.10 = bf16[16,24,2304]{2,1,0:T(8,128)(2,1)S(1)} all-to-all(bf16[16,24,2304]{2,1,0:T(8,128)(2,1)} %bitcast.32), channel_id=1, replica_groups=mesh['dp'=2,'expert'=16] {'expert'}, dimensions={0} | all-to-all | bytes 3538944 | tf_op jit(solution)/shard_map/all_to_all | solution.py:337
  51.3 3.7 %collective-permute-done.28.refs_1_ = bf16[384,2304]{1,0:T(8,128)(2,1)S(1)} collective-permute-done((bf16[384,2304]{1,0:T(8,128)(2,1)S(1)}, bf16[384,2304]{1,0:T(8,128)(2,1)S(1)}, u32[]{:S(2)}, u32[]{:S(2)}) %collective-permute-start.28) | collective-permute-done | bytes 1769504 | tf_op jit(solution)/shard_map/ppermute | solution.py:317
  55.0 1.2 copy-done.2
  56.2 6.5 %first_step.1 = (bf16[1152,256]{1,0:T(8,128)(2,1)}, bf16[768,256]{1,0:T(8,128)(2,1)}, bf16[1152,768]{1,0:T(8,128)(2,1)}) custom-call(bf16[384,2304]{1,0:T(8,128)(2,1)} %bitcast.23, bf16[384,2304]{1,0:T(8,128)(2,1)} %copy-done.2, bf16[1152,1536]{1,0:T(8,128)(2,1)} %bitcast.25, bf16[1536,1152]{1,0:T(8,128)(2,1)} %bitcast.28, f32[1152,1536]{1,0:T(8,128)} %bitcast.14, ...), custom_call_target="tpu_custom_call" | custom-call | flops 1358954496 | bytes 4128768 | tf_op jit(solution)/shard_map/first_step/pallas_call | solution.py:122
  62.7 14.6 %rest_step.1 = (bf16[768,1280]{1,0:T(8,128)(2,1)}, bf16[384,1152]{1,0:T(8,128)(2,1)}, bf16[384,1152]{1,0:T(8,128)(2,1)}) custom-call(bf16[384,2304]{1,0:T(8,128)(2,1)} %bitcast.24, bf16[384,2304]{1,0:T(8,128)(2,1)} %copy-done.2, bf16[768,256]{1,0:T(8,128)(2,1)} %get-tuple-element.100.refs_2_, bf16[1152,1536]{1,0:T(8,128)(2,1)} %bitcast.26, ...), custom_call_target="tpu_custom_call" | custom-call | flops 6794772480 | bytes 5898240 | tf_op jit(solution)/shard_map/rest_step/pallas_call | solution.py:171
  77.4 0.1 collective-permute-start.29
  77.5 2.5 %collective-permute-done.29 = bf16[384,1152]{1,0:T(8,128)(2,1)S(1)} collective-permute-done((bf16[384,1152]{1,0:T(8,128)(2,1)}, bf16[384,1152]{1,0:T(8,128)(2,1)S(1)}, u32[]{:S(2)}, u32[]{:S(2)}) %collective-permute-start.29) | collective-permute-done | bytes 884768 | tf_op jit(solution)/shard_map/ppermute | solution.py:317
  80.0 2.3 %add_convert_fusion = bf16[384,1152]{1,0:T(8,128)(2,1)} fusion(bf16[384,1152]{1,0:T(8,128)(2,1)S(1)} %collective-permute-done.29, bf16[384,1152]{1,0:T(8,128)(2,1)} %get-tuple-element.101), kind=kLoop, calls=%fused_computation | loop fusion | flops 1769472 | bytes 2654208 | tf_op jit(solution)/shard_map/convert_element_type | solution.py:363
  82.3 5.7 %all-to-all-start.1 = ((bf16[16,24,1152]{2,1,0:T(8,128)(2,1)}), bf16[16,24,1152]{2,1,0:T(8,128)(2,1)S(1)}, u32[]{:S(2)}, u32[]{:S(2)}) async-start(bf16[16,24,1152]{2,1,0:T(8,128)(2,1)} %bitcast.8), calls=%async_computation.1 | async-start | bytes 1769472 | tf_op jit(solution)/shard_map/all_to_all | solution.py:362
  88.0 6.3 %shard_map.138.refs_7_ = bf16[576,1024]{1,0:T(8,128)(2,1)} custom-call(bf16[1152,768]{1,0:T(8,128)(2,1)} %get-tuple-element.104.xt_ref, bf16[768,1280]{1,0:T(8,128)(2,1)} %get-tuple-element.105.pre_ref, f32[1152,1536]{1,0:T(8,128)} %bitcast.15, f32[1152,1536]{1,0:T(8,128)} %bitcast.19), custom_call_target="tpu_custom_call" | custom-call | flops 905969664 | bytes 5898240 | tf_op jit(solution)/shard_map/pallas_call | solution.py:205
  94.3 0.6 collective-permute-start.32
  95.0 4.3 %shard_map.136.refs_2_ = bf16[1152,256]{1,0:T(8,128)(2,1)} custom-call(bf16[1152,768]{1,0:T(8,128)(2,1)} %get-tuple-element.104.xt_ref, bf16[768,1280]{1,0:T(8,128)(2,1)} %get-tuple-element.105.pre_ref, f32[1152,1536]{1,0:T(8,128)} %bitcast.16, f32[1152,1536]{1,0:T(8,128)} %bitcast.20), custom_call_target="tpu_custom_call" | custom-call | flops 452984832 | bytes 2949120 | tf_op jit(solution)/shard_map/pallas_call | solution.py:205
  99.3 2.4 %collective-permute-start.31 = (bf16[1152,256]{1,0:T(8,128)(2,1)}, bf16[1152,256]{1,0:T(8,128)(2,1)S(1)}, u32[]{:S(2)}, u32[]{:S(2)}) collective-permute-start(bf16[1152,256]{1,0:T(8,128)(2,1)} %shard_map.136.refs_2_), channel_id=1, source_target_pairs={{0,8},{1,9},{2,10},{3,11},{4,12},{5,13},{6,14},{7,15},{8,0},{9,1},... | collective-permute-start | bytes 1769480 | tf_op jit(solution)/shard_map/ppermute | solution.py:374
  101.7 0.5 collective-permute-start.30
  102.2 0.7 fusion.2
  105.5 0.6 dynamic_slice.7
  106.1 0.6 dynamic_slice.6
  108.7 5.5 %shard_map.137.refs_4_ = bf16[576,1024]{1,0:T(8,128)(2,1)S(1)} custom-call(bf16[1152,768]{1,0:T(8,128)(2,1)} %get-tuple-element.104.xt_ref, bf16[768,1280]{1,0:T(8,128)(2,1)} %get-tuple-element.105.pre_ref, f32[1152,1536]{1,0:T(8,128)} %bitcast.17, f32[1152,1536]{1,0:T(8,128)} %bitcast.21), custom_call_target="tpu_custom_call" | custom-call | flops 905969664 | bytes 5898240 | tf_op jit(solution)/shard_map/pallas_call | solution.py:205
  114.2 12.8 %collective-permute-done.32 = bf16[576,1024]{1,0:T(8,128)(2,1)} collective-permute-done((bf16[576,1024]{1,0:T(8,128)(2,1)}, bf16[576,1024]{1,0:T(8,128)(2,1)}, u32[]{:S(2)}, u32[]{:S(2)}) %collective-permute-start.32) | collective-permute-done | bytes 1179680 | tf_op jit(solution)/shard_map/ppermute | solution.py:381
  127.0 84.5 %conditional.3 = (bf16[576,1024]{1,0:T(8,128)(2,1)}, bf16[576,1024]{1,0:T(8,128)(2,1)}) conditional(s32[]{:T(128)} %bitcast.12, (bf16[576,1024]{1,0:T(8,128)(2,1)S(1)}, bf16[576,1024]{1,0:T(8,128)(2,1)}) %tuple.64, (bf16[576,1024]{1,0:T(8,128)(2,1)S(1)}, bf16[576,1024]{1,0:T(8,128)(2,1)}) %tuple.64, ...), branch_computations={%region_10.11_spmd, %region_11.12_spmd, %region_12.13_spmd, %regio... | conditional | bytes 9437280 | solution.py:399
  127.0 5.6 %collective-permute-start.16 = (bf16[576,1024]{1,0:T(8,128)(2,1)S(1)}, bf16[576,1024]{1,0:T(8,128)(2,1)}, u32[]{:S(2)}, u32[]{:S(2)}) collective-permute-start(bf16[576,1024]{1,0:T(8,128)(2,1)S(1)} %get-tuple-element.72), channel_id=1, source_target_pairs={{3,11},{11,3},{7,15},{15,7},{19,27},{27,19},{23,31},{31,23}} | collective-permute-start | bytes 3538952 | tf_op jit(solution)/shard_map/cond/branch_1_fun/ppermute | solution.py:390
  132.6 1.3 collective-permute-start.17
  133.9 77.6 %collective-permute-done.16 = bf16[576,1024]{1,0:T(8,128)(2,1)} collective-permute-done((bf16[576,1024]{1,0:T(8,128)(2,1)S(1)}, bf16[576,1024]{1,0:T(8,128)(2,1)}, u32[]{:S(2)}, u32[]{:S(2)}) %collective-permute-start.16) | collective-permute-done | bytes 1179680 | tf_op jit(solution)/shard_map/cond/branch_1_fun/ppermute | solution.py:390
  211.5 0.0 collective-permute-done.17
  211.5 3.4 %conditional.2 = (bf16[576,1024]{1,0:T(8,128)(2,1)}, bf16[576,1024]{1,0:T(8,128)(2,1)}) conditional(s32[]{:T(128)} %bitcast.11, (bf16[576,1024]{1,0:T(8,128)(2,1)S(1)}, bf16[576,1024]{1,0:T(8,128)(2,1)}) %tuple.64, (bf16[576,1024]{1,0:T(8,128)(2,1)S(1)}, bf16[576,1024]{1,0:T(8,128)(2,1)}) %tuple.64, ...), branch_computations={%region_3.4_spmd, %region_4.5_spmd, %region_5.6_spmd, %region_6.7_... | conditional | bytes 9437280 | solution.py:399
  211.5 1.7 collective-permute-start
  213.3 1.7 collective-permute-start.1
  215.0 0.8 copy-done.4
  215.8 3.1 %place.1 = bf16[1152,1536]{1,0:T(8,128)(2,1)} custom-call(s32[1]{0:T(128)} %bitcast.10.source_ref, bf16[1152,256]{1,0:T(8,128)(2,1)} %get-tuple-element.103.refs_0_, bf16[1152,256]{1,0:T(8,128)(2,1)} %collective-permute-done.30.refs_1_, bf16[1152,256]{1,0:T(8,128)(2,1)} %shard_map.136.refs_2_, bf16[1152,256]{1,0:T(8,128)(2,1)} %copy-done.4, ...), custom_call_target="tpu_custom_call" | custom-call | bytes 7077888 | tf_op jit(solution)/shard_map/place/pallas_call | solution.py:257
  218.9 0.9 copy-done.1
  219.8 2.3 %combine_rows.1 = bf16[128,1152]{1,0:T(8,128)(2,1)} custom-call(s32[2,128]{1,0:T(2,128)} %get-tuple-element.98.where_ref, bf16[384,1152]{1,0:T(8,128)(2,1)} %bitcast.31), custom_call_target="tpu_custom_call" | custom-call | tf_op jit(solution)/shard_map/combine_rows/pallas_call | solution.py:308
  (21 shorter events, 0.0 us)
Async XLA Ops:
  51.3 3.7 %copy-start = (bf16[16,24,2304]{2,1,0:T(8,128)(2,1)}, bf16[16,24,2304]{2,1,0:T(8,128)(2,1)S(1)}, u32[]{:S(2)}) copy-start(bf16[16,24,2304]{2,1,0:T(8,128)(2,1)S(1)} %all_to_all.10) | copy-start | bytes 5308420
  51.3 3.7 %collective-permute-start.28 = (bf16[384,2304]{1,0:T(8,128)(2,1)S(1)}, bf16[384,2304]{1,0:T(8,128)(2,1)S(1)}, u32[]{:S(2)}, u32[]{:S(2)}) collective-permute-start(bf16[384,2304]{1,0:T(8,128)(2,1)S(1)} %bitcast.22), channel_id=1, source_target_pairs={{0,16},{16,0},{1,17},{17,1},{2,18},{18,2},{3,19},{19,3},{4,20},{20... | collective-permute-start | bytes 5308424 | tf_op jit(solution)/shard_map/ppermute | solution.py:317
  55.0 1.2 copy-start.2
  77.4 2.6 %collective-permute-start.29 = (bf16[384,1152]{1,0:T(8,128)(2,1)}, bf16[384,1152]{1,0:T(8,128)(2,1)S(1)}, u32[]{:S(2)}, u32[]{:S(2)}) collective-permute-start(bf16[384,1152]{1,0:T(8,128)(2,1)} %get-tuple-element.102), channel_id=1, source_target_pairs={{0,16},{16,0},{1,17},{17,1},{2,18},{18,2},{3,19},{19,3},{4,20},{20... | collective-permute-start | bytes 2654216 | tf_op jit(solution)/shard_map/ppermute | solution.py:317
  82.3 136.6 %all-to-all-start.1 = ((bf16[16,24,1152]{2,1,0:T(8,128)(2,1)}), bf16[16,24,1152]{2,1,0:T(8,128)(2,1)S(1)}, u32[]{:S(2)}, u32[]{:S(2)}) async-start(bf16[16,24,1152]{2,1,0:T(8,128)(2,1)} %bitcast.8), calls=%async_computation.1 | async-start | bytes 1769472 | tf_op jit(solution)/shard_map/all_to_all | solution.py:362
  94.3 7.4 %copy-start.3 = (bf16[1152,256]{1,0:T(8,128)(2,1)S(1)}, bf16[1152,256]{1,0:T(8,128)(2,1)}, u32[]{:S(2)}) copy-start(bf16[1152,256]{1,0:T(8,128)(2,1)} %get-tuple-element.103.refs_0_) | copy-start | bytes 1769476
  94.3 7.9 %copy-start.5 = (s32[16]{0:T(128)S(1)}, s32[16]{0:T(128)}, u32[]{:S(2)}) copy-start(s32[16]{0:T(128)} %param.30) | copy-start | bytes 196
  94.3 7.9 %copy-start.6 = (pred[16]{0:T(512)(128)(4,1)S(1)}, pred[16]{0:T(512)(128)(4,1)}, u32[]{:S(2)}) copy-start(pred[16]{0:T(512)(128)(4,1)} %constant.32.clone) | copy-start | bytes 52
  94.3 11.2 %copy-start.8 = (s32[256]{0:T(256)S(1)}, s32[256]{0:T(256)}, u32[]{:S(2)}) copy-start(s32[256]{0:T(256)} %constant.31.clone) | copy-start | bytes 3076
  94.3 11.8 %copy-start.7 = (s32[256]{0:T(256)S(1)}, s32[256]{0:T(256)}, u32[]{:S(2)}) copy-start(s32[256]{0:T(256)} %constant.30.clone) | copy-start | bytes 3076
  94.3 32.7 %collective-permute-start.32 = (bf16[576,1024]{1,0:T(8,128)(2,1)}, bf16[576,1024]{1,0:T(8,128)(2,1)}, u32[]{:S(2)}, u32[]{:S(2)}) collective-permute-start(bf16[576,1024]{1,0:T(8,128)(2,1)} %shard_map.138.refs_7_), channel_id=1, source_target_pairs={{0,1},{1,0},{2,3},{3,2},{4,5},{5,4},{6,7},{7,6},{8,9},{9,8},{10,11... | collective-permute-start | bytes 3538952 | tf_op jit(solution)/shard_map/ppermute | solution.py:381
  99.3 115.7 %collective-permute-start.31 = (bf16[1152,256]{1,0:T(8,128)(2,1)}, bf16[1152,256]{1,0:T(8,128)(2,1)S(1)}, u32[]{:S(2)}, u32[]{:S(2)}) collective-permute-start(bf16[1152,256]{1,0:T(8,128)(2,1)} %shard_map.136.refs_2_), channel_id=1, source_target_pairs={{0,8},{1,9},{2,10},{3,11},{4,12},{5,13},{6,14},{7,15},{8,0},{9,1},... | collective-permute-start | bytes 1769480 | tf_op jit(solution)/shard_map/ppermute | solution.py:374
  101.7 113.3 %collective-permute-start.30 = (bf16[1152,256]{1,0:T(8,128)(2,1)S(1)}, bf16[1152,256]{1,0:T(8,128)(2,1)}, u32[]{:S(2)}, u32[]{:S(2)}) collective-permute-start(bf16[1152,256]{1,0:T(8,128)(2,1)S(1)} %copy-done.3), channel_id=1, source_target_pairs={{0,8},{1,9},{2,10},{3,11},{4,12},{5,13},{6,14},{7,15},{8,0},{9,1},... | collective-permute-start | bytes 1769480 | tf_op jit(solution)/shard_map/ppermute | solution.py:355
  127.0 84.5 %collective-permute-start.16 = (bf16[576,1024]{1,0:T(8,128)(2,1)S(1)}, bf16[576,1024]{1,0:T(8,128)(2,1)}, u32[]{:S(2)}, u32[]{:S(2)}) collective-permute-start(bf16[576,1024]{1,0:T(8,128)(2,1)S(1)} %get-tuple-element.72), channel_id=1, source_target_pairs={{3,11},{11,3},{7,15},{15,7},{19,27},{27,19},{23,31},{31,23}} | collective-permute-start | bytes 3538952 | tf_op jit(solution)/shard_map/cond/branch_1_fun/ppermute | solution.py:390
  132.6 78.9 %collective-permute-start.17 = (bf16[576,1024]{1,0:T(8,128)(2,1)}, bf16[576,1024]{1,0:T(8,128)(2,1)}, u32[]{:S(2)}, u32[]{:S(2)}) collective-permute-start(bf16[576,1024]{1,0:T(8,128)(2,1)} %get-tuple-element.73), channel_id=1, source_target_pairs={{2,11},{10,3},{6,15},{14,7},{18,27},{26,19},{22,31},{30,23}} | collective-permute-start | bytes 3538952 | tf_op jit(solution)/shard_map/cond/branch_1_fun/ppermute | solution.py:391
  211.5 3.4 %collective-permute-start = (bf16[576,1024]{1,0:T(8,128)(2,1)S(1)}, bf16[576,1024]{1,0:T(8,128)(2,1)}, u32[]{:S(2)}, u32[]{:S(2)}) collective-permute-start(bf16[576,1024]{1,0:T(8,128)(2,1)S(1)} %get-tuple-element.56), channel_id=1, source_target_pairs={{0,8},{8,0},{1,9},{9,1},{16,24},{24,16},{17,25},{25,17}} | collective-permute-start | bytes 3538952 | tf_op jit(solution)/shard_map/cond/branch_0_fun/ppermute | solution.py:390
  213.3 1.7 collective-permute-start.1
  215.0 0.8 copy-start.4
  218.9 0.9 copy-start.1

commit v2 on v1

--- a/solution.py
+++ b/solution.py
@@ -19,7 +19,7 @@
 adam_eps = 1e-08
 
 
-VMEM_LIMIT = 60 * 1024 * 1024
+MIB = 2**20
 
 f32 = jnp.float32
 bf16 = jnp.bfloat16
@@ -134,7 +134,7 @@
             jax.ShapeDtypeStruct((total, tile), bf16),
             jax.ShapeDtypeStruct((width, total), bf16),
         ],
-        compiler_params=pltpu.CompilerParams(vmem_limit_bytes=VMEM_LIMIT),
+        compiler_params=pltpu.CompilerParams(vmem_limit_bytes=56 * MIB),
         cost_estimate=pl.CostEstimate(
             flops=6 * total * width * tile, bytes_accessed=14 * tile * width, transcendentals=0
         ),
@@ -183,7 +183,7 @@
         out_shape=[jax.ShapeDtypeStruct((total, tiles * tile), bf16)]
         + [jax.ShapeDtypeStruct((per, width), bf16) for _ in rows],
         scratch_shapes=[pltpu.VMEM((total, width), f32)],
-        compiler_params=pltpu.CompilerParams(vmem_limit_bytes=VMEM_LIMIT),
+        compiler_params=pltpu.CompilerParams(vmem_limit_bytes=56 * MIB),
         cost_estimate=pl.CostEstimate(
             flops=6 * total * width * tile * tiles,
             bytes_accessed=4 * tile * width * tiles,
@@ -213,7 +213,7 @@
         ],
         out_specs=pl.BlockSpec((rows, tile), lambda j: (0, j)),
         out_shape=jax.ShapeDtypeStruct((rows, tiles * tile), bf16),
-        compiler_params=pltpu.CompilerParams(vmem_limit_bytes=VMEM_LIMIT),
+        compiler_params=pltpu.CompilerParams(vmem_limit_bytes=60 * MIB),
         cost_estimate=pl.CostEstimate(
             flops=2 * total * rows * tile * tiles,
             bytes_accessed=10 * tile * rows * tiles,
@@ -262,7 +262,7 @@
         out_shape=jax.ShapeDtypeStruct((width, inner), bf16),
         scratch_shapes=[pltpu.VMEM((box[2], box[3]), bf16) for box in boxes]
         + [pltpu.SemaphoreType.DMA((len(boxes),)), pltpu.SemaphoreType.DMA((len(boxes),))],
-        compiler_params=pltpu.CompilerParams(vmem_limit_bytes=VMEM_LIMIT),
+        compiler_params=pltpu.CompilerParams(vmem_limit_bytes=8 * MIB),
         cost_estimate=pl.CostEstimate(
             flops=0, bytes_accessed=4 * width * inner, transcendentals=0
         ),
@@ -367,6 +367,7 @@
         tiled=True,
     ).reshape(slots, width)
 
+    x_grad = combine_rows(where_to, returned, tok_count)
     switches = swap_plans(half) if tiles > 2 else []
     direct = 1 if switches else tiles - 1
     moments = (first_moment[0], second_moment[0])
@@ -393,6 +394,7 @@
 
             return run
 
+        near, lent, x_grad = lax.optimization_barrier((near, lent, x_grad))
         near_all, far_all = [near], [far]
         for n, (plans, table) in enumerate(switches):
             choice = jnp.asarray(table, jnp.int32)[moved_mask]
@@ -406,7 +408,6 @@
         pieces.append((0, at * tile, width // 2, wide, near_all))
         pieces.append((width // 2, at * tile, width // 2, wide, far_all))
 
-    x_grad = combine_rows(where_to, returned, tok_count)
     source = (is_moved * (1 + group)).reshape(1)
     adam_out = place(source, pieces, width, inner)
     return (x_grad, adam_out[None])

time: 223 us -> 220 us (0.987)
    all_to_all x1, waiting for transfers between devices: 0.01 us -> 19.1 us  [shards(): lax.all_to_all(total.astype(bf16).reshape(expert_count, capacity, width),...]
    ppermute x1, waiting for transfers between devices: 12.8 us -> 0.01 us  [shards(): lent = lax.ppermute(far, 'expert', across)]
    ppermute x2, waiting for transfers between devices: 77.6 us -> 70 us  [run(): lax.ppermute(near, 'expert', pairs)]
where the time goes in v2:
time: 220 us; the launch traced here: 219 us
  waiting for transfers between devices  95.3 us (43%)
  blocking collectives  47.6 us (22%)
  Pallas kernels  47 us (21%)
  starting transfers between devices  18.5 us (8%)
  between operations  5.24 us (2%)
  other arithmetic  3.07 us (1%)
  local copies, waits for them, and re-layouts  2.48 us (1%)
    ppermute x2, waiting for transfers between devices, run(): lax.ppermute(near, 'expert', pairs)  70 us
    all_to_all x1, blocking collectives, shards(): lax.all_to_all(rows.reshape(expert_count, capacity, 2 * width), 'expert',...  47.6 us
    all_to_all x1, waiting for transfers between devices, shards(): lax.all_to_all(total.astype(bf16).reshape(expert_count, capacity, width),...  19.1 us
    pallas_call x3, Pallas kernels, adam_block(): pl.pallas_call(adam_kernel, grid=(tiles,), in_specs=[pl.BlockSpec((rows,...  17 us
    pallas_call x1, Pallas kernels, rest_step(): pl.pallas_call(functools.partial(rest_kernel, len(rows)), grid=(tiles,),...  14.6 us
    pallas_call x1, Pallas kernels, first_step(): pl.pallas_call(functools.partial(first_kernel, len(rows)), grid=(1,), in_...  6.56 us
    all_to_all x1, starting transfers between devices, shards(): lax.all_to_all(total.astype(bf16).reshape(expert_count, capacity, width),...  6.28 us
    ppermute x2, waiting for transfers between devices, dp_shift(): return lax.ppermute(block, 'dp', [(i, i ^ apart) for i in range(count)])  6.18 us
  transfers between devices with their start and end apart: 10, of which 4 were waited for; matrix products, arithmetic and copies ran while one was open for 1% of the time, Pallas kernels for 9%

profile of v2, /device:TPU:6, one launch (start us, length us, event | category | flops | bytes accessed | tf_op | source)
XLA Modules:
  0.0 219.2 jit_solution(5116458409120180340)
XLA Ops:
  0.6 3.1 %pack_rows.1 = (bf16[384,2304]{1,0:T(8,128)(2,1)}, s32[2,128]{1,0:T(2,128)}) custom-call(s32[2,128]{1,0:T(2,128)} %bitcast.32, f32[2,128]{1,0:T(2,128)} %bitcast.33, bf16[128,1152]{1,0:T(8,128)(2,1)} %x_ref.1, bf16[128,1152]{1,0:T(8,128)(2,1)} %g_ref.1), custom_call_target="tpu_custom_call" | custom-call | tf_op jit(solution)/shard_map/pack_rows/pallas_call | solution.py:88
  3.7 47.6 %all_to_all.10 = bf16[16,24,2304]{2,1,0:T(8,128)(2,1)S(1)} all-to-all(bf16[16,24,2304]{2,1,0:T(8,128)(2,1)} %bitcast.31), channel_id=1, replica_groups=mesh['dp'=2,'expert'=16] {'expert'}, dimensions={0} | all-to-all | bytes 3538944 | tf_op jit(solution)/shard_map/all_to_all | solution.py:337
  51.3 3.7 %collective-permute-done.28.refs_1_ = bf16[384,2304]{1,0:T(8,128)(2,1)S(1)} collective-permute-done((bf16[384,2304]{1,0:T(8,128)(2,1)S(1)}, bf16[384,2304]{1,0:T(8,128)(2,1)S(1)}, u32[]{:S(2)}, u32[]{:S(2)}) %collective-permute-start.28) | collective-permute-done | bytes 1769504 | tf_op jit(solution)/shard_map/ppermute | solution.py:317
  55.0 1.2 copy-done.4
  56.2 6.6 %first_step.1 = (bf16[1152,256]{1,0:T(8,128)(2,1)}, bf16[768,256]{1,0:T(8,128)(2,1)}, bf16[1152,768]{1,0:T(8,128)(2,1)}) custom-call(bf16[384,2304]{1,0:T(8,128)(2,1)} %bitcast.23, bf16[384,2304]{1,0:T(8,128)(2,1)} %copy-done.4, bf16[1152,1536]{1,0:T(8,128)(2,1)} %bitcast.25, bf16[1536,1152]{1,0:T(8,128)(2,1)} %bitcast.28, f32[1152,1536]{1,0:T(8,128)} %bitcast.14, ...), custom_call_target="tpu_custom_call" | custom-call | flops 1358954496 | bytes 4128768 | tf_op jit(solution)/shard_map/first_step/pallas_call | solution.py:122
  62.7 14.6 %rest_step.1 = (bf16[768,1280]{1,0:T(8,128)(2,1)}, bf16[384,1152]{1,0:T(8,128)(2,1)}, bf16[384,1152]{1,0:T(8,128)(2,1)}) custom-call(bf16[384,2304]{1,0:T(8,128)(2,1)} %bitcast.24, bf16[384,2304]{1,0:T(8,128)(2,1)} %copy-done.4, bf16[768,256]{1,0:T(8,128)(2,1)} %get-tuple-element.103.refs_2_, bf16[1152,1536]{1,0:T(8,128)(2,1)} %bitcast.26, ...), custom_call_target="tpu_custom_call" | custom-call | flops 6794772480 | bytes 5898240 | tf_op jit(solution)/shard_map/rest_step/pallas_call | solution.py:171
  77.4 0.1 collective-permute-start.30
  77.5 2.5 %collective-permute-done.30 = bf16[384,1152]{1,0:T(8,128)(2,1)S(1)} collective-permute-done((bf16[384,1152]{1,0:T(8,128)(2,1)}, bf16[384,1152]{1,0:T(8,128)(2,1)S(1)}, u32[]{:S(2)}, u32[]{:S(2)}) %collective-permute-start.30) | collective-permute-done | bytes 884768 | tf_op jit(solution)/shard_map/ppermute | solution.py:317
  80.0 2.4 %add_convert_fusion = bf16[384,1152]{1,0:T(8,128)(2,1)} fusion(bf16[384,1152]{1,0:T(8,128)(2,1)S(1)} %collective-permute-done.30, bf16[384,1152]{1,0:T(8,128)(2,1)} %get-tuple-element.106), kind=kLoop, calls=%fused_computation | loop fusion | flops 1769472 | bytes 2654208 | tf_op jit(solution)/shard_map/convert_element_type | solution.py:363
  82.4 6.3 %all-to-all-start.1 = ((bf16[16,24,1152]{2,1,0:T(8,128)(2,1)}), bf16[16,24,1152]{2,1,0:T(8,128)(2,1)}, u32[]{:S(2)}, u32[]{:S(2)}) async-start(bf16[16,24,1152]{2,1,0:T(8,128)(2,1)} %bitcast.8), calls=%async_computation.1 | async-start | bytes 1769472 | tf_op jit(solution)/shard_map/all_to_all | solution.py:362
  88.7 6.3 %shard_map.137.refs_7_ = bf16[576,1024]{1,0:T(8,128)(2,1)} custom-call(bf16[1152,768]{1,0:T(8,128)(2,1)} %get-tuple-element.102.xt_ref, bf16[768,1280]{1,0:T(8,128)(2,1)} %get-tuple-element.104.pre_ref, f32[1152,1536]{1,0:T(8,128)} %bitcast.15, f32[1152,1536]{1,0:T(8,128)} %bitcast.19), custom_call_target="tpu_custom_call" | custom-call | flops 905969664 | bytes 5898240 | tf_op jit(solution)/shard_map/pallas_call | solution.py:205
  95.0 0.0 copy-start.8
  95.0 0.0 copy-start.7
  95.0 0.6 collective-permute-start.29
  95.6 4.3 %shard_map.138.refs_2_ = bf16[1152,256]{1,0:T(8,128)(2,1)} custom-call(bf16[1152,768]{1,0:T(8,128)(2,1)} %get-tuple-element.102.xt_ref, bf16[768,1280]{1,0:T(8,128)(2,1)} %get-tuple-element.104.pre_ref, f32[1152,1536]{1,0:T(8,128)} %bitcast.16, f32[1152,1536]{1,0:T(8,128)} %bitcast.20), custom_call_target="tpu_custom_call" | custom-call | flops 452984832 | bytes 2949120 | tf_op jit(solution)/shard_map/pallas_call | solution.py:205
  100.0 2.4 %collective-permute-start.32 = (bf16[1152,256]{1,0:T(8,128)(2,1)}, bf16[1152,256]{1,0:T(8,128)(2,1)S(1)}, u32[]{:S(2)}, u32[]{:S(2)}) collective-permute-start(bf16[1152,256]{1,0:T(8,128)(2,1)} %shard_map.138.refs_2_), channel_id=1, source_target_pairs={{0,8},{1,9},{2,10},{3,11},{4,12},{5,13},{6,14},{7,15},{8,0},{9,1},... | collective-permute-start | bytes 1769480 | tf_op jit(solution)/shard_map/ppermute | solution.py:375
  102.4 0.5 collective-permute-start.31
  102.9 0.7 fusion.2
  106.2 0.7 dynamic_slice.7
  106.9 0.6 dynamic_slice.6
  109.4 6.4 %shard_map.136.refs_4_ = bf16[576,1024]{1,0:T(8,128)(2,1)} custom-call(bf16[1152,768]{1,0:T(8,128)(2,1)} %get-tuple-element.102.xt_ref, bf16[768,1280]{1,0:T(8,128)(2,1)} %get-tuple-element.104.pre_ref, f32[1152,1536]{1,0:T(8,128)} %bitcast.17, f32[1152,1536]{1,0:T(8,128)} %bitcast.21), custom_call_target="tpu_custom_call" | custom-call | flops 905969664 | bytes 5898240 | tf_op jit(solution)/shard_map/pallas_call | solution.py:205
  115.8 19.1 %all-to-all-done.1 = bf16[16,24,1152]{2,1,0:T(8,128)(2,1)} async-done(((bf16[16,24,1152]{2,1,0:T(8,128)(2,1)}), bf16[16,24,1152]{2,1,0:T(8,128)(2,1)}, u32[]{:S(2)}, u32[]{:S(2)}) %all-to-all-start.1) | async-done | bytes 884768 | tf_op jit(solution)/shard_map/all_to_all | solution.py:362
  134.9 2.3 %combine_rows.1 = bf16[128,1152]{1,0:T(8,128)(2,1)} custom-call(s32[2,128]{1,0:T(2,128)} %get-tuple-element.105.where_ref, bf16[384,1152]{1,0:T(8,128)(2,1)} %bitcast.9.back_ref), custom_call_target="tpu_custom_call" | custom-call | tf_op jit(solution)/shard_map/combine_rows/pallas_call | solution.py:308
  137.1 75.1 %conditional.3 = (bf16[576,1024]{1,0:T(8,128)(2,1)}, bf16[576,1024]{1,0:T(8,128)(2,1)}) conditional(s32[]{:T(128)} %bitcast.12, (bf16[576,1024]{1,0:T(8,128)(2,1)}, bf16[576,1024]{1,0:T(8,128)(2,1)}) %tuple.66, (bf16[576,1024]{1,0:T(8,128)(2,1)}, bf16[576,1024]{1,0:T(8,128)(2,1)}) %tuple.66, ...), branch_computations={%region_10.11_spmd, %region_11.12_spmd, %region_12.13_spmd, %regio... | conditional | bytes 9437280 | solution.py:401
  137.1 3.8 %collective-permute-start.16 = (bf16[576,1024]{1,0:T(8,128)(2,1)}, bf16[576,1024]{1,0:T(8,128)(2,1)}, u32[]{:S(2)}, u32[]{:S(2)}) collective-permute-start(bf16[576,1024]{1,0:T(8,128)(2,1)} %get-tuple-element.72), channel_id=1, source_target_pairs={{3,11},{11,3},{7,15},{15,7},{19,27},{27,19},{23,31},{31,23}} | collective-permute-start | bytes 3538952 | tf_op jit(solution)/shard_map/cond/branch_1_fun/ppermute | solution.py:391
  140.9 1.3 collective-permute-start.17
  142.2 70.0 %collective-permute-done.16 = bf16[576,1024]{1,0:T(8,128)(2,1)} collective-permute-done((bf16[576,1024]{1,0:T(8,128)(2,1)}, bf16[576,1024]{1,0:T(8,128)(2,1)}, u32[]{:S(2)}, u32[]{:S(2)}) %collective-permute-start.16) | collective-permute-done | bytes 1179680 | tf_op jit(solution)/shard_map/cond/branch_1_fun/ppermute | solution.py:391
  212.2 0.0 collective-permute-done.17
  212.2 3.5 %conditional.2 = (bf16[576,1024]{1,0:T(8,128)(2,1)}, bf16[576,1024]{1,0:T(8,128)(2,1)}) conditional(s32[]{:T(128)} %bitcast.11, (bf16[576,1024]{1,0:T(8,128)(2,1)}, bf16[576,1024]{1,0:T(8,128)(2,1)}) %tuple.66, (bf16[576,1024]{1,0:T(8,128)(2,1)}, bf16[576,1024]{1,0:T(8,128)(2,1)}) %tuple.66, ...), branch_computations={%region_3.4_spmd, %region_4.5_spmd, %region_5.6_spmd, %region_6.7_... | conditional | bytes 9437280 | solution.py:401
  212.2 1.7 collective-permute-start
  213.9 1.8 collective-permute-start.1
  215.8 3.4 %place.1 = bf16[1152,1536]{1,0:T(8,128)(2,1)} custom-call(s32[1]{0:T(128)} %bitcast.10.source_ref, bf16[1152,256]{1,0:T(8,128)(2,1)S(1)} %copy-done.2, bf16[1152,256]{1,0:T(8,128)(2,1)S(1)} %collective-permute-done.31.refs_1_, bf16[1152,256]{1,0:T(8,128)(2,1)S(1)} %copy-done.1, bf16[1152,256]{1,0:T(8,128)(2,1)S(1)} %collective-permute-done.32.refs_3_, ...), custom_call_target="tpu_custom_call" | custom-call | bytes 7077888 | tf_op jit(solution)/shard_map/place/pallas_call | solution.py:257
  (21 shorter events, 0.0 us)
Async XLA Ops:
  51.3 3.7 %copy-start.3 = (bf16[16,24,2304]{2,1,0:T(8,128)(2,1)}, bf16[16,24,2304]{2,1,0:T(8,128)(2,1)S(1)}, u32[]{:S(2)}) copy-start(bf16[16,24,2304]{2,1,0:T(8,128)(2,1)S(1)} %all_to_all.10) | copy-start | bytes 5308420
  51.3 3.7 %collective-permute-start.28 = (bf16[384,2304]{1,0:T(8,128)(2,1)S(1)}, bf16[384,2304]{1,0:T(8,128)(2,1)S(1)}, u32[]{:S(2)}, u32[]{:S(2)}) collective-permute-start(bf16[384,2304]{1,0:T(8,128)(2,1)S(1)} %bitcast.22), channel_id=1, source_target_pairs={{0,16},{16,0},{1,17},{17,1},{2,18},{18,2},{3,19},{19,3},{4,20},{20... | collective-permute-start | bytes 5308424 | tf_op jit(solution)/shard_map/ppermute | solution.py:317
  55.0 1.2 copy-start.4
  77.4 2.6 %collective-permute-start.30 = (bf16[384,1152]{1,0:T(8,128)(2,1)}, bf16[384,1152]{1,0:T(8,128)(2,1)S(1)}, u32[]{:S(2)}, u32[]{:S(2)}) collective-permute-start(bf16[384,1152]{1,0:T(8,128)(2,1)} %get-tuple-element.107), channel_id=1, source_target_pairs={{0,16},{16,0},{1,17},{17,1},{2,18},{18,2},{3,19},{19,3},{4,20},{20... | collective-permute-start | bytes 2654216 | tf_op jit(solution)/shard_map/ppermute | solution.py:317
  82.4 52.5 %all-to-all-start.1 = ((bf16[16,24,1152]{2,1,0:T(8,128)(2,1)}), bf16[16,24,1152]{2,1,0:T(8,128)(2,1)}, u32[]{:S(2)}, u32[]{:S(2)}) async-start(bf16[16,24,1152]{2,1,0:T(8,128)(2,1)} %bitcast.8), calls=%async_computation.1 | async-start | bytes 1769472 | tf_op jit(solution)/shard_map/all_to_all | solution.py:362
  95.0 7.4 %copy-start.2 = (bf16[1152,256]{1,0:T(8,128)(2,1)S(1)}, bf16[1152,256]{1,0:T(8,128)(2,1)}, u32[]{:S(2)}) copy-start(bf16[1152,256]{1,0:T(8,128)(2,1)} %get-tuple-element.109.refs_0_) | copy-start | bytes 1769476
  95.0 7.9 %copy-start.5 = (s32[16]{0:T(128)S(1)}, s32[16]{0:T(128)}, u32[]{:S(2)}) copy-start(s32[16]{0:T(128)} %param.30) | copy-start | bytes 196
  95.0 7.9 %copy-start.6 = (pred[16]{0:T(512)(128)(4,1)S(1)}, pred[16]{0:T(512)(128)(4,1)}, u32[]{:S(2)}) copy-start(pred[16]{0:T(512)(128)(4,1)} %constant.32.clone) | copy-start | bytes 52
  95.0 11.3 %copy-start.8 = (s32[256]{0:T(256)S(1)}, s32[256]{0:T(256)}, u32[]{:S(2)}) copy-start(s32[256]{0:T(256)} %constant.31.clone) | copy-start | bytes 3076
  95.0 11.9 %copy-start.7 = (s32[256]{0:T(256)S(1)}, s32[256]{0:T(256)}, u32[]{:S(2)}) copy-start(s32[256]{0:T(256)} %constant.30.clone) | copy-start | bytes 3076
  95.0 42.1 %collective-permute-start.29 = (bf16[576,1024]{1,0:T(8,128)(2,1)}, bf16[576,1024]{1,0:T(8,128)(2,1)}, u32[]{:S(2)}, u32[]{:S(2)}) collective-permute-start(bf16[576,1024]{1,0:T(8,128)(2,1)} %shard_map.137.refs_7_), channel_id=1, source_target_pairs={{0,1},{1,0},{2,3},{3,2},{4,5},{5,4},{6,7},{7,6},{8,9},{9,8},{10,11... | collective-permute-start | bytes 3538952 | tf_op jit(solution)/shard_map/ppermute | solution.py:382
  100.0 115.8 %collective-permute-start.32 = (bf16[1152,256]{1,0:T(8,128)(2,1)}, bf16[1152,256]{1,0:T(8,128)(2,1)S(1)}, u32[]{:S(2)}, u32[]{:S(2)}) collective-permute-start(bf16[1152,256]{1,0:T(8,128)(2,1)} %shard_map.138.refs_2_), channel_id=1, source_target_pairs={{0,8},{1,9},{2,10},{3,11},{4,12},{5,13},{6,14},{7,15},{8,0},{9,1},... | collective-permute-start | bytes 1769480 | tf_op jit(solution)/shard_map/ppermute | solution.py:375
  102.4 113.3 %collective-permute-start.31 = (bf16[1152,256]{1,0:T(8,128)(2,1)S(1)}, bf16[1152,256]{1,0:T(8,128)(2,1)S(1)}, u32[]{:S(2)}, u32[]{:S(2)}) collective-permute-start(bf16[1152,256]{1,0:T(8,128)(2,1)S(1)} %copy-done.2), channel_id=1, source_target_pairs={{0,8},{1,9},{2,10},{3,11},{4,12},{5,13},{6,14},{7,15},{8,0},{9,1},... | collective-permute-start | bytes 1769480 | tf_op jit(solution)/shard_map/ppermute | solution.py:355
  109.4 106.4 %copy-start.1 = (bf16[1152,256]{1,0:T(8,128)(2,1)S(1)}, bf16[1152,256]{1,0:T(8,128)(2,1)}, u32[]{:S(2)}) copy-start(bf16[1152,256]{1,0:T(8,128)(2,1)} %shard_map.138.refs_2_) | copy-start | bytes 1769476
  115.8 100.0 %copy-start = (bf16[576,1024]{1,0:T(8,128)(2,1)S(1)}, bf16[576,1024]{1,0:T(8,128)(2,1)}, u32[]{:S(2)}) copy-start(bf16[576,1024]{1,0:T(8,128)(2,1)} %shard_map.137.refs_7_) | copy-start | bytes 3538948
  137.1 75.1 %collective-permute-start.16 = (bf16[576,1024]{1,0:T(8,128)(2,1)}, bf16[576,1024]{1,0:T(8,128)(2,1)}, u32[]{:S(2)}, u32[]{:S(2)}) collective-permute-start(bf16[576,1024]{1,0:T(8,128)(2,1)} %get-tuple-element.72), channel_id=1, source_target_pairs={{3,11},{11,3},{7,15},{15,7},{19,27},{27,19},{23,31},{31,23}} | collective-permute-start | bytes 3538952 | tf_op jit(solution)/shard_map/cond/branch_1_fun/ppermute | solution.py:391
  140.9 71.3 %collective-permute-start.17 = (bf16[576,1024]{1,0:T(8,128)(2,1)}, bf16[576,1024]{1,0:T(8,128)(2,1)}, u32[]{:S(2)}, u32[]{:S(2)}) collective-permute-start(bf16[576,1024]{1,0:T(8,128)(2,1)} %get-tuple-element.73), channel_id=1, source_target_pairs={{2,11},{10,3},{6,15},{14,7},{18,27},{26,19},{22,31},{30,23}} | collective-permute-start | bytes 3538952 | tf_op jit(solution)/shard_map/cond/branch_1_fun/ppermute | solution.py:392
  212.2 3.5 %collective-permute-start = (bf16[576,1024]{1,0:T(8,128)(2,1)}, bf16[576,1024]{1,0:T(8,128)(2,1)}, u32[]{:S(2)}, u32[]{:S(2)}) collective-permute-start(bf16[576,1024]{1,0:T(8,128)(2,1)} %get-tuple-element.56), channel_id=1, source_target_pairs={{0,8},{8,0},{1,9},{9,1},{16,24},{24,16},{17,25},{25,17}} | collective-permute-start | bytes 3538952 | tf_op jit(solution)/shard_map/cond/branch_0_fun/ppermute | solution.py:391
  213.9 1.8 collective-permute-start.1

commit v3 on v2

--- a/solution.py
+++ b/solution.py
@@ -296,20 +296,38 @@
     return switches
 
 
-def combine_kernel(where_ref, back_ref, out_ref):
-    slots, tok_count = back_ref.shape[0], out_ref.shape[0]
-    row = lax.broadcasted_iota(jnp.int32, (slots, tok_count), 0)
-    pick = (row == where_ref[0:1, :]) | (row == where_ref[1:2, :])
-    pick = jnp.where(pick, 1.0, 0.0).astype(bf16)
-    out_ref[...] = mxu(pick, back_ref[...], TN).astype(bf16)
-
-
-def combine_rows(where_to, returned, tok_count):
-    return pl.pallas_call(
-        combine_kernel,
-        out_shape=jax.ShapeDtypeStruct((tok_count, returned.shape[1]), bf16),
+def combine_kernel(capacity, half, upper_ref, where_ref, mirror_ref, back_ref, own_ref, sum_ref):
+    slots, tok_count = back_ref.shape[0], own_ref.shape[0]
+    row = lax.broadcasted_iota(jnp.int32, (slots, tok_count), 0).astype(f32)
+    block = jnp.floor((row + 0.5) * (1.0 / capacity))
+    expert = jnp.floor(block * 0.5)
+    side = block - 2.0 * expert
+    upper = upper_ref[0].astype(f32)
+    place_of = (expert + half * upper) * capacity + (row - block * capacity)
+    for ref, out, wanted in ((where_ref, own_ref, upper), (mirror_ref, sum_ref, 1.0 - upper)):
+        first, second = ref[0:1, :].astype(f32), ref[1:2, :].astype(f32)
+        hit = ((place_of == first) | (place_of == second)) & (side == wanted)
+        pick = jnp.where(hit, 1.0, 0.0).astype(bf16)
+        out[...] = mxu(pick, back_ref[...], TN).astype(out.dtype)
+
+
+def combine_rows(upper, where_to, mirror_to, returned, tok_count, capacity, half):
+    width = returned.shape[1]
+    vmem = pl.BlockSpec(memory_space=pltpu.VMEM)
+    return pl.pallas_call(
+        functools.partial(combine_kernel, capacity, half),
+        in_specs=[pl.BlockSpec(memory_space=pltpu.SMEM), vmem, vmem, vmem],
+        out_shape=(
+            jax.ShapeDtypeStruct((tok_count, width), f32),
+            jax.ShapeDtypeStruct((tok_count, width), bf16),
+        ),
+        cost_estimate=pl.CostEstimate(
+            flops=4 * tok_count * returned.shape[0] * width,
+            bytes_accessed=2 * returned.size + 6 * tok_count * width,
+            transcendentals=0,
+        ),
         name="combine_rows",
-    )(where_to, returned)
+    )(upper, where_to, mirror_to, returned)
 
 
 def dp_shift(block, apart):
@@ -359,15 +377,21 @@
     total = parts[0].astype(f32)
     for d in range(1, dp_count):
         total = total + dp_shift(parts[d], d).astype(f32)
+    total = total.astype(bf16).reshape(2, half, capacity, width).transpose(1, 0, 2, 3)
     returned = lax.all_to_all(
-        total.astype(bf16).reshape(expert_count, capacity, width),
+        total.reshape(half, 2 * capacity, width),
         "expert",
         split_axis=0,
         concat_axis=0,
+        axis_index_groups=[list(range(half)), list(range(half, expert_count))],
         tiled=True,
     ).reshape(slots, width)
-
-    x_grad = combine_rows(where_to, returned, tok_count)
+    upper = (own_index >= half).astype(jnp.int32).reshape(1)
+    mirror_to = lax.ppermute(where_to, "expert", route)
+    own_sum, mirror_sum = combine_rows(
+        upper, where_to, mirror_to, returned, tok_count, capacity, half
+    )
+    x_grad = (own_sum + lax.ppermute(mirror_sum, "expert", route).astype(f32)).astype(bf16)
     switches = swap_plans(half) if tiles > 2 else []
     direct = 1 if switches else tiles - 1
     moments = (first_moment[0], second_moment[0])

time: 220 us -> 228 us (1.036)
  waiting for transfers between devices: 95.3 us -> 101 us
    ppermute x0 -> x2, waiting for transfers between devices: none -> 24.2 us  [the longest x1 20 us: shards(): lax.ppermute(mirror_sum, 'expert', route).astype(f32)]
    all_to_all x1, waiting for transfers between devices: 19.1 us -> 0.94 us  [shards(): lax.all_to_all(total.reshape(half, 2 * capacity, width), 'expert', split_...]
  transfers between devices with their start and end apart: 10 -> 12, of which waited for: 4 -> 6; matrix products, arithmetic and copies ran while one was open for 1% -> 2% of each run, Pallas kernels for 9% -> 9%
where the time goes in v3:
time: 228 us
  waiting for transfers between devices  101 us (44%)
  blocking collectives  47.6 us (21%)
  Pallas kernels  47.2 us (21%)
  starting transfers between devices  17.8 us (8%)
  between operations  5.45 us (2%)
  local copies, waits for them, and re-layouts  4.61 us (2%)
  other arithmetic  3.83 us (2%)
    ppermute x2, waiting for transfers between devices, run(): lax.ppermute(near, 'expert', pairs)  70 us
    all_to_all x1, blocking collectives, shards(): lax.all_to_all(rows.reshape(expert_count, capacity, 2 * width), 'expert',...  47.6 us
    ppermute x1, waiting for transfers between devices, shards(): lax.ppermute(mirror_sum, 'expert', route).astype(f32)  20 us
    pallas_call x3, Pallas kernels, adam_block(): pl.pallas_call(adam_kernel, grid=(tiles,), in_specs=[pl.BlockSpec((rows,...  17 us
    pallas_call x1, Pallas kernels, rest_step(): pl.pallas_call(functools.partial(rest_kernel, len(rows)), grid=(tiles,),...  14.6 us
    pallas_call x1, Pallas kernels, first_step(): pl.pallas_call(functools.partial(first_kernel, len(rows)), grid=(1,), in_...  6.58 us
    ppermute x2, waiting for transfers between devices, dp_shift(): return lax.ppermute(block, 'dp', [(i, i ^ apart) for i in range(count)])  6.18 us
    all_to_all x1, starting transfers between devices, shards(): lax.all_to_all(total.reshape(half, 2 * capacity, width), 'expert', split_...  5.7 us
  transfers between devices with their start and end apart: 12, of which 6 were waited for; matrix products, arithmetic and copies ran while one was open for 2% of the time, Pallas kernels for 9%

profile of v3, /device:TPU:6, one launch (start us, length us, event | category | flops | bytes accessed | tf_op | source)
XLA Modules:
  0.0 227.8 jit_solution(11250185705796845306)
XLA Ops:
  0.6 3.1 %pack_rows.1 = (bf16[384,2304]{1,0:T(8,128)(2,1)}, s32[2,128]{1,0:T(2,128)}) custom-call(s32[2,128]{1,0:T(2,128)} %bitcast.38, f32[2,128]{1,0:T(2,128)} %bitcast.39, bf16[128,1152]{1,0:T(8,128)(2,1)} %x_ref.1, bf16[128,1152]{1,0:T(8,128)(2,1)} %g_ref.1), custom_call_target="tpu_custom_call" | custom-call | tf_op jit(solution)/shard_map/pack_rows/pallas_call | solution.py:88
  3.7 47.6 %all_to_all.10 = bf16[16,24,2304]{2,1,0:T(8,128)(2,1)S(1)} all-to-all(bf16[16,24,2304]{2,1,0:T(8,128)(2,1)} %bitcast.37), channel_id=1, replica_groups=mesh['dp'=2,'expert'=16] {'expert'}, dimensions={0} | all-to-all | bytes 3538944 | tf_op jit(solution)/shard_map/all_to_all | solution.py:355
  51.3 3.7 %collective-permute-done.28.refs_1_ = bf16[384,2304]{1,0:T(8,128)(2,1)S(1)} collective-permute-done((bf16[384,2304]{1,0:T(8,128)(2,1)S(1)}, bf16[384,2304]{1,0:T(8,128)(2,1)S(1)}, u32[]{:S(2)}, u32[]{:S(2)}) %collective-permute-start.28) | collective-permute-done | bytes 1769504 | tf_op jit(solution)/shard_map/ppermute | solution.py:335
  55.0 1.2 copy-done.5
  56.2 6.6 %first_step.1 = (bf16[1152,256]{1,0:T(8,128)(2,1)}, bf16[768,256]{1,0:T(8,128)(2,1)}, bf16[1152,768]{1,0:T(8,128)(2,1)}) custom-call(bf16[384,2304]{1,0:T(8,128)(2,1)} %bitcast.27, bf16[384,2304]{1,0:T(8,128)(2,1)} %copy-done.5, bf16[1152,1536]{1,0:T(8,128)(2,1)} %bitcast.29, bf16[1536,1152]{1,0:T(8,128)(2,1)} %bitcast.32, f32[1152,1536]{1,0:T(8,128)} %bitcast.18, ...), custom_call_target="tpu_custom_call" | custom-call | flops 1358954496 | bytes 4128768 | tf_op jit(solution)/shard_map/first_step/pallas_call | solution.py:122
  62.8 14.6 %rest_step.1 = (bf16[768,1280]{1,0:T(8,128)(2,1)}, bf16[384,1152]{1,0:T(8,128)(2,1)}, bf16[384,1152]{1,0:T(8,128)(2,1)}) custom-call(bf16[384,2304]{1,0:T(8,128)(2,1)} %bitcast.28, bf16[384,2304]{1,0:T(8,128)(2,1)} %copy-done.5, bf16[768,256]{1,0:T(8,128)(2,1)} %get-tuple-element.105.refs_2_, bf16[1152,1536]{1,0:T(8,128)(2,1)} %bitcast.30, ...), custom_call_target="tpu_custom_call" | custom-call | flops 6794772480 | bytes 5898240 | tf_op jit(solution)/shard_map/rest_step/pallas_call | solution.py:171
  77.5 2.5 %collective-permute-done.31 = bf16[384,1152]{1,0:T(8,128)(2,1)S(1)} collective-permute-done((bf16[384,1152]{1,0:T(8,128)(2,1)}, bf16[384,1152]{1,0:T(8,128)(2,1)S(1)}, u32[]{:S(2)}, u32[]{:S(2)}) %collective-permute-start.31) | collective-permute-done | bytes 884768 | tf_op jit(solution)/shard_map/ppermute | solution.py:335
  80.0 1.4 add_convert_fusion
  81.4 1.0 copy.14
  82.4 5.7 %all-to-all-start.1 = ((bf16[8,48,1152]{2,1,0:T(8,128)(2,1)}), bf16[8,48,1152]{2,1,0:T(8,128)(2,1)S(1)}, u32[]{:S(2)}, u32[]{:S(2)}) async-start(bf16[8,48,1152]{2,1,0:T(8,128)(2,1)} %bitcast.11), calls=%async_computation.1 | async-start | bytes 1769472 | tf_op jit(solution)/shard_map/all_to_all | solution.py:381
  88.1 6.3 %shard_map.137.refs_7_ = bf16[576,1024]{1,0:T(8,128)(2,1)} custom-call(bf16[1152,768]{1,0:T(8,128)(2,1)} %get-tuple-element.104.xt_ref, bf16[768,1280]{1,0:T(8,128)(2,1)} %get-tuple-element.106.pre_ref, f32[1152,1536]{1,0:T(8,128)} %bitcast.19, f32[1152,1536]{1,0:T(8,128)} %bitcast.23), custom_call_target="tpu_custom_call" | custom-call | flops 905969664 | bytes 5898240 | tf_op jit(solution)/shard_map/pallas_call | solution.py:205
  95.3 4.1 %collective-permute-done.30.mirror_ref = s32[2,128]{1,0:T(2,128)S(1)} collective-permute-done((s32[2,128]{1,0:T(2,128)S(1)}, s32[2,128]{1,0:T(2,128)S(1)}, u32[]{:S(2)}, u32[]{:S(2)}) %collective-permute-start.30) | collective-permute-done | bytes 1056 | tf_op jit(solution)/shard_map/ppermute | solution.py:390
  99.5 0.9 all-to-all-done.1
  100.4 1.0 copy-done.4
  101.4 2.5 %combine_rows.1 = (f32[128,1152]{1,0:T(8,128)}, bf16[128,1152]{1,0:T(8,128)(2,1)}) custom-call(s32[1]{0:T(128)} %bitcast.8.upper_ref, s32[2,128]{1,0:T(2,128)} %get-tuple-element.107.where_ref, s32[2,128]{1,0:T(2,128)} %copy-done.8, bf16[384,1152]{1,0:T(8,128)(2,1)} %bitcast.35), custom_call_target="tpu_custom_call" | custom-call | flops 226492416 | bytes 1769472 | tf_op jit(solution)/shard_map/combine_rows/pallas_call | solution.py:317
  103.9 1.5 collective-permute-start.32
  105.4 4.3 %shard_map.138.refs_2_ = bf16[1152,256]{1,0:T(8,128)(2,1)} custom-call(bf16[1152,768]{1,0:T(8,128)(2,1)} %get-tuple-element.104.xt_ref, bf16[768,1280]{1,0:T(8,128)(2,1)} %get-tuple-element.106.pre_ref, f32[1152,1536]{1,0:T(8,128)} %bitcast.20, f32[1152,1536]{1,0:T(8,128)} %bitcast.24), custom_call_target="tpu_custom_call" | custom-call | flops 452984832 | bytes 2949120 | tf_op jit(solution)/shard_map/pallas_call | solution.py:205
  109.7 1.5 collective-permute-start.34
  111.3 1.4 collective-permute-start.33
  112.6 0.7 fusion.2
  116.1 0.7 dynamic_slice.7
  119.5 6.4 %shard_map.136.refs_4_ = bf16[576,1024]{1,0:T(8,128)(2,1)} custom-call(bf16[1152,768]{1,0:T(8,128)(2,1)} %get-tuple-element.104.xt_ref, bf16[768,1280]{1,0:T(8,128)(2,1)} %get-tuple-element.106.pre_ref, f32[1152,1536]{1,0:T(8,128)} %bitcast.21, f32[1152,1536]{1,0:T(8,128)} %bitcast.25), custom_call_target="tpu_custom_call" | custom-call | flops 905969664 | bytes 5898240 | tf_op jit(solution)/shard_map/pallas_call | solution.py:205
  125.9 20.0 %collective-permute-done.32 = bf16[128,1152]{1,0:T(8,128)(2,1)} collective-permute-done((bf16[128,1152]{1,0:T(8,128)(2,1)}, bf16[128,1152]{1,0:T(8,128)(2,1)}, u32[]{:S(2)}, u32[]{:S(2)}) %collective-permute-start.32) | collective-permute-done | bytes 294944 | tf_op jit(solution)/shard_map/ppermute | solution.py:394
  145.9 1.7 add_convert_fusion.1
  147.6 73.2 %conditional.3 = (bf16[576,1024]{1,0:T(8,128)(2,1)}, bf16[576,1024]{1,0:T(8,128)(2,1)}) conditional(s32[]{:T(128)} %bitcast.15, (bf16[576,1024]{1,0:T(8,128)(2,1)}, bf16[576,1024]{1,0:T(8,128)(2,1)}) %tuple.66, (bf16[576,1024]{1,0:T(8,128)(2,1)}, bf16[576,1024]{1,0:T(8,128)(2,1)}) %tuple.66, ...), branch_computations={%region_10.11_spmd, %region_11.12_spmd, %region_12.13_spmd, %regio... | conditional | bytes 9437280 | solution.py:425
  147.6 1.9 collective-permute-start.16
  149.6 1.3 collective-permute-start.17
  150.9 70.0 %collective-permute-done.16 = bf16[576,1024]{1,0:T(8,128)(2,1)} collective-permute-done((bf16[576,1024]{1,0:T(8,128)(2,1)}, bf16[576,1024]{1,0:T(8,128)(2,1)}, u32[]{:S(2)}, u32[]{:S(2)}) %collective-permute-start.16) | collective-permute-done | bytes 1179680 | tf_op jit(solution)/shard_map/cond/branch_1_fun/ppermute | solution.py:415
  220.8 3.4 %conditional.2 = (bf16[576,1024]{1,0:T(8,128)(2,1)}, bf16[576,1024]{1,0:T(8,128)(2,1)}) conditional(s32[]{:T(128)} %bitcast.14, (bf16[576,1024]{1,0:T(8,128)(2,1)}, bf16[576,1024]{1,0:T(8,128)(2,1)}) %tuple.66, (bf16[576,1024]{1,0:T(8,128)(2,1)}, bf16[576,1024]{1,0:T(8,128)(2,1)}) %tuple.66, ...), branch_computations={%region_3.4_spmd, %region_4.5_spmd, %region_5.6_spmd, %region_6.7_... | conditional | bytes 9437280 | solution.py:425
  220.8 1.7 collective-permute-start
  222.6 1.7 collective-permute-start.1
  224.3 3.4 %place.1 = bf16[1152,1536]{1,0:T(8,128)(2,1)} custom-call(s32[1]{0:T(128)} %bitcast.13.source_ref, bf16[1152,256]{1,0:T(8,128)(2,1)S(1)} %copy-done.2, bf16[1152,256]{1,0:T(8,128)(2,1)S(1)} %collective-permute-done.33.refs_1_, bf16[1152,256]{1,0:T(8,128)(2,1)S(1)} %copy-done.1, bf16[1152,256]{1,0:T(8,128)(2,1)S(1)} %collective-permute-done.34.refs_3_, ...), custom_call_target="tpu_custom_call" | custom-call | bytes 7077888 | tf_op jit(solution)/shard_map/place/pallas_call | solution.py:257
  (35 shorter events, 1.8 us)
Async XLA Ops:
  51.3 3.7 %copy-start.3 = (bf16[16,24,2304]{2,1,0:T(8,128)(2,1)}, bf16[16,24,2304]{2,1,0:T(8,128)(2,1)S(1)}, u32[]{:S(2)}) copy-start(bf16[16,24,2304]{2,1,0:T(8,128)(2,1)S(1)} %all_to_all.10) | copy-start | bytes 5308420
  51.3 3.7 %collective-permute-start.28 = (bf16[384,2304]{1,0:T(8,128)(2,1)S(1)}, bf16[384,2304]{1,0:T(8,128)(2,1)S(1)}, u32[]{:S(2)}, u32[]{:S(2)}) collective-permute-start(bf16[384,2304]{1,0:T(8,128)(2,1)S(1)} %bitcast.26), channel_id=1, source_target_pairs={{0,16},{16,0},{1,17},{17,1},{2,18},{18,2},{3,19},{19,3},{4,20},{20... | collective-permute-start | bytes 5308424 | tf_op jit(solution)/shard_map/ppermute | solution.py:335
  55.0 1.3 copy-start.5
  77.4 2.6 %collective-permute-start.31 = (bf16[384,1152]{1,0:T(8,128)(2,1)}, bf16[384,1152]{1,0:T(8,128)(2,1)S(1)}, u32[]{:S(2)}, u32[]{:S(2)}) collective-permute-start(bf16[384,1152]{1,0:T(8,128)(2,1)} %get-tuple-element.109), channel_id=1, source_target_pairs={{0,16},{16,0},{1,17},{17,1},{2,18},{18,2},{3,19},{19,3},{4,20},{20... | collective-permute-start | bytes 2654216 | tf_op jit(solution)/shard_map/ppermute | solution.py:335
  82.4 18.0 %all-to-all-start.1 = ((bf16[8,48,1152]{2,1,0:T(8,128)(2,1)}), bf16[8,48,1152]{2,1,0:T(8,128)(2,1)S(1)}, u32[]{:S(2)}, u32[]{:S(2)}) async-start(bf16[8,48,1152]{2,1,0:T(8,128)(2,1)} %bitcast.11), calls=%async_computation.1 | async-start | bytes 1769472 | tf_op jit(solution)/shard_map/all_to_all | solution.py:381
  88.1 6.9 %copy-start.7 = (s32[2,128]{1,0:T(2,128)S(1)}, s32[2,128]{1,0:T(2,128)}, u32[]{:S(2)}) copy-start(s32[2,128]{1,0:T(2,128)} %get-tuple-element.107.where_ref) | copy-start | bytes 3076
  94.4 53.2 %collective-permute-start.29 = (bf16[576,1024]{1,0:T(8,128)(2,1)}, bf16[576,1024]{1,0:T(8,128)(2,1)}, u32[]{:S(2)}, u32[]{:S(2)}) collective-permute-start(bf16[576,1024]{1,0:T(8,128)(2,1)} %shard_map.137.refs_7_), channel_id=1, source_target_pairs={{0,1},{1,0},{2,3},{3,2},{4,5},{5,4},{6,7},{7,6},{8,9},{9,8},{10,11... | collective-permute-start | bytes 3538952 | tf_op jit(solution)/shard_map/ppermute | solution.py:406
  95.0 4.5 %collective-permute-start.30 = (s32[2,128]{1,0:T(2,128)S(1)}, s32[2,128]{1,0:T(2,128)S(1)}, u32[]{:S(2)}, u32[]{:S(2)}) collective-permute-start(s32[2,128]{1,0:T(2,128)S(1)} %copy-done.7), channel_id=1, source_target_pairs={{0,8},{1,9},{2,10},{3,11},{4,12},{5,13},{6,14},{7,15},{8,0},{9,1},... | collective-permute-start | bytes 3080 | tf_op jit(solution)/shard_map/ppermute | solution.py:390
  99.5 0.9 copy-start.8
  100.4 1.0 copy-start.4
  103.9 7.4 %copy-start.2 = (bf16[1152,256]{1,0:T(8,128)(2,1)S(1)}, bf16[1152,256]{1,0:T(8,128)(2,1)}, u32[]{:S(2)}) copy-start(bf16[1152,256]{1,0:T(8,128)(2,1)} %get-tuple-element.113.refs_0_) | copy-start | bytes 1769476
  103.9 8.7 %copy-start.9 = (s32[16]{0:T(128)S(1)}, s32[16]{0:T(128)}, u32[]{:S(2)}) copy-start(s32[16]{0:T(128)} %param.30) | copy-start | bytes 196
  103.9 8.7 %copy-start.10 = (pred[16]{0:T(512)(128)(4,1)S(1)}, pred[16]{0:T(512)(128)(4,1)}, u32[]{:S(2)}) copy-start(pred[16]{0:T(512)(128)(4,1)} %constant.33.clone) | copy-start | bytes 52
  103.9 12.2 %copy-start.12 = (s32[256]{0:T(256)S(1)}, s32[256]{0:T(256)}, u32[]{:S(2)}) copy-start(s32[256]{0:T(256)} %constant.32.clone) | copy-start | bytes 3076
  103.9 12.8 %copy-start.11 = (s32[256]{0:T(256)S(1)}, s32[256]{0:T(256)}, u32[]{:S(2)}) copy-start(s32[256]{0:T(256)} %constant.31.clone) | copy-start | bytes 3076
  103.9 42.0 %collective-permute-start.32 = (bf16[128,1152]{1,0:T(8,128)(2,1)}, bf16[128,1152]{1,0:T(8,128)(2,1)}, u32[]{:S(2)}, u32[]{:S(2)}) collective-permute-start(bf16[128,1152]{1,0:T(8,128)(2,1)} %get-tuple-element.111), channel_id=1, source_target_pairs={{0,8},{1,9},{2,10},{3,11},{4,12},{5,13},{6,14},{7,15},{8,0},{9,1},... | collective-permute-start | bytes 884744 | tf_op jit(solution)/shard_map/ppermute | solution.py:394
  109.7 114.6 %collective-permute-start.34 = (bf16[1152,256]{1,0:T(8,128)(2,1)}, bf16[1152,256]{1,0:T(8,128)(2,1)S(1)}, u32[]{:S(2)}, u32[]{:S(2)}) collective-permute-start(bf16[1152,256]{1,0:T(8,128)(2,1)} %shard_map.138.refs_2_), channel_id=1, source_target_pairs={{0,8},{1,9},{2,10},{3,11},{4,12},{5,13},{6,14},{7,15},{8,0},{9,1},... | collective-permute-start | bytes 1769480 | tf_op jit(solution)/shard_map/ppermute | solution.py:399
  111.3 113.0 %collective-permute-start.33 = (bf16[1152,256]{1,0:T(8,128)(2,1)S(1)}, bf16[1152,256]{1,0:T(8,128)(2,1)S(1)}, u32[]{:S(2)}, u32[]{:S(2)}) collective-permute-start(bf16[1152,256]{1,0:T(8,128)(2,1)S(1)} %copy-done.2), channel_id=1, source_target_pairs={{0,8},{1,9},{2,10},{3,11},{4,12},{5,13},{6,14},{7,15},{8,0},{9,1},... | collective-permute-start | bytes 1769480 | tf_op jit(solution)/shard_map/ppermute | solution.py:373
  119.4 26.5 %copy-start.6 = (f32[128,1152]{1,0:T(8,128)S(1)}, f32[128,1152]{1,0:T(8,128)}, u32[]{:S(2)}) copy-start(f32[128,1152]{1,0:T(8,128)} %get-tuple-element.110) | copy-start | bytes 1769476
  119.5 104.8 %copy-start.1 = (bf16[1152,256]{1,0:T(8,128)(2,1)S(1)}, bf16[1152,256]{1,0:T(8,128)(2,1)}, u32[]{:S(2)}) copy-start(bf16[1152,256]{1,0:T(8,128)(2,1)} %shard_map.138.refs_2_) | copy-start | bytes 1769476
  125.9 98.4 %copy-start = (bf16[576,1024]{1,0:T(8,128)(2,1)S(1)}, bf16[576,1024]{1,0:T(8,128)(2,1)}, u32[]{:S(2)}) copy-start(bf16[576,1024]{1,0:T(8,128)(2,1)} %shard_map.137.refs_7_) | copy-start | bytes 3538948
  147.6 73.2 %collective-permute-start.16 = (bf16[576,1024]{1,0:T(8,128)(2,1)}, bf16[576,1024]{1,0:T(8,128)(2,1)}, u32[]{:S(2)}, u32[]{:S(2)}) collective-permute-start(bf16[576,1024]{1,0:T(8,128)(2,1)} %get-tuple-element.72), channel_id=1, source_target_pairs={{3,11},{11,3},{7,15},{15,7},{19,27},{27,19},{23,31},{31,23}} | collective-permute-start | bytes 3538952 | tf_op jit(solution)/shard_map/cond/branch_1_fun/ppermute | solution.py:415
  149.6 71.3 %collective-permute-start.17 = (bf16[576,1024]{1,0:T(8,128)(2,1)}, bf16[576,1024]{1,0:T(8,128)(2,1)}, u32[]{:S(2)}, u32[]{:S(2)}) collective-permute-start(bf16[576,1024]{1,0:T(8,128)(2,1)} %get-tuple-element.73), channel_id=1, source_target_pairs={{2,11},{10,3},{6,15},{14,7},{18,27},{26,19},{22,31},{30,23}} | collective-permute-start | bytes 3538952 | tf_op jit(solution)/shard_map/cond/branch_1_fun/ppermute | solution.py:416
  220.8 3.4 %collective-permute-start = (bf16[576,1024]{1,0:T(8,128)(2,1)}, bf16[576,1024]{1,0:T(8,128)(2,1)}, u32[]{:S(2)}, u32[]{:S(2)}) collective-permute-start(bf16[576,1024]{1,0:T(8,128)(2,1)} %get-tuple-element.56), channel_id=1, source_target_pairs={{0,8},{8,0},{1,9},{9,1},{16,24},{24,16},{17,25},{25,17}} | collective-permute-start | bytes 3538952 | tf_op jit(solution)/shard_map/cond/branch_0_fun/ppermute | solution.py:415
  222.6 1.7 collective-permute-start.1

commit v4 on v3

--- a/solution.py
+++ b/solution.py
@@ -222,14 +222,14 @@
     )(x_t, pre_rest, first_moment, second_moment)
 
 
-def place_kernel(boxes, source_ref, *refs):
+def place_kernel(boxes, source_ref, own_ref, other_ref, *refs):
     sources, at = [], 0
     for box in boxes:
         sources.append(refs[at : at + box[4]])
         at += box[4]
-    out_ref = refs[at]
-    bufs = refs[at + 1 : at + 1 + len(boxes)]
-    in_sem, out_sem = refs[at + 1 + len(boxes) :]
+    out_ref, sum_ref = refs[at : at + 2]
+    bufs = refs[at + 2 : at + 2 + len(boxes)]
+    in_sem, out_sem = refs[at + 2 + len(boxes) :]
     for n, arrays in enumerate(sources):
         for k, array in enumerate(arrays):
             last = k == len(arrays) - 1
@@ -239,6 +239,7 @@
             def _(n=n, array=array):
                 pltpu.make_async_copy(array, bufs[n], in_sem.at[n]).start()
 
+    sum_ref[...] = (own_ref[...] + other_ref[...].astype(f32)).astype(bf16)
     puts = []
     for n, (row, col, high, wide, _) in enumerate(boxes):
         pltpu.make_async_copy(sources[n][0], bufs[n], in_sem.at[n]).wait()
@@ -251,15 +252,19 @@
         put.wait()
 
 
-def place(source, pieces, width, inner):
+def place(source, own_sum, other_sum, pieces, width, inner):
     boxes = [piece[:4] + (len(piece[4]),) for piece in pieces]
     args = [array for piece in pieces for array in piece[4]]
     return pl.pallas_call(
         functools.partial(place_kernel, boxes),
         in_specs=[pl.BlockSpec(memory_space=pltpu.SMEM)]
+        + [pl.BlockSpec(memory_space=pltpu.VMEM)] * 2
         + [pl.BlockSpec(memory_space=pl.ANY) for _ in args],
-        out_specs=pl.BlockSpec(memory_space=pl.ANY),
-        out_shape=jax.ShapeDtypeStruct((width, inner), bf16),
+        out_specs=[pl.BlockSpec(memory_space=pl.ANY), pl.BlockSpec(memory_space=pltpu.VMEM)],
+        out_shape=[
+            jax.ShapeDtypeStruct((width, inner), bf16),
+            jax.ShapeDtypeStruct(own_sum.shape, bf16),
+        ],
         scratch_shapes=[pltpu.VMEM((box[2], box[3]), bf16) for box in boxes]
         + [pltpu.SemaphoreType.DMA((len(boxes),)), pltpu.SemaphoreType.DMA((len(boxes),))],
         compiler_params=pltpu.CompilerParams(vmem_limit_bytes=8 * MIB),
@@ -267,7 +272,7 @@
             flops=0, bytes_accessed=4 * width * inner, transcendentals=0
         ),
         name="place",
-    )(source, *args)
+    )(source, own_sum, other_sum, *args)
 
 
 def swap_plans(half):
@@ -391,7 +396,7 @@
     own_sum, mirror_sum = combine_rows(
         upper, where_to, mirror_to, returned, tok_count, capacity, half
     )
-    x_grad = (own_sum + lax.ppermute(mirror_sum, "expert", route).astype(f32)).astype(bf16)
+    other_sum = lax.ppermute(mirror_sum, "expert", route)
     switches = swap_plans(half) if tiles > 2 else []
     direct = 1 if switches else tiles - 1
     moments = (first_moment[0], second_moment[0])
@@ -418,11 +423,14 @@
 
             return run
 
-        near, lent, x_grad = lax.optimization_barrier((near, lent, x_grad))
+        choices = [
+            lax.dynamic_index_in_dim(jnp.asarray(table, jnp.int32), moved_mask, keepdims=False)
+            for _, table in switches
+        ]
+        near, lent, own_sum = lax.optimization_barrier((near, lent, own_sum))
         near_all, far_all = [near], [far]
         for n, (plans, table) in enumerate(switches):
-            choice = jnp.asarray(table, jnp.int32)[moved_mask]
-            near_got, far_got = lax.switch(choice, [branch(p) for p in plans], near, lent)
+            near_got, far_got = lax.switch(choices[n], [branch(p) for p in plans], near, lent)
             near_all.append(near_got)
             far_all.append(far_got)
             members = {e for plan in plans for p in plan for e in (p, p ^ half)}
@@ -433,7 +441,7 @@
         pieces.append((width // 2, at * tile, width // 2, wide, far_all))
 
     source = (is_moved * (1 + group)).reshape(1)
-    adam_out = place(source, pieces, width, inner)
+    adam_out, x_grad = place(source, own_sum, other_sum, pieces, width, inner)
     return (x_grad, adam_out[None])
 
 

time: 228 us -> 240 us (1.053)
  the two profiles are of different devices: /device:TPU:6 before, /device:TPU:7 now
where the time goes in v4:
time: 240 us; the launch traced here: 239 us
  waiting for transfers between devices  112 us (47%)
  Pallas kernels  48.9 us (20%)
  blocking collectives  46.3 us (19%)
  starting transfers between devices  19.5 us (8%)
  local copies, waits for them, and re-layouts  5.42 us (2%)
  between operations  5.1 us (2%)
    ppermute x1, waiting for transfers between devices, shards(): mirror_to = lax.ppermute(where_to, 'expert', route)  50.9 us
    ppermute x2, waiting for transfers between devices, run(): lax.ppermute(near, 'expert', pairs)  48.9 us
    all_to_all x1, blocking collectives, shards(): lax.all_to_all(rows.reshape(expert_count, capacity, 2 * width), 'expert',...  46.3 us
    pallas_call x3, Pallas kernels, adam_block(): pl.pallas_call(adam_kernel, grid=(tiles,), in_specs=[pl.BlockSpec((rows,...  17.1 us
    pallas_call x1, Pallas kernels, rest_step(): pl.pallas_call(functools.partial(rest_kernel, len(rows)), grid=(tiles,),...  14.6 us
    pallas_call x1, Pallas kernels, first_step(): pl.pallas_call(functools.partial(first_kernel, len(rows)), grid=(1,), in_...  6.58 us
    ppermute x2, waiting for transfers between devices, run(): lax.ppermute(lent, 'expert', skew)  6.53 us
    ppermute x2, starting transfers between devices, run(): lax.ppermute(near, 'expert', pairs)  6.03 us
  transfers between devices with their start and end apart: 12, of which 5 were waited for; matrix products, arithmetic and copies ran while one was open for 1% of the time, Pallas kernels for 8%

profile of v4, /device:TPU:7, one launch (start us, length us, event | category | flops | bytes accessed | tf_op | source)
XLA Modules:
  0.0 239.3 jit_solution(7569358202231786788)
XLA Ops:
  0.6 3.1 %pack_rows.1 = (bf16[384,2304]{1,0:T(8,128)(2,1)}, s32[2,128]{1,0:T(2,128)}) custom-call(s32[2,128]{1,0:T(2,128)} %bitcast.37, f32[2,128]{1,0:T(2,128)} %bitcast.38, bf16[128,1152]{1,0:T(8,128)(2,1)} %x_ref.1, bf16[128,1152]{1,0:T(8,128)(2,1)} %g_ref.1), custom_call_target="tpu_custom_call" | custom-call | tf_op jit(solution)/shard_map/pack_rows/pallas_call | solution.py:88
  3.7 46.3 %all_to_all.10 = bf16[16,24,2304]{2,1,0:T(8,128)(2,1)S(1)} all-to-all(bf16[16,24,2304]{2,1,0:T(8,128)(2,1)} %bitcast.36), channel_id=1, replica_groups=mesh['dp'=2,'expert'=16] {'expert'}, dimensions={0} | all-to-all | bytes 3538944 | tf_op jit(solution)/shard_map/all_to_all | solution.py:360
  50.0 2.0 collective-permute-start.28
  52.0 3.3 %collective-permute-done.28.refs_1_ = bf16[384,2304]{1,0:T(8,128)(2,1)S(1)} collective-permute-done((bf16[384,2304]{1,0:T(8,128)(2,1)S(1)}, bf16[384,2304]{1,0:T(8,128)(2,1)S(1)}, u32[]{:S(2)}, u32[]{:S(2)}) %collective-permute-start.28) | collective-permute-done | bytes 1769504 | tf_op jit(solution)/shard_map/ppermute | solution.py:340
  55.3 1.3 copy-done.6
  56.6 6.6 %first_step.1 = (bf16[1152,256]{1,0:T(8,128)(2,1)}, bf16[768,256]{1,0:T(8,128)(2,1)}, bf16[1152,768]{1,0:T(8,128)(2,1)}) custom-call(bf16[384,2304]{1,0:T(8,128)(2,1)} %bitcast.27, bf16[384,2304]{1,0:T(8,128)(2,1)} %copy-done.6, bf16[1152,1536]{1,0:T(8,128)(2,1)} %bitcast.29, bf16[1536,1152]{1,0:T(8,128)(2,1)} %bitcast.32, f32[1152,1536]{1,0:T(8,128)} %bitcast.18, ...), custom_call_target="tpu_custom_call" | custom-call | flops 1358954496 | bytes 4128768 | tf_op jit(solution)/shard_map/first_step/pallas_call | solution.py:122
  63.1 14.6 %rest_step.1 = (bf16[768,1280]{1,0:T(8,128)(2,1)}, bf16[384,1152]{1,0:T(8,128)(2,1)}, bf16[384,1152]{1,0:T(8,128)(2,1)}) custom-call(bf16[384,2304]{1,0:T(8,128)(2,1)} %bitcast.28, bf16[384,2304]{1,0:T(8,128)(2,1)} %copy-done.6, bf16[768,256]{1,0:T(8,128)(2,1)} %get-tuple-element.107.refs_2_, bf16[1152,1536]{1,0:T(8,128)(2,1)} %bitcast.30, ...), custom_call_target="tpu_custom_call" | custom-call | flops 6794772480 | bytes 5898240 | tf_op jit(solution)/shard_map/rest_step/pallas_call | solution.py:171
  77.7 0.4 collective-permute-start.31
  78.1 2.3 collective-permute-done.31
  80.3 1.4 add_convert_fusion
  81.7 1.0 copy.14
  82.7 5.4 %all-to-all-start.1 = ((bf16[8,48,1152]{2,1,0:T(8,128)(2,1)}), bf16[8,48,1152]{2,1,0:T(8,128)(2,1)S(1)}, u32[]{:S(2)}, u32[]{:S(2)}) async-start(bf16[8,48,1152]{2,1,0:T(8,128)(2,1)} %bitcast.12), calls=%async_computation.1 | async-start | bytes 1769472 | tf_op jit(solution)/shard_map/all_to_all | solution.py:386
  88.1 6.3 %shard_map.137.refs_7_ = bf16[576,1024]{1,0:T(8,128)(2,1)} custom-call(bf16[1152,768]{1,0:T(8,128)(2,1)} %get-tuple-element.106.xt_ref, bf16[768,1280]{1,0:T(8,128)(2,1)} %get-tuple-element.108.pre_ref, f32[1152,1536]{1,0:T(8,128)} %bitcast.19, f32[1152,1536]{1,0:T(8,128)} %bitcast.23), custom_call_target="tpu_custom_call" | custom-call | flops 905969664 | bytes 5898240 | tf_op jit(solution)/shard_map/pallas_call | solution.py:205
  94.8 4.3 %shard_map.138.refs_2_ = bf16[1152,256]{1,0:T(8,128)(2,1)} custom-call(bf16[1152,768]{1,0:T(8,128)(2,1)} %get-tuple-element.106.xt_ref, bf16[768,1280]{1,0:T(8,128)(2,1)} %get-tuple-element.108.pre_ref, f32[1152,1536]{1,0:T(8,128)} %bitcast.20, f32[1152,1536]{1,0:T(8,128)} %bitcast.24), custom_call_target="tpu_custom_call" | custom-call | flops 452984832 | bytes 2949120 | tf_op jit(solution)/shard_map/pallas_call | solution.py:205
  99.2 2.3 collective-permute-start.33
  101.6 50.9 %collective-permute-done.30.mirror_ref = s32[2,128]{1,0:T(2,128)S(1)} collective-permute-done((s32[2,128]{1,0:T(2,128)S(1)}, s32[2,128]{1,0:T(2,128)S(1)}, u32[]{:S(2)}, u32[]{:S(2)}) %collective-permute-start.30) | collective-permute-done | bytes 1056 | tf_op jit(solution)/shard_map/ppermute | solution.py:395
  152.5 0.6 copy-done.8
  153.5 2.5 %combine_rows.1 = (f32[128,1152]{1,0:T(8,128)}, bf16[128,1152]{1,0:T(8,128)(2,1)}) custom-call(s32[1]{0:T(128)} %bitcast.9.upper_ref, s32[2,128]{1,0:T(2,128)} %get-tuple-element.109.where_ref, s32[2,128]{1,0:T(2,128)} %copy-done.8, bf16[384,1152]{1,0:T(8,128)(2,1)} %bitcast.34), custom_call_target="tpu_custom_call" | custom-call | flops 226492416 | bytes 1769472 | tf_op jit(solution)/shard_map/combine_rows/pallas_call | solution.py:322
  156.0 0.7 fusion.2
  159.3 0.6 dynamic_slice.8
  159.9 0.6 dynamic_slice.7
  162.2 6.4 %shard_map.136.refs_4_ = bf16[576,1024]{1,0:T(8,128)(2,1)} custom-call(bf16[1152,768]{1,0:T(8,128)(2,1)} %get-tuple-element.106.xt_ref, bf16[768,1280]{1,0:T(8,128)(2,1)} %get-tuple-element.108.pre_ref, f32[1152,1536]{1,0:T(8,128)} %bitcast.21, f32[1152,1536]{1,0:T(8,128)} %bitcast.25), custom_call_target="tpu_custom_call" | custom-call | flops 905969664 | bytes 5898240 | tf_op jit(solution)/shard_map/pallas_call | solution.py:205
  168.7 61.0 %conditional.3 = (bf16[576,1024]{1,0:T(8,128)(2,1)}, bf16[576,1024]{1,0:T(8,128)(2,1)}) conditional(s32[]{:T(128)} %bitcast.15, (bf16[576,1024]{1,0:T(8,128)(2,1)}, bf16[576,1024]{1,0:T(8,128)(2,1)}) %tuple.66, (bf16[576,1024]{1,0:T(8,128)(2,1)}, bf16[576,1024]{1,0:T(8,128)(2,1)}) %tuple.66, ...), branch_computations={%region_10.11_spmd, %region_11.12_spmd, %region_12.13_spmd, %regio... | conditional | bytes 9437280 | solution.py:433
  168.7 4.3 %collective-permute-start.16 = (bf16[576,1024]{1,0:T(8,128)(2,1)}, bf16[576,1024]{1,0:T(8,128)(2,1)}, u32[]{:S(2)}, u32[]{:S(2)}) collective-permute-start(bf16[576,1024]{1,0:T(8,128)(2,1)} %get-tuple-element.72), channel_id=1, source_target_pairs={{3,11},{11,3},{7,15},{15,7},{19,27},{27,19},{23,31},{31,23}} | collective-permute-start | bytes 3538952 | tf_op jit(solution)/shard_map/cond/branch_1_fun/ppermute | solution.py:420
  172.9 1.3 collective-permute-start.17
  174.2 48.9 %collective-permute-done.16 = bf16[576,1024]{1,0:T(8,128)(2,1)} collective-permute-done((bf16[576,1024]{1,0:T(8,128)(2,1)}, bf16[576,1024]{1,0:T(8,128)(2,1)}, u32[]{:S(2)}, u32[]{:S(2)}) %collective-permute-start.16) | collective-permute-done | bytes 1179680 | tf_op jit(solution)/shard_map/cond/branch_1_fun/ppermute | solution.py:420
  223.1 6.5 %collective-permute-done.17 = bf16[576,1024]{1,0:T(8,128)(2,1)} collective-permute-done((bf16[576,1024]{1,0:T(8,128)(2,1)}, bf16[576,1024]{1,0:T(8,128)(2,1)}, u32[]{:S(2)}, u32[]{:S(2)}) %collective-permute-start.17) | collective-permute-done | bytes 1179680 | tf_op jit(solution)/shard_map/cond/branch_1_fun/ppermute | solution.py:421
  229.7 3.4 %conditional.2 = (bf16[576,1024]{1,0:T(8,128)(2,1)}, bf16[576,1024]{1,0:T(8,128)(2,1)}) conditional(s32[]{:T(128)} %bitcast.14, (bf16[576,1024]{1,0:T(8,128)(2,1)}, bf16[576,1024]{1,0:T(8,128)(2,1)}) %tuple.66, (bf16[576,1024]{1,0:T(8,128)(2,1)}, bf16[576,1024]{1,0:T(8,128)(2,1)}) %tuple.66, ...), branch_computations={%region_3.4_spmd, %region_4.5_spmd, %region_5.6_spmd, %region_6.7_... | conditional | bytes 9437280 | solution.py:433
  229.7 1.8 collective-permute-start
  231.4 1.7 collective-permute-start.1
  233.2 1.1 copy-done.3
  234.2 5.1 %place.1 = (bf16[1152,1536]{1,0:T(8,128)(2,1)}, bf16[128,1152]{1,0:T(8,128)(2,1)}) custom-call(s32[1]{0:T(128)} %bitcast.source_ref, f32[128,1152]{1,0:T(8,128)S(1)} %copy-done.3, bf16[128,1152]{1,0:T(8,128)(2,1)} %collective-permute-done.32.other_ref, bf16[1152,256]{1,0:T(8,128)(2,1)S(1)} %copy-done.2, ...), custom_call_target="tpu_custom_call" | custom-call | bytes 7077888 | tf_op jit(solution)/shard_map/place/pallas_call | solution.py:258
  (34 shorter events, 0.9 us)
Async XLA Ops:
  50.0 5.3 %copy-start.4 = (bf16[16,24,2304]{2,1,0:T(8,128)(2,1)}, bf16[16,24,2304]{2,1,0:T(8,128)(2,1)S(1)}, u32[]{:S(2)}) copy-start(bf16[16,24,2304]{2,1,0:T(8,128)(2,1)S(1)} %all_to_all.10) | copy-start | bytes 5308420
  50.0 5.3 %collective-permute-start.28 = (bf16[384,2304]{1,0:T(8,128)(2,1)S(1)}, bf16[384,2304]{1,0:T(8,128)(2,1)S(1)}, u32[]{:S(2)}, u32[]{:S(2)}) collective-permute-start(bf16[384,2304]{1,0:T(8,128)(2,1)S(1)} %bitcast.26), channel_id=1, source_target_pairs={{0,16},{16,0},{1,17},{17,1},{2,18},{18,2},{3,19},{19,3},{4,20},{20... | collective-permute-start | bytes 5308424 | tf_op jit(solution)/shard_map/ppermute | solution.py:340
  55.3 1.3 copy-start.6
  77.7 2.6 %collective-permute-start.31 = (bf16[384,1152]{1,0:T(8,128)(2,1)}, bf16[384,1152]{1,0:T(8,128)(2,1)S(1)}, u32[]{:S(2)}, u32[]{:S(2)}) collective-permute-start(bf16[384,1152]{1,0:T(8,128)(2,1)} %get-tuple-element.111), channel_id=1, source_target_pairs={{0,16},{16,0},{1,17},{17,1},{2,18},{18,2},{3,19},{19,3},{4,20},{20... | collective-permute-start | bytes 2654216 | tf_op jit(solution)/shard_map/ppermute | solution.py:340
  82.7 69.8 %all-to-all-start.1 = ((bf16[8,48,1152]{2,1,0:T(8,128)(2,1)}), bf16[8,48,1152]{2,1,0:T(8,128)(2,1)S(1)}, u32[]{:S(2)}, u32[]{:S(2)}) async-start(bf16[8,48,1152]{2,1,0:T(8,128)(2,1)} %bitcast.12), calls=%async_computation.1 | async-start | bytes 1769472 | tf_op jit(solution)/shard_map/all_to_all | solution.py:386
  94.4 4.8 %copy-start.2 = (bf16[1152,256]{1,0:T(8,128)(2,1)S(1)}, bf16[1152,256]{1,0:T(8,128)(2,1)}, u32[]{:S(2)}) copy-start(bf16[1152,256]{1,0:T(8,128)(2,1)} %get-tuple-element.115.refs_0_) | copy-start | bytes 1769476
  94.4 7.1 %copy-start.7 = (s32[2,128]{1,0:T(2,128)S(1)}, s32[2,128]{1,0:T(2,128)}, u32[]{:S(2)}) copy-start(s32[2,128]{1,0:T(2,128)} %get-tuple-element.109.where_ref) | copy-start | bytes 3076
  94.4 61.6 %copy-start.9 = (s32[16]{0:T(128)S(1)}, s32[16]{0:T(128)}, u32[]{:S(2)}) copy-start(s32[16]{0:T(128)} %param.30) | copy-start | bytes 196
  94.5 61.5 %copy-start.10 = (pred[16]{0:T(512)(128)(4,1)S(1)}, pred[16]{0:T(512)(128)(4,1)}, u32[]{:S(2)}) copy-start(pred[16]{0:T(512)(128)(4,1)} %constant.38.clone) | copy-start | bytes 52
  94.5 64.8 %copy-start.12 = (s32[256]{0:T(256)S(1)}, s32[256]{0:T(256)}, u32[]{:S(2)}) copy-start(s32[256]{0:T(256)} %constant.37.clone) | copy-start | bytes 3076
  94.5 65.4 %copy-start.11 = (s32[256]{0:T(256)S(1)}, s32[256]{0:T(256)}, u32[]{:S(2)}) copy-start(s32[256]{0:T(256)} %constant.36.clone) | copy-start | bytes 3076
  94.5 74.2 %collective-permute-start.29 = (bf16[576,1024]{1,0:T(8,128)(2,1)}, bf16[576,1024]{1,0:T(8,128)(2,1)}, u32[]{:S(2)}, u32[]{:S(2)}) collective-permute-start(bf16[576,1024]{1,0:T(8,128)(2,1)} %shard_map.137.refs_7_), channel_id=1, source_target_pairs={{0,1},{1,0},{2,3},{3,2},{4,5},{5,4},{6,7},{7,6},{8,9},{9,8},{10,11... | collective-permute-start | bytes 3538952 | tf_op jit(solution)/shard_map/ppermute | solution.py:411
  99.1 134.0 %collective-permute-start.34 = (bf16[1152,256]{1,0:T(8,128)(2,1)}, bf16[1152,256]{1,0:T(8,128)(2,1)S(1)}, u32[]{:S(2)}, u32[]{:S(2)}) collective-permute-start(bf16[1152,256]{1,0:T(8,128)(2,1)} %shard_map.138.refs_2_), channel_id=1, source_target_pairs={{0,8},{1,9},{2,10},{3,11},{4,12},{5,13},{6,14},{7,15},{8,0},{9,1},... | collective-permute-start | bytes 1769480 | tf_op jit(solution)/shard_map/ppermute | solution.py:404
  99.2 133.9 %collective-permute-start.33 = (bf16[1152,256]{1,0:T(8,128)(2,1)S(1)}, bf16[1152,256]{1,0:T(8,128)(2,1)S(1)}, u32[]{:S(2)}, u32[]{:S(2)}) collective-permute-start(bf16[1152,256]{1,0:T(8,128)(2,1)S(1)} %copy-done.2), channel_id=1, source_target_pairs={{0,8},{1,9},{2,10},{3,11},{4,12},{5,13},{6,14},{7,15},{8,0},{9,1},... | collective-permute-start | bytes 1769480 | tf_op jit(solution)/shard_map/ppermute | solution.py:378
  101.5 51.0 %collective-permute-start.30 = (s32[2,128]{1,0:T(2,128)S(1)}, s32[2,128]{1,0:T(2,128)S(1)}, u32[]{:S(2)}, u32[]{:S(2)}) collective-permute-start(s32[2,128]{1,0:T(2,128)S(1)} %copy-done.7), channel_id=1, source_target_pairs={{0,8},{1,9},{2,10},{3,11},{4,12},{5,13},{6,14},{7,15},{8,0},{9,1},... | collective-permute-start | bytes 3080 | tf_op jit(solution)/shard_map/ppermute | solution.py:395
  152.5 0.6 copy-start.8
  152.5 0.9 copy-start.5
  156.0 77.1 %collective-permute-start.32 = (bf16[128,1152]{1,0:T(8,128)(2,1)}, bf16[128,1152]{1,0:T(8,128)(2,1)}, u32[]{:S(2)}, u32[]{:S(2)}) collective-permute-start(bf16[128,1152]{1,0:T(8,128)(2,1)} %get-tuple-element.114), channel_id=1, source_target_pairs={{0,8},{1,9},{2,10},{3,11},{4,12},{5,13},{6,14},{7,15},{8,0},{9,1},... | collective-permute-start | bytes 884744 | tf_op jit(solution)/shard_map/ppermute | solution.py:399
  162.2 70.9 %copy-start = (bf16[576,1024]{1,0:T(8,128)(2,1)S(1)}, bf16[576,1024]{1,0:T(8,128)(2,1)}, u32[]{:S(2)}) copy-start(bf16[576,1024]{1,0:T(8,128)(2,1)} %shard_map.137.refs_7_) | copy-start | bytes 3538948
  162.2 70.9 %copy-start.1 = (bf16[1152,256]{1,0:T(8,128)(2,1)S(1)}, bf16[1152,256]{1,0:T(8,128)(2,1)}, u32[]{:S(2)}) copy-start(bf16[1152,256]{1,0:T(8,128)(2,1)} %shard_map.138.refs_2_) | copy-start | bytes 1769476
  168.7 54.5 %collective-permute-start.16 = (bf16[576,1024]{1,0:T(8,128)(2,1)}, bf16[576,1024]{1,0:T(8,128)(2,1)}, u32[]{:S(2)}, u32[]{:S(2)}) collective-permute-start(bf16[576,1024]{1,0:T(8,128)(2,1)} %get-tuple-element.72), channel_id=1, source_target_pairs={{3,11},{11,3},{7,15},{15,7},{19,27},{27,19},{23,31},{31,23}} | collective-permute-start | bytes 3538952 | tf_op jit(solution)/shard_map/cond/branch_1_fun/ppermute | solution.py:420
  172.9 56.7 %collective-permute-start.17 = (bf16[576,1024]{1,0:T(8,128)(2,1)}, bf16[576,1024]{1,0:T(8,128)(2,1)}, u32[]{:S(2)}, u32[]{:S(2)}) collective-permute-start(bf16[576,1024]{1,0:T(8,128)(2,1)} %get-tuple-element.73), channel_id=1, source_target_pairs={{2,11},{10,3},{6,15},{14,7},{18,27},{26,19},{22,31},{30,23}} | collective-permute-start | bytes 3538952 | tf_op jit(solution)/shard_map/cond/branch_1_fun/ppermute | solution.py:421
  229.7 3.4 %collective-permute-start = (bf16[576,1024]{1,0:T(8,128)(2,1)}, bf16[576,1024]{1,0:T(8,128)(2,1)}, u32[]{:S(2)}, u32[]{:S(2)}) collective-permute-start(bf16[576,1024]{1,0:T(8,128)(2,1)} %get-tuple-element.56), channel_id=1, source_target_pairs={{0,8},{8,0},{1,9},{9,1},{16,24},{24,16},{17,25},{25,17}} | collective-permute-start | bytes 3538952 | tf_op jit(solution)/shard_map/cond/branch_0_fun/ppermute | solution.py:420
  231.4 1.7 collective-permute-start.1
  233.2 1.1 copy-start.3

commit v5 on v4

--- a/solution.py
+++ b/solution.py
@@ -229,7 +229,8 @@
         at += box[4]
     out_ref, sum_ref = refs[at : at + 2]
     bufs = refs[at + 2 : at + 2 + len(boxes)]
-    in_sem, out_sem = refs[at + 2 + len(boxes) :]
+    own_buf, other_buf, sum_buf, in_sem, out_sem = refs[at + 2 + len(boxes) :]
+    count = len(boxes)
     for n, arrays in enumerate(sources):
         for k, array in enumerate(arrays):
             last = k == len(arrays) - 1
@@ -239,7 +240,8 @@
             def _(n=n, array=array):
                 pltpu.make_async_copy(array, bufs[n], in_sem.at[n]).start()
 
-    sum_ref[...] = (own_ref[...] + other_ref[...].astype(f32)).astype(bf16)
+    pltpu.make_async_copy(own_ref, own_buf, in_sem.at[count]).start()
+    pltpu.make_async_copy(other_ref, other_buf, in_sem.at[count + 1]).start()
     puts = []
     for n, (row, col, high, wide, _) in enumerate(boxes):
         pltpu.make_async_copy(sources[n][0], bufs[n], in_sem.at[n]).wait()
@@ -248,6 +250,12 @@
         )
         put.start()
         puts.append(put)
+    pltpu.make_async_copy(own_ref, own_buf, in_sem.at[count]).wait()
+    pltpu.make_async_copy(other_ref, other_buf, in_sem.at[count + 1]).wait()
+    sum_buf[...] = (own_buf[...].astype(f32) + other_buf[...].astype(f32)).astype(bf16)
+    put = pltpu.make_async_copy(sum_buf, sum_ref, out_sem.at[count])
+    put.start()
+    puts.append(put)
     for put in puts:
         put.wait()
 
@@ -258,15 +266,15 @@
     return pl.pallas_call(
         functools.partial(place_kernel, boxes),
         in_specs=[pl.BlockSpec(memory_space=pltpu.SMEM)]
-        + [pl.BlockSpec(memory_space=pltpu.VMEM)] * 2
-        + [pl.BlockSpec(memory_space=pl.ANY) for _ in args],
-        out_specs=[pl.BlockSpec(memory_space=pl.ANY), pl.BlockSpec(memory_space=pltpu.VMEM)],
+        + [pl.BlockSpec(memory_space=pl.ANY)] * (2 + len(args)),
+        out_specs=[pl.BlockSpec(memory_space=pl.ANY)] * 2,
         out_shape=[
             jax.ShapeDtypeStruct((width, inner), bf16),
             jax.ShapeDtypeStruct(own_sum.shape, bf16),
         ],
         scratch_shapes=[pltpu.VMEM((box[2], box[3]), bf16) for box in boxes]
-        + [pltpu.SemaphoreType.DMA((len(boxes),)), pltpu.SemaphoreType.DMA((len(boxes),))],
+        + [pltpu.VMEM(own_sum.shape, bf16)] * 3
+        + [pltpu.SemaphoreType.DMA((len(boxes) + 2,)), pltpu.SemaphoreType.DMA((len(boxes) + 1,))],
         compiler_params=pltpu.CompilerParams(vmem_limit_bytes=8 * MIB),
         cost_estimate=pl.CostEstimate(
             flops=0, bytes_accessed=4 * width * inner, transcendentals=0
@@ -323,7 +331,7 @@
         functools.partial(combine_kernel, capacity, half),
         in_specs=[pl.BlockSpec(memory_space=pltpu.SMEM), vmem, vmem, vmem],
         out_shape=(
-            jax.ShapeDtypeStruct((tok_count, width), f32),
+            jax.ShapeDtypeStruct((tok_count, width), bf16),
             jax.ShapeDtypeStruct((tok_count, width), bf16),
         ),
         cost_estimate=pl.CostEstimate(

time: 240 us -> 239 us (level)
  no operation moved by 1% of the time
where the time goes in v5:
time: 239 us; the launch traced here: 238 us
  waiting for transfers between devices  112 us (47%)
  Pallas kernels  47.3 us (20%)
  blocking collectives  46.3 us (19%)
  starting transfers between devices  19.5 us (8%)
  local copies, waits for them, and re-layouts  5.47 us (2%)
  between operations  5.37 us (2%)
    ppermute x1, waiting for transfers between devices, shards(): mirror_to = lax.ppermute(where_to, 'expert', route)  51 us
    ppermute x2, waiting for transfers between devices, run(): lax.ppermute(near, 'expert', pairs)  48.9 us
    all_to_all x1, blocking collectives, shards(): lax.all_to_all(rows.reshape(expert_count, capacity, 2 * width), 'expert',...  46.3 us
    pallas_call x3, Pallas kernels, adam_block(): pl.pallas_call(adam_kernel, grid=(tiles,), in_specs=[pl.BlockSpec((rows,...  17.1 us
    pallas_call x1, Pallas kernels, rest_step(): pl.pallas_call(functools.partial(rest_kernel, len(rows)), grid=(tiles,),...  14.6 us
    pallas_call x1, Pallas kernels, first_step(): pl.pallas_call(functools.partial(first_kernel, len(rows)), grid=(1,), in_...  6.53 us
    ppermute x2, waiting for transfers between devices, run(): lax.ppermute(lent, 'expert', skew)  6.51 us
    ppermute x2, starting transfers between devices, run(): lax.ppermute(near, 'expert', pairs)  6.04 us
  transfers between devices with their start and end apart: 12, of which 5 were waited for; matrix products, arithmetic and copies ran while one was open for 1% of the time, Pallas kernels for 8%

profile of v5, /device:TPU:7, one launch (start us, length us, event | category | flops | bytes accessed | tf_op | source)
XLA Modules:
  0.0 238.1 jit_solution(18376494274006904761)
XLA Ops:
  0.6 3.1 %pack_rows.1 = (bf16[384,2304]{1,0:T(8,128)(2,1)}, s32[2,128]{1,0:T(2,128)}) custom-call(s32[2,128]{1,0:T(2,128)} %bitcast.37, f32[2,128]{1,0:T(2,128)} %bitcast.38, bf16[128,1152]{1,0:T(8,128)(2,1)} %x_ref.1, bf16[128,1152]{1,0:T(8,128)(2,1)} %g_ref.1), custom_call_target="tpu_custom_call" | custom-call | tf_op jit(solution)/shard_map/pack_rows/pallas_call | solution.py:88
  3.7 46.3 %all_to_all.10 = bf16[16,24,2304]{2,1,0:T(8,128)(2,1)S(1)} all-to-all(bf16[16,24,2304]{2,1,0:T(8,128)(2,1)} %bitcast.36), channel_id=1, replica_groups=mesh['dp'=2,'expert'=16] {'expert'}, dimensions={0} | all-to-all | bytes 3538944 | tf_op jit(solution)/shard_map/all_to_all | solution.py:368
  50.0 2.0 collective-permute-start.28
  52.0 3.3 %collective-permute-done.28.refs_1_ = bf16[384,2304]{1,0:T(8,128)(2,1)S(1)} collective-permute-done((bf16[384,2304]{1,0:T(8,128)(2,1)S(1)}, bf16[384,2304]{1,0:T(8,128)(2,1)S(1)}, u32[]{:S(2)}, u32[]{:S(2)}) %collective-permute-start.28) | collective-permute-done | bytes 1769504 | tf_op jit(solution)/shard_map/ppermute | solution.py:348
  55.3 1.3 copy-done.6
  56.6 6.5 %first_step.1 = (bf16[1152,256]{1,0:T(8,128)(2,1)}, bf16[768,256]{1,0:T(8,128)(2,1)}, bf16[1152,768]{1,0:T(8,128)(2,1)}) custom-call(bf16[384,2304]{1,0:T(8,128)(2,1)} %bitcast.27, bf16[384,2304]{1,0:T(8,128)(2,1)} %copy-done.6, bf16[1152,1536]{1,0:T(8,128)(2,1)} %bitcast.29, bf16[1536,1152]{1,0:T(8,128)(2,1)} %bitcast.32, f32[1152,1536]{1,0:T(8,128)} %bitcast.18, ...), custom_call_target="tpu_custom_call" | custom-call | flops 1358954496 | bytes 4128768 | tf_op jit(solution)/shard_map/first_step/pallas_call | solution.py:122
  63.1 14.6 %rest_step.1 = (bf16[768,1280]{1,0:T(8,128)(2,1)}, bf16[384,1152]{1,0:T(8,128)(2,1)}, bf16[384,1152]{1,0:T(8,128)(2,1)}) custom-call(bf16[384,2304]{1,0:T(8,128)(2,1)} %bitcast.28, bf16[384,2304]{1,0:T(8,128)(2,1)} %copy-done.6, bf16[768,256]{1,0:T(8,128)(2,1)} %get-tuple-element.107.refs_2_, bf16[1152,1536]{1,0:T(8,128)(2,1)} %bitcast.30, ...), custom_call_target="tpu_custom_call" | custom-call | flops 6794772480 | bytes 5898240 | tf_op jit(solution)/shard_map/rest_step/pallas_call | solution.py:171
  77.7 0.4 collective-permute-start.31
  78.1 2.3 collective-permute-done.31
  80.3 1.4 add_convert_fusion
  81.7 1.0 copy.14
  82.7 5.4 %all-to-all-start.1 = ((bf16[8,48,1152]{2,1,0:T(8,128)(2,1)}), bf16[8,48,1152]{2,1,0:T(8,128)(2,1)S(1)}, u32[]{:S(2)}, u32[]{:S(2)}) async-start(bf16[8,48,1152]{2,1,0:T(8,128)(2,1)} %bitcast.12), calls=%async_computation.1 | async-start | bytes 1769472 | tf_op jit(solution)/shard_map/all_to_all | solution.py:394
  88.1 6.4 %shard_map.137.refs_7_ = bf16[576,1024]{1,0:T(8,128)(2,1)} custom-call(bf16[1152,768]{1,0:T(8,128)(2,1)} %get-tuple-element.106.xt_ref, bf16[768,1280]{1,0:T(8,128)(2,1)} %get-tuple-element.108.pre_ref, f32[1152,1536]{1,0:T(8,128)} %bitcast.19, f32[1152,1536]{1,0:T(8,128)} %bitcast.23), custom_call_target="tpu_custom_call" | custom-call | flops 905969664 | bytes 5898240 | tf_op jit(solution)/shard_map/pallas_call | solution.py:205
  94.9 4.3 %shard_map.138.refs_2_ = bf16[1152,256]{1,0:T(8,128)(2,1)} custom-call(bf16[1152,768]{1,0:T(8,128)(2,1)} %get-tuple-element.106.xt_ref, bf16[768,1280]{1,0:T(8,128)(2,1)} %get-tuple-element.108.pre_ref, f32[1152,1536]{1,0:T(8,128)} %bitcast.20, f32[1152,1536]{1,0:T(8,128)} %bitcast.24), custom_call_target="tpu_custom_call" | custom-call | flops 452984832 | bytes 2949120 | tf_op jit(solution)/shard_map/pallas_call | solution.py:205
  99.3 2.3 collective-permute-start.33
  101.6 51.0 %collective-permute-done.30.mirror_ref = s32[2,128]{1,0:T(2,128)S(1)} collective-permute-done((s32[2,128]{1,0:T(2,128)S(1)}, s32[2,128]{1,0:T(2,128)S(1)}, u32[]{:S(2)}, u32[]{:S(2)}) %collective-permute-start.30) | collective-permute-done | bytes 1056 | tf_op jit(solution)/shard_map/ppermute | solution.py:403
  152.6 0.6 copy-done.8
  153.5 2.5 %combine_rows.1 = (bf16[128,1152]{1,0:T(8,128)(2,1)}, bf16[128,1152]{1,0:T(8,128)(2,1)}) custom-call(s32[1]{0:T(128)} %bitcast.9.upper_ref, s32[2,128]{1,0:T(2,128)} %get-tuple-element.109.where_ref, s32[2,128]{1,0:T(2,128)} %copy-done.8, bf16[384,1152]{1,0:T(8,128)(2,1)} %bitcast.34), custom_call_target="tpu_custom_call" | custom-call | flops 226492416 | bytes 1769472 | tf_op jit(solution)/shard_map/combine_rows/pallas_call | solution.py:330
  156.0 0.7 fusion.2
  159.4 0.6 dynamic_slice.8
  160.0 0.7 dynamic_slice.7
  162.7 6.5 %shard_map.136.refs_4_ = bf16[576,1024]{1,0:T(8,128)(2,1)} custom-call(bf16[1152,768]{1,0:T(8,128)(2,1)} %get-tuple-element.106.xt_ref, bf16[768,1280]{1,0:T(8,128)(2,1)} %get-tuple-element.108.pre_ref, f32[1152,1536]{1,0:T(8,128)} %bitcast.21, f32[1152,1536]{1,0:T(8,128)} %bitcast.25), custom_call_target="tpu_custom_call" | custom-call | flops 905969664 | bytes 5898240 | tf_op jit(solution)/shard_map/pallas_call | solution.py:205
  169.1 61.0 %conditional.3 = (bf16[576,1024]{1,0:T(8,128)(2,1)}, bf16[576,1024]{1,0:T(8,128)(2,1)}) conditional(s32[]{:T(128)} %bitcast.15, (bf16[576,1024]{1,0:T(8,128)(2,1)}, bf16[576,1024]{1,0:T(8,128)(2,1)}) %tuple.66, (bf16[576,1024]{1,0:T(8,128)(2,1)}, bf16[576,1024]{1,0:T(8,128)(2,1)}) %tuple.66, ...), branch_computations={%region_10.11_spmd, %region_11.12_spmd, %region_12.13_spmd, %regio... | conditional | bytes 9437280 | solution.py:441
  169.1 4.3 %collective-permute-start.16 = (bf16[576,1024]{1,0:T(8,128)(2,1)}, bf16[576,1024]{1,0:T(8,128)(2,1)}, u32[]{:S(2)}, u32[]{:S(2)}) collective-permute-start(bf16[576,1024]{1,0:T(8,128)(2,1)} %get-tuple-element.72), channel_id=1, source_target_pairs={{3,11},{11,3},{7,15},{15,7},{19,27},{27,19},{23,31},{31,23}} | collective-permute-start | bytes 3538952 | tf_op jit(solution)/shard_map/cond/branch_1_fun/ppermute | solution.py:428
  173.4 1.3 collective-permute-start.17
  174.7 48.9 %collective-permute-done.16 = bf16[576,1024]{1,0:T(8,128)(2,1)} collective-permute-done((bf16[576,1024]{1,0:T(8,128)(2,1)}, bf16[576,1024]{1,0:T(8,128)(2,1)}, u32[]{:S(2)}, u32[]{:S(2)}) %collective-permute-start.16) | collective-permute-done | bytes 1179680 | tf_op jit(solution)/shard_map/cond/branch_1_fun/ppermute | solution.py:428
  223.6 6.5 %collective-permute-done.17 = bf16[576,1024]{1,0:T(8,128)(2,1)} collective-permute-done((bf16[576,1024]{1,0:T(8,128)(2,1)}, bf16[576,1024]{1,0:T(8,128)(2,1)}, u32[]{:S(2)}, u32[]{:S(2)}) %collective-permute-start.17) | collective-permute-done | bytes 1179680 | tf_op jit(solution)/shard_map/cond/branch_1_fun/ppermute | solution.py:429
  230.1 3.5 %conditional.2 = (bf16[576,1024]{1,0:T(8,128)(2,1)}, bf16[576,1024]{1,0:T(8,128)(2,1)}) conditional(s32[]{:T(128)} %bitcast.14, (bf16[576,1024]{1,0:T(8,128)(2,1)}, bf16[576,1024]{1,0:T(8,128)(2,1)}) %tuple.66, (bf16[576,1024]{1,0:T(8,128)(2,1)}, bf16[576,1024]{1,0:T(8,128)(2,1)}) %tuple.66, ...), branch_computations={%region_3.4_spmd, %region_4.5_spmd, %region_5.6_spmd, %region_6.7_... | conditional | bytes 9437280 | solution.py:441
  230.1 1.8 collective-permute-start
  231.9 1.7 collective-permute-start.1
  233.6 1.0 copy-done.3
  234.6 3.5 %place.1 = (bf16[1152,1536]{1,0:T(8,128)(2,1)}, bf16[128,1152]{1,0:T(8,128)(2,1)}) custom-call(s32[1]{0:T(128)} %bitcast.source_ref, bf16[128,1152]{1,0:T(8,128)(2,1)S(1)} %copy-done.3, bf16[128,1152]{1,0:T(8,128)(2,1)} %collective-permute-done.32.other_ref, bf16[1152,256]{1,0:T(8,128)(2,1)S(1)} %copy-done.2, ...), custom_call_target="tpu_custom_call" | custom-call | bytes 7077888 | tf_op jit(solution)/shard_map/place/pallas_call | solution.py:266
  (34 shorter events, 0.9 us)
Async XLA Ops:
  50.0 5.3 %copy-start.4 = (bf16[16,24,2304]{2,1,0:T(8,128)(2,1)}, bf16[16,24,2304]{2,1,0:T(8,128)(2,1)S(1)}, u32[]{:S(2)}) copy-start(bf16[16,24,2304]{2,1,0:T(8,128)(2,1)S(1)} %all_to_all.10) | copy-start | bytes 5308420
  50.0 5.3 %collective-permute-start.28 = (bf16[384,2304]{1,0:T(8,128)(2,1)S(1)}, bf16[384,2304]{1,0:T(8,128)(2,1)S(1)}, u32[]{:S(2)}, u32[]{:S(2)}) collective-permute-start(bf16[384,2304]{1,0:T(8,128)(2,1)S(1)} %bitcast.26), channel_id=1, source_target_pairs={{0,16},{16,0},{1,17},{17,1},{2,18},{18,2},{3,19},{19,3},{4,20},{20... | collective-permute-start | bytes 5308424 | tf_op jit(solution)/shard_map/ppermute | solution.py:348
  55.3 1.3 copy-start.6
  77.7 2.7 %collective-permute-start.31 = (bf16[384,1152]{1,0:T(8,128)(2,1)}, bf16[384,1152]{1,0:T(8,128)(2,1)S(1)}, u32[]{:S(2)}, u32[]{:S(2)}) collective-permute-start(bf16[384,1152]{1,0:T(8,128)(2,1)} %get-tuple-element.111), channel_id=1, source_target_pairs={{0,16},{16,0},{1,17},{17,1},{2,18},{18,2},{3,19},{19,3},{4,20},{20... | collective-permute-start | bytes 2654216 | tf_op jit(solution)/shard_map/ppermute | solution.py:348
  82.7 69.9 %all-to-all-start.1 = ((bf16[8,48,1152]{2,1,0:T(8,128)(2,1)}), bf16[8,48,1152]{2,1,0:T(8,128)(2,1)S(1)}, u32[]{:S(2)}, u32[]{:S(2)}) async-start(bf16[8,48,1152]{2,1,0:T(8,128)(2,1)} %bitcast.12), calls=%async_computation.1 | async-start | bytes 1769472 | tf_op jit(solution)/shard_map/all_to_all | solution.py:394
  94.5 4.8 %copy-start.2 = (bf16[1152,256]{1,0:T(8,128)(2,1)S(1)}, bf16[1152,256]{1,0:T(8,128)(2,1)}, u32[]{:S(2)}) copy-start(bf16[1152,256]{1,0:T(8,128)(2,1)} %get-tuple-element.115.refs_0_) | copy-start | bytes 1769476
  94.5 7.1 %copy-start.7 = (s32[2,128]{1,0:T(2,128)S(1)}, s32[2,128]{1,0:T(2,128)}, u32[]{:S(2)}) copy-start(s32[2,128]{1,0:T(2,128)} %get-tuple-element.109.where_ref) | copy-start | bytes 3076
  94.5 61.5 %copy-start.9 = (s32[16]{0:T(128)S(1)}, s32[16]{0:T(128)}, u32[]{:S(2)}) copy-start(s32[16]{0:T(128)} %param.30) | copy-start | bytes 196
  94.5 61.5 %copy-start.10 = (pred[16]{0:T(512)(128)(4,1)S(1)}, pred[16]{0:T(512)(128)(4,1)}, u32[]{:S(2)}) copy-start(pred[16]{0:T(512)(128)(4,1)} %constant.38.clone) | copy-start | bytes 52
  94.5 64.9 %copy-start.12 = (s32[256]{0:T(256)S(1)}, s32[256]{0:T(256)}, u32[]{:S(2)}) copy-start(s32[256]{0:T(256)} %constant.37.clone) | copy-start | bytes 3076
  94.5 65.5 %copy-start.11 = (s32[256]{0:T(256)S(1)}, s32[256]{0:T(256)}, u32[]{:S(2)}) copy-start(s32[256]{0:T(256)} %constant.36.clone) | copy-start | bytes 3076
  94.5 74.6 %collective-permute-start.29 = (bf16[576,1024]{1,0:T(8,128)(2,1)}, bf16[576,1024]{1,0:T(8,128)(2,1)}, u32[]{:S(2)}, u32[]{:S(2)}) collective-permute-start(bf16[576,1024]{1,0:T(8,128)(2,1)} %shard_map.137.refs_7_), channel_id=1, source_target_pairs={{0,1},{1,0},{2,3},{3,2},{4,5},{5,4},{6,7},{7,6},{8,9},{9,8},{10,11... | collective-permute-start | bytes 3538952 | tf_op jit(solution)/shard_map/ppermute | solution.py:419
  99.2 134.4 %collective-permute-start.34 = (bf16[1152,256]{1,0:T(8,128)(2,1)}, bf16[1152,256]{1,0:T(8,128)(2,1)S(1)}, u32[]{:S(2)}, u32[]{:S(2)}) collective-permute-start(bf16[1152,256]{1,0:T(8,128)(2,1)} %shard_map.138.refs_2_), channel_id=1, source_target_pairs={{0,8},{1,9},{2,10},{3,11},{4,12},{5,13},{6,14},{7,15},{8,0},{9,1},... | collective-permute-start | bytes 1769480 | tf_op jit(solution)/shard_map/ppermute | solution.py:412
  99.3 134.3 %collective-permute-start.33 = (bf16[1152,256]{1,0:T(8,128)(2,1)S(1)}, bf16[1152,256]{1,0:T(8,128)(2,1)S(1)}, u32[]{:S(2)}, u32[]{:S(2)}) collective-permute-start(bf16[1152,256]{1,0:T(8,128)(2,1)S(1)} %copy-done.2), channel_id=1, source_target_pairs={{0,8},{1,9},{2,10},{3,11},{4,12},{5,13},{6,14},{7,15},{8,0},{9,1},... | collective-permute-start | bytes 1769480 | tf_op jit(solution)/shard_map/ppermute | solution.py:386
  101.6 51.0 %collective-permute-start.30 = (s32[2,128]{1,0:T(2,128)S(1)}, s32[2,128]{1,0:T(2,128)S(1)}, u32[]{:S(2)}, u32[]{:S(2)}) collective-permute-start(s32[2,128]{1,0:T(2,128)S(1)} %copy-done.7), channel_id=1, source_target_pairs={{0,8},{1,9},{2,10},{3,11},{4,12},{5,13},{6,14},{7,15},{8,0},{9,1},... | collective-permute-start | bytes 3080 | tf_op jit(solution)/shard_map/ppermute | solution.py:403
  152.6 0.6 copy-start.8
  152.6 0.9 copy-start.5
  156.0 77.6 %collective-permute-start.32 = (bf16[128,1152]{1,0:T(8,128)(2,1)}, bf16[128,1152]{1,0:T(8,128)(2,1)}, u32[]{:S(2)}, u32[]{:S(2)}) collective-permute-start(bf16[128,1152]{1,0:T(8,128)(2,1)} %get-tuple-element.114), channel_id=1, source_target_pairs={{0,8},{1,9},{2,10},{3,11},{4,12},{5,13},{6,14},{7,15},{8,0},{9,1},... | collective-permute-start | bytes 884744 | tf_op jit(solution)/shard_map/ppermute | solution.py:407
  162.7 71.0 %copy-start = (bf16[576,1024]{1,0:T(8,128)(2,1)S(1)}, bf16[576,1024]{1,0:T(8,128)(2,1)}, u32[]{:S(2)}) copy-start(bf16[576,1024]{1,0:T(8,128)(2,1)} %shard_map.137.refs_7_) | copy-start | bytes 3538948
  162.7 71.0 %copy-start.1 = (bf16[1152,256]{1,0:T(8,128)(2,1)S(1)}, bf16[1152,256]{1,0:T(8,128)(2,1)}, u32[]{:S(2)}) copy-start(bf16[1152,256]{1,0:T(8,128)(2,1)} %shard_map.138.refs_2_) | copy-start | bytes 1769476
  169.1 54.5 %collective-permute-start.16 = (bf16[576,1024]{1,0:T(8,128)(2,1)}, bf16[576,1024]{1,0:T(8,128)(2,1)}, u32[]{:S(2)}, u32[]{:S(2)}) collective-permute-start(bf16[576,1024]{1,0:T(8,128)(2,1)} %get-tuple-element.72), channel_id=1, source_target_pairs={{3,11},{11,3},{7,15},{15,7},{19,27},{27,19},{23,31},{31,23}} | collective-permute-start | bytes 3538952 | tf_op jit(solution)/shard_map/cond/branch_1_fun/ppermute | solution.py:428
  173.4 56.7 %collective-permute-start.17 = (bf16[576,1024]{1,0:T(8,128)(2,1)}, bf16[576,1024]{1,0:T(8,128)(2,1)}, u32[]{:S(2)}, u32[]{:S(2)}) collective-permute-start(bf16[576,1024]{1,0:T(8,128)(2,1)} %get-tuple-element.73), channel_id=1, source_target_pairs={{2,11},{10,3},{6,15},{14,7},{18,27},{26,19},{22,31},{30,23}} | collective-permute-start | bytes 3538952 | tf_op jit(solution)/shard_map/cond/branch_1_fun/ppermute | solution.py:429
  230.1 3.5 %collective-permute-start = (bf16[576,1024]{1,0:T(8,128)(2,1)}, bf16[576,1024]{1,0:T(8,128)(2,1)}, u32[]{:S(2)}, u32[]{:S(2)}) collective-permute-start(bf16[576,1024]{1,0:T(8,128)(2,1)} %get-tuple-element.56), channel_id=1, source_target_pairs={{0,8},{8,0},{1,9},{9,1},{16,24},{24,16},{17,25},{25,17}} | collective-permute-start | bytes 3538952 | tf_op jit(solution)/shard_map/cond/branch_0_fun/ppermute | solution.py:428
  231.9 1.7 collective-permute-start.1
  233.6 1.0 copy-start.3

commit v6 on v2

--- a/solution.py
+++ b/solution.py
@@ -225,25 +225,30 @@
 def place_kernel(boxes, source_ref, *refs):
     sources, at = [], 0
     for box in boxes:
-        sources.append(refs[at : at + box[4]])
-        at += box[4]
+        sources.append(refs[at : at + box[5]])
+        at += box[5]
     out_ref = refs[at]
     bufs = refs[at + 1 : at + 1 + len(boxes)]
     in_sem, out_sem = refs[at + 1 + len(boxes) :]
     for n, arrays in enumerate(sources):
+        start, high = boxes[n][2], boxes[n][3]
         for k, array in enumerate(arrays):
             last = k == len(arrays) - 1
             wanted = source_ref[0] >= k if last else source_ref[0] == k
 
             @pl.when(wanted)
-            def _(n=n, array=array):
-                pltpu.make_async_copy(array, bufs[n], in_sem.at[n]).start()
+            def _(n=n, array=array, start=start, high=high):
+                pltpu.make_async_copy(
+                    array.at[pl.ds(start, high)], bufs[n], in_sem.at[n]
+                ).start()
 
     puts = []
-    for n, (row, col, high, wide, _) in enumerate(boxes):
-        pltpu.make_async_copy(sources[n][0], bufs[n], in_sem.at[n]).wait()
+    for n, (row, col, start, high, wide, _) in enumerate(boxes):
+        pltpu.make_async_copy(
+            sources[n][0].at[pl.ds(start, high)], bufs[n], in_sem.at[n]
+        ).wait()
         put = pltpu.make_async_copy(
-            bufs[n], out_ref.at[pl.ds(row, high), pl.ds(col, wide)], out_sem.at[n]
+            bufs[n], out_ref.at[pl.ds(row + start, high), pl.ds(col, wide)], out_sem.at[n]
         )
         put.start()
         puts.append(put)
@@ -252,15 +257,15 @@
 
 
 def place(source, pieces, width, inner):
-    boxes = [piece[:4] + (len(piece[4]),) for piece in pieces]
-    args = [array for piece in pieces for array in piece[4]]
+    boxes = [piece[:5] + (len(piece[5]),) for piece in pieces]
+    args = [array for piece in pieces for array in piece[5]]
     return pl.pallas_call(
         functools.partial(place_kernel, boxes),
         in_specs=[pl.BlockSpec(memory_space=pltpu.SMEM)]
         + [pl.BlockSpec(memory_space=pl.ANY) for _ in args],
         out_specs=pl.BlockSpec(memory_space=pl.ANY),
         out_shape=jax.ShapeDtypeStruct((width, inner), bf16),
-        scratch_shapes=[pltpu.VMEM((box[2], box[3]), bf16) for box in boxes]
+        scratch_shapes=[pltpu.VMEM((box[3], box[4]), bf16) for box in boxes]
         + [pltpu.SemaphoreType.DMA((len(boxes),)), pltpu.SemaphoreType.DMA((len(boxes),))],
         compiler_params=pltpu.CompilerParams(vmem_limit_bytes=8 * MIB),
         cost_estimate=pl.CostEstimate(
@@ -342,6 +347,8 @@
         tiled=True,
     ).reshape(slots, 2 * width)
     all_rows = [own] + [dp_shift(own, d) for d in range(1, dp_count)]
+    if dp_count == 2:
+        all_rows = [pltpu.with_memory_space_constraint(r, pltpu.VMEM) for r in all_rows]
 
     inner = w_in.shape[2]
     tile = 256 if inner % 256 == 0 else 128
@@ -409,7 +416,12 @@
         pieces.append((width // 2, at * tile, width // 2, wide, far_all))
 
     source = (is_moved * (1 + group)).reshape(1)
-    adam_out = place(source, pieces, width, inner)
+    cut = []
+    for row, col, high, wide, arrays in pieces:
+        step = width // 4
+        for at in range(0, high, step):
+            cut.append((row, col, at, min(step, high - at), wide, arrays))
+    adam_out = place(source, cut, width, inner)
     return (x_grad, adam_out[None])
 
 

time: 220 us -> 218 us (level)
  no operation moved by 1% of the time
where the time goes in v6:
time: 218 us; the launch traced here: 217 us
  waiting for transfers between devices  95.3 us (44%)
  blocking collectives  47.6 us (22%)
  Pallas kernels  46.2 us (21%)
  starting transfers between devices  18.5 us (8%)
  between operations  5.26 us (2%)
  other arithmetic  3.05 us (1%)
    ppermute x2, waiting for transfers between devices, run(): lax.ppermute(near, 'expert', pairs)  70 us
    all_to_all x1, blocking collectives, shards(): lax.all_to_all(rows.reshape(expert_count, capacity, 2 * width), 'expert',...  47.6 us
    all_to_all x1, waiting for transfers between devices, shards(): lax.all_to_all(total.astype(bf16).reshape(expert_count, capacity, width),...  19.1 us
    pallas_call x3, Pallas kernels, adam_block(): pl.pallas_call(adam_kernel, grid=(tiles,), in_specs=[pl.BlockSpec((rows,...  17 us
    pallas_call x1, Pallas kernels, rest_step(): pl.pallas_call(functools.partial(rest_kernel, len(rows)), grid=(tiles,),...  13.5 us
    all_to_all x1, starting transfers between devices, shards(): lax.all_to_all(total.astype(bf16).reshape(expert_count, capacity, width),...  6.28 us
    ppermute x2, waiting for transfers between devices, dp_shift(): return lax.ppermute(block, 'dp', [(i, i ^ apart) for i in range(count)])  6.19 us
    pallas_call x1, Pallas kernels, first_step(): pl.pallas_call(functools.partial(first_kernel, len(rows)), grid=(1,), in_...  5.52 us
  transfers between devices with their start and end apart: 10, of which 4 were waited for; matrix products, arithmetic and copies ran while one was open for 1% of the time, Pallas kernels for 9%

profile of v6, /device:TPU:6, one launch (start us, length us, event | category | flops | bytes accessed | tf_op | source)
XLA Modules:
  0.0 217.2 jit_solution(14523886757205052099)
XLA Ops:
  0.6 3.1 %pack_rows.1 = (bf16[384,2304]{1,0:T(8,128)(2,1)}, s32[2,128]{1,0:T(2,128)}) custom-call(s32[2,128]{1,0:T(2,128)} %bitcast.32, f32[2,128]{1,0:T(2,128)} %bitcast.33, bf16[128,1152]{1,0:T(8,128)(2,1)} %x_ref.1, bf16[128,1152]{1,0:T(8,128)(2,1)} %g_ref.1), custom_call_target="tpu_custom_call" | custom-call | tf_op jit(solution)/shard_map/pack_rows/pallas_call | solution.py:88
  3.7 47.6 %all_to_all.10 = bf16[16,24,2304]{2,1,0:T(8,128)(2,1)S(1)} all-to-all(bf16[16,24,2304]{2,1,0:T(8,128)(2,1)} %bitcast.31), channel_id=1, replica_groups=mesh['dp'=2,'expert'=16] {'expert'}, dimensions={0} | all-to-all | bytes 3538944 | tf_op jit(solution)/shard_map/all_to_all | solution.py:342
  51.3 0.0 collective-permute-start.28
  51.3 3.7 %collective-permute-done.28.refs_1_ = bf16[384,2304]{1,0:T(8,128)(2,1)S(1)} collective-permute-done((bf16[384,2304]{1,0:T(8,128)(2,1)S(1)}, bf16[384,2304]{1,0:T(8,128)(2,1)S(1)}, u32[]{:S(2)}, u32[]{:S(2)}) %collective-permute-start.28) | collective-permute-done | bytes 1769504 | tf_op jit(solution)/shard_map/ppermute | solution.py:322
  55.0 5.5 %first_step.1 = (bf16[1152,256]{1,0:T(8,128)(2,1)}, bf16[768,256]{1,0:T(8,128)(2,1)}, bf16[1152,768]{1,0:T(8,128)(2,1)}) custom-call(bf16[384,2304]{1,0:T(8,128)(2,1)S(1)} %bitcast.15, bf16[384,2304]{1,0:T(8,128)(2,1)S(1)} %collective-permute-done.28.refs_1_, bf16[1152,1536]{1,0:T(8,128)(2,1)} %bitcast.25, bf16[1536,1152]{1,0:T(8,128)(2,1)} %bitcast.28, ...), custom_call_target="tpu_custom_call" | custom-call | flops 1358954496 | bytes 4128768 | tf_op jit(solution)/shard_map/first_step/pallas_call | solution.py:122
  60.5 13.5 %rest_step.1 = (bf16[768,1280]{1,0:T(8,128)(2,1)}, bf16[384,1152]{1,0:T(8,128)(2,1)}, bf16[384,1152]{1,0:T(8,128)(2,1)}) custom-call(bf16[384,2304]{1,0:T(8,128)(2,1)S(1)} %bitcast.16, bf16[384,2304]{1,0:T(8,128)(2,1)S(1)} %collective-permute-done.28.refs_1_, bf16[768,256]{1,0:T(8,128)(2,1)} %get-tuple-element.103.refs_2_, bf16[1152,1536]{1,0:T(8,128)(2,1)} %bitcast.26, ...), custom_call_target="tpu_custom_call" | custom-call | flops 6794772480 | bytes 5898240 | tf_op jit(solution)/shard_map/rest_step/pallas_call | solution.py:171
  74.0 0.1 collective-permute-start.30
  74.1 2.5 %collective-permute-done.30 = bf16[384,1152]{1,0:T(8,128)(2,1)S(1)} collective-permute-done((bf16[384,1152]{1,0:T(8,128)(2,1)}, bf16[384,1152]{1,0:T(8,128)(2,1)S(1)}, u32[]{:S(2)}, u32[]{:S(2)}) %collective-permute-start.30) | collective-permute-done | bytes 884768 | tf_op jit(solution)/shard_map/ppermute | solution.py:322
  76.6 2.4 %add_convert_fusion = bf16[384,1152]{1,0:T(8,128)(2,1)} fusion(bf16[384,1152]{1,0:T(8,128)(2,1)S(1)} %collective-permute-done.30, bf16[384,1152]{1,0:T(8,128)(2,1)} %get-tuple-element.106), kind=kLoop, calls=%fused_computation | loop fusion | flops 1769472 | bytes 2654208 | tf_op jit(solution)/shard_map/convert_element_type | solution.py:370
  79.0 6.3 %all-to-all-start.1 = ((bf16[16,24,1152]{2,1,0:T(8,128)(2,1)}), bf16[16,24,1152]{2,1,0:T(8,128)(2,1)}, u32[]{:S(2)}, u32[]{:S(2)}) async-start(bf16[16,24,1152]{2,1,0:T(8,128)(2,1)} %bitcast.8), calls=%async_computation.1 | async-start | bytes 1769472 | tf_op jit(solution)/shard_map/all_to_all | solution.py:369
  85.3 6.3 %shard_map.137.refs_22_.refs_25_ = bf16[576,1024]{1,0:T(8,128)(2,1)} custom-call(bf16[1152,768]{1,0:T(8,128)(2,1)} %get-tuple-element.102.xt_ref, bf16[768,1280]{1,0:T(8,128)(2,1)} %get-tuple-element.104.pre_ref, f32[1152,1536]{1,0:T(8,128)} %bitcast.18, f32[1152,1536]{1,0:T(8,128)} %bitcast.22), custom_call_target="tpu_custom_call" | custom-call | flops 905969664 | bytes 5898240 | tf_op jit(solution)/shard_map/pallas_call | solution.py:205
  91.6 0.0 copy-start.6
  91.6 0.0 copy-start.5
  91.6 0.6 collective-permute-start.29
  92.3 4.3 %shard_map.138.refs_8_.refs_10_.refs_12_.refs_14_ = bf16[1152,256]{1,0:T(8,128)(2,1)} custom-call(bf16[1152,768]{1,0:T(8,128)(2,1)} %get-tuple-element.102.xt_ref, bf16[768,1280]{1,0:T(8,128)(2,1)} %get-tuple-element.104.pre_ref, f32[1152,1536]{1,0:T(8,128)} %bitcast.19, f32[1152,1536]{1,0:T(8,128)} %bitcast.23), custom_call_target="tpu_custom_call" | custom-call | flops 452984832 | bytes 2949120 | tf_op jit(solution)/shard_map/pallas_call | solution.py:205
  96.6 2.4 %collective-permute-start.32 = (bf16[1152,256]{1,0:T(8,128)(2,1)}, bf16[1152,256]{1,0:T(8,128)(2,1)S(1)}, u32[]{:S(2)}, u32[]{:S(2)}) collective-permute-start(bf16[1152,256]{1,0:T(8,128)(2,1)} %shard_map.138.refs_8_.refs_10_.refs_12_.refs_14_), channel_id=1, source_target_pairs={{0,8},{1,9},{2,10},{3,11},{4,12},{5,13},{6,14},{7,15},{8,0},{9,1},... | collective-permute-start | bytes 1769480 | tf_op jit(solution)/shard_map/ppermute | solution.py:382
  99.0 0.5 collective-permute-start.31
  99.5 0.7 fusion.2
  102.8 0.7 dynamic_slice.7
  103.5 0.6 dynamic_slice.6
  106.0 6.4 %shard_map.136.refs_16_.refs_19_ = bf16[576,1024]{1,0:T(8,128)(2,1)} custom-call(bf16[1152,768]{1,0:T(8,128)(2,1)} %get-tuple-element.102.xt_ref, bf16[768,1280]{1,0:T(8,128)(2,1)} %get-tuple-element.104.pre_ref, f32[1152,1536]{1,0:T(8,128)} %bitcast.20, f32[1152,1536]{1,0:T(8,128)} %bitcast.24), custom_call_target="tpu_custom_call" | custom-call | flops 905969664 | bytes 5898240 | tf_op jit(solution)/shard_map/pallas_call | solution.py:205
  112.4 19.1 %all-to-all-done.1 = bf16[16,24,1152]{2,1,0:T(8,128)(2,1)} async-done(((bf16[16,24,1152]{2,1,0:T(8,128)(2,1)}), bf16[16,24,1152]{2,1,0:T(8,128)(2,1)}, u32[]{:S(2)}, u32[]{:S(2)}) %all-to-all-start.1) | async-done | bytes 884768 | tf_op jit(solution)/shard_map/all_to_all | solution.py:369
  131.5 2.3 %combine_rows.1 = bf16[128,1152]{1,0:T(8,128)(2,1)} custom-call(s32[2,128]{1,0:T(2,128)} %get-tuple-element.105.where_ref, bf16[384,1152]{1,0:T(8,128)(2,1)} %bitcast.9.back_ref), custom_call_target="tpu_custom_call" | custom-call | tf_op jit(solution)/shard_map/combine_rows/pallas_call | solution.py:313
  133.8 75.1 %conditional.3 = (bf16[576,1024]{1,0:T(8,128)(2,1)}, bf16[576,1024]{1,0:T(8,128)(2,1)}) conditional(s32[]{:T(128)} %bitcast.12, (bf16[576,1024]{1,0:T(8,128)(2,1)}, bf16[576,1024]{1,0:T(8,128)(2,1)}) %tuple.66, (bf16[576,1024]{1,0:T(8,128)(2,1)}, bf16[576,1024]{1,0:T(8,128)(2,1)}) %tuple.66, ...), branch_computations={%region_10.11_spmd, %region_11.12_spmd, %region_12.13_spmd, %regio... | conditional | bytes 9437280 | solution.py:408
  133.8 3.8 %collective-permute-start.16 = (bf16[576,1024]{1,0:T(8,128)(2,1)}, bf16[576,1024]{1,0:T(8,128)(2,1)}, u32[]{:S(2)}, u32[]{:S(2)}) collective-permute-start(bf16[576,1024]{1,0:T(8,128)(2,1)} %get-tuple-element.72), channel_id=1, source_target_pairs={{3,11},{11,3},{7,15},{15,7},{19,27},{27,19},{23,31},{31,23}} | collective-permute-start | bytes 3538952 | tf_op jit(solution)/shard_map/cond/branch_1_fun/ppermute | solution.py:398
  137.5 1.3 collective-permute-start.17
  138.8 70.0 %collective-permute-done.16 = bf16[576,1024]{1,0:T(8,128)(2,1)} collective-permute-done((bf16[576,1024]{1,0:T(8,128)(2,1)}, bf16[576,1024]{1,0:T(8,128)(2,1)}, u32[]{:S(2)}, u32[]{:S(2)}) %collective-permute-start.16) | collective-permute-done | bytes 1179680 | tf_op jit(solution)/shard_map/cond/branch_1_fun/ppermute | solution.py:398
  208.9 0.0 collective-permute-done.17
  208.9 3.5 %conditional.2 = (bf16[576,1024]{1,0:T(8,128)(2,1)}, bf16[576,1024]{1,0:T(8,128)(2,1)}) conditional(s32[]{:T(128)} %bitcast.11, (bf16[576,1024]{1,0:T(8,128)(2,1)}, bf16[576,1024]{1,0:T(8,128)(2,1)}) %tuple.66, (bf16[576,1024]{1,0:T(8,128)(2,1)}, bf16[576,1024]{1,0:T(8,128)(2,1)}) %tuple.66, ...), branch_computations={%region_3.4_spmd, %region_4.5_spmd, %region_5.6_spmd, %region_6.7_... | conditional | bytes 9437280 | solution.py:408
  208.9 1.7 collective-permute-start
  210.6 1.8 collective-permute-start.1
  212.4 4.8 %place.1 = bf16[1152,1536]{1,0:T(8,128)(2,1)} custom-call(s32[1]{0:T(128)} %bitcast.10.source_ref, bf16[1152,256]{1,0:T(8,128)(2,1)S(1)} %copy-done.2, bf16[1152,256]{1,0:T(8,128)(2,1)S(1)} %collective-permute-done.31.refs_1_.refs_3_.refs_5_.refs_7_, bf16[1152,256]{1,0:T(8,128)(2,1)S(1)} %copy-done.2, ...), custom_call_target="tpu_custom_call" | custom-call | bytes 7077888 | tf_op jit(solution)/shard_map/place/pallas_call | solution.py:262
  (17 shorter events, 0.0 us)
Async XLA Ops:
  51.3 3.7 %collective-permute-start.28 = (bf16[384,2304]{1,0:T(8,128)(2,1)S(1)}, bf16[384,2304]{1,0:T(8,128)(2,1)S(1)}, u32[]{:S(2)}, u32[]{:S(2)}) collective-permute-start(bf16[384,2304]{1,0:T(8,128)(2,1)S(1)} %bitcast.14), channel_id=1, source_target_pairs={{0,16},{16,0},{1,17},{17,1},{2,18},{18,2},{3,19},{19,3},{4,20},{20... | collective-permute-start | bytes 5308424 | tf_op jit(solution)/shard_map/ppermute | solution.py:322
  74.0 2.6 %collective-permute-start.30 = (bf16[384,1152]{1,0:T(8,128)(2,1)}, bf16[384,1152]{1,0:T(8,128)(2,1)S(1)}, u32[]{:S(2)}, u32[]{:S(2)}) collective-permute-start(bf16[384,1152]{1,0:T(8,128)(2,1)} %get-tuple-element.107), channel_id=1, source_target_pairs={{0,16},{16,0},{1,17},{17,1},{2,18},{18,2},{3,19},{19,3},{4,20},{20... | collective-permute-start | bytes 2654216 | tf_op jit(solution)/shard_map/ppermute | solution.py:322
  79.0 52.5 %all-to-all-start.1 = ((bf16[16,24,1152]{2,1,0:T(8,128)(2,1)}), bf16[16,24,1152]{2,1,0:T(8,128)(2,1)}, u32[]{:S(2)}, u32[]{:S(2)}) async-start(bf16[16,24,1152]{2,1,0:T(8,128)(2,1)} %bitcast.8), calls=%async_computation.1 | async-start | bytes 1769472 | tf_op jit(solution)/shard_map/all_to_all | solution.py:369
  91.6 7.4 %copy-start.2 = (bf16[1152,256]{1,0:T(8,128)(2,1)S(1)}, bf16[1152,256]{1,0:T(8,128)(2,1)}, u32[]{:S(2)}) copy-start(bf16[1152,256]{1,0:T(8,128)(2,1)} %get-tuple-element.109.refs_0_.refs_2_.refs_4_.refs_6_) | copy-start | bytes 1769476
  91.6 7.9 %copy-start.3 = (s32[16]{0:T(128)S(1)}, s32[16]{0:T(128)}, u32[]{:S(2)}) copy-start(s32[16]{0:T(128)} %param.30) | copy-start | bytes 196
  91.6 7.9 %copy-start.4 = (pred[16]{0:T(512)(128)(4,1)S(1)}, pred[16]{0:T(512)(128)(4,1)}, u32[]{:S(2)}) copy-start(pred[16]{0:T(512)(128)(4,1)} %constant.32.clone) | copy-start | bytes 52
  91.6 11.2 %copy-start.6 = (s32[256]{0:T(256)S(1)}, s32[256]{0:T(256)}, u32[]{:S(2)}) copy-start(s32[256]{0:T(256)} %constant.31.clone) | copy-start | bytes 3076
  91.6 11.8 %copy-start.5 = (s32[256]{0:T(256)S(1)}, s32[256]{0:T(256)}, u32[]{:S(2)}) copy-start(s32[256]{0:T(256)} %constant.30.clone) | copy-start | bytes 3076
  91.6 42.1 %collective-permute-start.29 = (bf16[576,1024]{1,0:T(8,128)(2,1)}, bf16[576,1024]{1,0:T(8,128)(2,1)}, u32[]{:S(2)}, u32[]{:S(2)}) collective-permute-start(bf16[576,1024]{1,0:T(8,128)(2,1)} %shard_map.137.refs_22_.refs_25_), channel_id=1, source_target_pairs={{0,1},{1,0},{2,3},{3,2},{4,5},{5,4},{6,7},{7,6},{8,9},{9,8},{10,11... | collective-permute-start | bytes 3538952 | tf_op jit(solution)/shard_map/ppermute | solution.py:389
  96.6 115.7 %collective-permute-start.32 = (bf16[1152,256]{1,0:T(8,128)(2,1)}, bf16[1152,256]{1,0:T(8,128)(2,1)S(1)}, u32[]{:S(2)}, u32[]{:S(2)}) collective-permute-start(bf16[1152,256]{1,0:T(8,128)(2,1)} %shard_map.138.refs_8_.refs_10_.refs_12_.refs_14_), channel_id=1, source_target_pairs={{0,8},{1,9},{2,10},{3,11},{4,12},{5,13},{6,14},{7,15},{8,0},{9,1},... | collective-permute-start | bytes 1769480 | tf_op jit(solution)/shard_map/ppermute | solution.py:382
  99.0 113.3 %collective-permute-start.31 = (bf16[1152,256]{1,0:T(8,128)(2,1)S(1)}, bf16[1152,256]{1,0:T(8,128)(2,1)S(1)}, u32[]{:S(2)}, u32[]{:S(2)}) collective-permute-start(bf16[1152,256]{1,0:T(8,128)(2,1)S(1)} %copy-done.2), channel_id=1, source_target_pairs={{0,8},{1,9},{2,10},{3,11},{4,12},{5,13},{6,14},{7,15},{8,0},{9,1},... | collective-permute-start | bytes 1769480 | tf_op jit(solution)/shard_map/ppermute | solution.py:362
  106.0 106.3 %copy-start.1 = (bf16[576,1024]{1,0:T(8,128)(2,1)S(1)}, bf16[576,1024]{1,0:T(8,128)(2,1)}, u32[]{:S(2)}) copy-start(bf16[576,1024]{1,0:T(8,128)(2,1)} %shard_map.137.refs_22_.refs_25_) | copy-start | bytes 3538948
  112.4 99.9 %copy-start = (bf16[1152,256]{1,0:T(8,128)(2,1)S(1)}, bf16[1152,256]{1,0:T(8,128)(2,1)}, u32[]{:S(2)}) copy-start(bf16[1152,256]{1,0:T(8,128)(2,1)} %shard_map.138.refs_8_.refs_10_.refs_12_.refs_14_) | copy-start | bytes 1769476
  133.8 75.1 %collective-permute-start.16 = (bf16[576,1024]{1,0:T(8,128)(2,1)}, bf16[576,1024]{1,0:T(8,128)(2,1)}, u32[]{:S(2)}, u32[]{:S(2)}) collective-permute-start(bf16[576,1024]{1,0:T(8,128)(2,1)} %get-tuple-element.72), channel_id=1, source_target_pairs={{3,11},{11,3},{7,15},{15,7},{19,27},{27,19},{23,31},{31,23}} | collective-permute-start | bytes 3538952 | tf_op jit(solution)/shard_map/cond/branch_1_fun/ppermute | solution.py:398
  137.5 71.3 %collective-permute-start.17 = (bf16[576,1024]{1,0:T(8,128)(2,1)}, bf16[576,1024]{1,0:T(8,128)(2,1)}, u32[]{:S(2)}, u32[]{:S(2)}) collective-permute-start(bf16[576,1024]{1,0:T(8,128)(2,1)} %get-tuple-element.73), channel_id=1, source_target_pairs={{2,11},{10,3},{6,15},{14,7},{18,27},{26,19},{22,31},{30,23}} | collective-permute-start | bytes 3538952 | tf_op jit(solution)/shard_map/cond/branch_1_fun/ppermute | solution.py:399
  208.9 3.5 %collective-permute-start = (bf16[576,1024]{1,0:T(8,128)(2,1)}, bf16[576,1024]{1,0:T(8,128)(2,1)}, u32[]{:S(2)}, u32[]{:S(2)}) collective-permute-start(bf16[576,1024]{1,0:T(8,128)(2,1)} %get-tuple-element.56), channel_id=1, source_target_pairs={{0,8},{8,0},{1,9},{9,1},{16,24},{24,16},{17,25},{25,17}} | collective-permute-start | bytes 3538952 | tf_op jit(solution)/shard_map/cond/branch_0_fun/ppermute | solution.py:398
  210.6 1.8 collective-permute-start.1

commit v7 on v6

--- a/solution.py
+++ b/solution.py
@@ -33,21 +33,20 @@
 
 
 def gelu_slope(pre_act):
-    inner_arg = coef_c * (pre_act + coef_a * pre_act * pre_act * pre_act)
-    tanh_val = jnp.tanh(inner_arg)
-    return 0.5 * (1.0 + tanh_val) + 0.5 * pre_act * (1.0 - tanh_val * tanh_val) * coef_c * (
-        1.0 + 3.0 * coef_a * pre_act * pre_act
-    )
+    square = pre_act * pre_act
+    tanh_val = jnp.tanh(pre_act * (coef_c + coef_c * coef_a * square))
+    bend = pre_act * (coef_c + 3.0 * coef_c * coef_a * square)
+    return 0.5 + 0.5 * (tanh_val + bend * (1.0 - tanh_val * tanh_val))
 
 
 def adam_step(weight_grad, first_moment, second_moment):
-    first_new = beta_one * first_moment + (1.0 - beta_one) * weight_grad
-    second_new = beta_two * second_moment + (1.0 - beta_two) * weight_grad * weight_grad
-    return (
-        first_new
-        / (1.0 - beta_one**ADAM_STEP)
-        / (jnp.sqrt(second_new / (1.0 - beta_two**ADAM_STEP)) + adam_eps)
-    ).astype(bf16)
+    unbias_one = 1.0 / (1.0 - beta_one**ADAM_STEP)
+    unbias_two = 1.0 / (1.0 - beta_two**ADAM_STEP)
+    first_hat = (beta_one * unbias_one) * first_moment + ((1.0 - beta_one) * unbias_one) * weight_grad
+    second_hat = (beta_two * unbias_two) * second_moment + (
+        (1.0 - beta_two) * unbias_two
+    ) * (weight_grad * weight_grad)
+    return (first_hat / (jnp.sqrt(second_hat) + adam_eps)).astype(bf16)
 
 
 def pack_kernel(expert_count, capacity, ids_ref, gates_ref, x_ref, g_ref, rows_ref, where_ref):
@@ -230,14 +229,14 @@
     out_ref = refs[at]
     bufs = refs[at + 1 : at + 1 + len(boxes)]
     in_sem, out_sem = refs[at + 1 + len(boxes) :]
-    for n, arrays in enumerate(sources):
-        start, high = boxes[n][2], boxes[n][3]
-        for k, array in enumerate(arrays):
-            last = k == len(arrays) - 1
-            wanted = source_ref[0] >= k if last else source_ref[0] == k
-
-            @pl.when(wanted)
-            def _(n=n, array=array, start=start, high=high):
+    most = max(len(arrays) for arrays in sources)
+    for k in range(most):
+
+        @pl.when(source_ref[0] == k)
+        def _(k=k):
+            for n, arrays in enumerate(sources):
+                array = arrays[min(k, len(arrays) - 1)]
+                start, high = boxes[n][2], boxes[n][3]
                 pltpu.make_async_copy(
                     array.at[pl.ds(start, high)], bufs[n], in_sem.at[n]
                 ).start()
@@ -418,7 +417,7 @@
     source = (is_moved * (1 + group)).reshape(1)
     cut = []
     for row, col, high, wide, arrays in pieces:
-        step = width // 4
+        step = width
         for at in range(0, high, step):
             cut.append((row, col, at, min(step, high - at), wide, arrays))
     adam_out = place(source, cut, width, inner)

time: 218 us -> 216 us (level)
  Pallas kernels: 46.2 us -> 43.8 us
where the time goes in v7:
time: 216 us; the launch traced here: 215 us
  waiting for transfers between devices  95.9 us (44%)
  blocking collectives  47.6 us (22%)
  Pallas kernels  43.8 us (20%)
  starting transfers between devices  18.5 us (9%)
  between operations  5.26 us (2%)
  other arithmetic  3.05 us (1%)
    ppermute x2, waiting for transfers between devices, run(): lax.ppermute(near, 'expert', pairs)  70 us
    all_to_all x1, blocking collectives, shards(): lax.all_to_all(rows.reshape(expert_count, capacity, 2 * width), 'expert',...  47.6 us
    all_to_all x1, waiting for transfers between devices, shards(): lax.all_to_all(total.astype(bf16).reshape(expert_count, capacity, width),...  19.7 us
    pallas_call x3, Pallas kernels, adam_block(): pl.pallas_call(adam_kernel, grid=(tiles,), in_specs=[pl.BlockSpec((rows,...  16.4 us
    pallas_call x1, Pallas kernels, rest_step(): pl.pallas_call(functools.partial(rest_kernel, len(rows)), grid=(tiles,),...  13.2 us
    all_to_all x1, starting transfers between devices, shards(): lax.all_to_all(total.astype(bf16).reshape(expert_count, capacity, width),...  6.29 us
    ppermute x2, waiting for transfers between devices, dp_shift(): return lax.ppermute(block, 'dp', [(i, i ^ apart) for i in range(count)])  6.18 us
    ppermute x2, starting transfers between devices, run(): lax.ppermute(near, 'expert', pairs)  5.47 us
  transfers between devices with their start and end apart: 10, of which 4 were waited for; matrix products, arithmetic and copies ran while one was open for 1% of the time, Pallas kernels for 9%

profile of v7, /device:TPU:6, one launch (start us, length us, event | category | flops | bytes accessed | tf_op | source)
XLA Modules:
  0.0 215.4 jit_solution(8254513571104201022)
XLA Ops:
  0.6 3.1 %pack_rows.1 = (bf16[384,2304]{1,0:T(8,128)(2,1)}, s32[2,128]{1,0:T(2,128)}) custom-call(s32[2,128]{1,0:T(2,128)} %bitcast.32, f32[2,128]{1,0:T(2,128)} %bitcast.33, bf16[128,1152]{1,0:T(8,128)(2,1)} %x_ref.1, bf16[128,1152]{1,0:T(8,128)(2,1)} %g_ref.1), custom_call_target="tpu_custom_call" | custom-call | tf_op jit(solution)/shard_map/pack_rows/pallas_call | solution.py:87
  3.7 47.6 %all_to_all.10 = bf16[16,24,2304]{2,1,0:T(8,128)(2,1)S(1)} all-to-all(bf16[16,24,2304]{2,1,0:T(8,128)(2,1)} %bitcast.31), channel_id=1, replica_groups=mesh['dp'=2,'expert'=16] {'expert'}, dimensions={0} | all-to-all | bytes 3538944 | tf_op jit(solution)/shard_map/all_to_all | solution.py:341
  51.3 0.0 collective-permute-start.28
  51.3 3.7 %collective-permute-done.28.refs_1_ = bf16[384,2304]{1,0:T(8,128)(2,1)S(1)} collective-permute-done((bf16[384,2304]{1,0:T(8,128)(2,1)S(1)}, bf16[384,2304]{1,0:T(8,128)(2,1)S(1)}, u32[]{:S(2)}, u32[]{:S(2)}) %collective-permute-start.28) | collective-permute-done | bytes 1769504 | tf_op jit(solution)/shard_map/ppermute | solution.py:321
  55.0 5.4 %first_step.1 = (bf16[1152,256]{1,0:T(8,128)(2,1)}, bf16[768,256]{1,0:T(8,128)(2,1)}, bf16[1152,768]{1,0:T(8,128)(2,1)}) custom-call(bf16[384,2304]{1,0:T(8,128)(2,1)S(1)} %bitcast.15, bf16[384,2304]{1,0:T(8,128)(2,1)S(1)} %collective-permute-done.28.refs_1_, bf16[1152,1536]{1,0:T(8,128)(2,1)} %bitcast.25, bf16[1536,1152]{1,0:T(8,128)(2,1)} %bitcast.28, ...), custom_call_target="tpu_custom_call" | custom-call | flops 1358954496 | bytes 4128768 | tf_op jit(solution)/shard_map/first_step/pallas_call | solution.py:121
  60.4 13.2 %rest_step.1 = (bf16[768,1280]{1,0:T(8,128)(2,1)}, bf16[384,1152]{1,0:T(8,128)(2,1)}, bf16[384,1152]{1,0:T(8,128)(2,1)}) custom-call(bf16[384,2304]{1,0:T(8,128)(2,1)S(1)} %bitcast.16, bf16[384,2304]{1,0:T(8,128)(2,1)S(1)} %collective-permute-done.28.refs_1_, bf16[768,256]{1,0:T(8,128)(2,1)} %get-tuple-element.103.refs_2_, bf16[1152,1536]{1,0:T(8,128)(2,1)} %bitcast.26, ...), custom_call_target="tpu_custom_call" | custom-call | flops 6794772480 | bytes 5898240 | tf_op jit(solution)/shard_map/rest_step/pallas_call | solution.py:170
  73.6 0.1 collective-permute-start.30
  73.8 2.5 %collective-permute-done.30 = bf16[384,1152]{1,0:T(8,128)(2,1)S(1)} collective-permute-done((bf16[384,1152]{1,0:T(8,128)(2,1)}, bf16[384,1152]{1,0:T(8,128)(2,1)S(1)}, u32[]{:S(2)}, u32[]{:S(2)}) %collective-permute-start.30) | collective-permute-done | bytes 884768 | tf_op jit(solution)/shard_map/ppermute | solution.py:321
  76.2 2.4 %add_convert_fusion = bf16[384,1152]{1,0:T(8,128)(2,1)} fusion(bf16[384,1152]{1,0:T(8,128)(2,1)S(1)} %collective-permute-done.30, bf16[384,1152]{1,0:T(8,128)(2,1)} %get-tuple-element.106), kind=kLoop, calls=%fused_computation | loop fusion | flops 1769472 | bytes 2654208 | tf_op jit(solution)/shard_map/convert_element_type | solution.py:369
  78.6 6.3 %all-to-all-start.1 = ((bf16[16,24,1152]{2,1,0:T(8,128)(2,1)}), bf16[16,24,1152]{2,1,0:T(8,128)(2,1)}, u32[]{:S(2)}, u32[]{:S(2)}) async-start(bf16[16,24,1152]{2,1,0:T(8,128)(2,1)} %bitcast.8), calls=%async_computation.1 | async-start | bytes 1769472 | tf_op jit(solution)/shard_map/all_to_all | solution.py:368
  84.9 6.1 %shard_map.137.refs_7_ = bf16[576,1024]{1,0:T(8,128)(2,1)} custom-call(bf16[1152,768]{1,0:T(8,128)(2,1)} %get-tuple-element.102.xt_ref, bf16[768,1280]{1,0:T(8,128)(2,1)} %get-tuple-element.104.pre_ref, f32[1152,1536]{1,0:T(8,128)} %bitcast.18, f32[1152,1536]{1,0:T(8,128)} %bitcast.22), custom_call_target="tpu_custom_call" | custom-call | flops 905969664 | bytes 5898240 | tf_op jit(solution)/shard_map/pallas_call | solution.py:204
  91.0 0.0 copy-start.6
  91.0 0.0 copy-start.5
  91.0 0.6 collective-permute-start.29
  91.7 4.2 %shard_map.138.refs_2_ = bf16[1152,256]{1,0:T(8,128)(2,1)} custom-call(bf16[1152,768]{1,0:T(8,128)(2,1)} %get-tuple-element.102.xt_ref, bf16[768,1280]{1,0:T(8,128)(2,1)} %get-tuple-element.104.pre_ref, f32[1152,1536]{1,0:T(8,128)} %bitcast.19, f32[1152,1536]{1,0:T(8,128)} %bitcast.23), custom_call_target="tpu_custom_call" | custom-call | flops 452984832 | bytes 2949120 | tf_op jit(solution)/shard_map/pallas_call | solution.py:204
  95.8 2.4 %collective-permute-start.32 = (bf16[1152,256]{1,0:T(8,128)(2,1)}, bf16[1152,256]{1,0:T(8,128)(2,1)S(1)}, u32[]{:S(2)}, u32[]{:S(2)}) collective-permute-start(bf16[1152,256]{1,0:T(8,128)(2,1)} %shard_map.138.refs_2_), channel_id=1, source_target_pairs={{0,8},{1,9},{2,10},{3,11},{4,12},{5,13},{6,14},{7,15},{8,0},{9,1},... | collective-permute-start | bytes 1769480 | tf_op jit(solution)/shard_map/ppermute | solution.py:381
  98.3 0.5 collective-permute-start.31
  98.8 0.7 fusion.2
  102.0 0.7 dynamic_slice.7
  102.7 0.6 dynamic_slice.6
  105.3 6.1 %shard_map.136.refs_4_ = bf16[576,1024]{1,0:T(8,128)(2,1)} custom-call(bf16[1152,768]{1,0:T(8,128)(2,1)} %get-tuple-element.102.xt_ref, bf16[768,1280]{1,0:T(8,128)(2,1)} %get-tuple-element.104.pre_ref, f32[1152,1536]{1,0:T(8,128)} %bitcast.20, f32[1152,1536]{1,0:T(8,128)} %bitcast.24), custom_call_target="tpu_custom_call" | custom-call | flops 905969664 | bytes 5898240 | tf_op jit(solution)/shard_map/pallas_call | solution.py:204
  111.4 19.7 %all-to-all-done.1 = bf16[16,24,1152]{2,1,0:T(8,128)(2,1)} async-done(((bf16[16,24,1152]{2,1,0:T(8,128)(2,1)}), bf16[16,24,1152]{2,1,0:T(8,128)(2,1)}, u32[]{:S(2)}, u32[]{:S(2)}) %all-to-all-start.1) | async-done | bytes 884768 | tf_op jit(solution)/shard_map/all_to_all | solution.py:368
  131.1 2.3 %combine_rows.1 = bf16[128,1152]{1,0:T(8,128)(2,1)} custom-call(s32[2,128]{1,0:T(2,128)} %get-tuple-element.105.where_ref, bf16[384,1152]{1,0:T(8,128)(2,1)} %bitcast.9.back_ref), custom_call_target="tpu_custom_call" | custom-call | tf_op jit(solution)/shard_map/combine_rows/pallas_call | solution.py:312
  133.4 75.1 %conditional.3 = (bf16[576,1024]{1,0:T(8,128)(2,1)}, bf16[576,1024]{1,0:T(8,128)(2,1)}) conditional(s32[]{:T(128)} %bitcast.12, (bf16[576,1024]{1,0:T(8,128)(2,1)}, bf16[576,1024]{1,0:T(8,128)(2,1)}) %tuple.66, (bf16[576,1024]{1,0:T(8,128)(2,1)}, bf16[576,1024]{1,0:T(8,128)(2,1)}) %tuple.66, ...), branch_computations={%region_10.11_spmd, %region_11.12_spmd, %region_12.13_spmd, %regio... | conditional | bytes 9437280 | solution.py:407
  133.4 3.8 %collective-permute-start.16 = (bf16[576,1024]{1,0:T(8,128)(2,1)}, bf16[576,1024]{1,0:T(8,128)(2,1)}, u32[]{:S(2)}, u32[]{:S(2)}) collective-permute-start(bf16[576,1024]{1,0:T(8,128)(2,1)} %get-tuple-element.72), channel_id=1, source_target_pairs={{3,11},{11,3},{7,15},{15,7},{19,27},{27,19},{23,31},{31,23}} | collective-permute-start | bytes 3538952 | tf_op jit(solution)/shard_map/cond/branch_1_fun/ppermute | solution.py:397
  137.2 1.3 collective-permute-start.17
  138.5 70.0 %collective-permute-done.16 = bf16[576,1024]{1,0:T(8,128)(2,1)} collective-permute-done((bf16[576,1024]{1,0:T(8,128)(2,1)}, bf16[576,1024]{1,0:T(8,128)(2,1)}, u32[]{:S(2)}, u32[]{:S(2)}) %collective-permute-start.16) | collective-permute-done | bytes 1179680 | tf_op jit(solution)/shard_map/cond/branch_1_fun/ppermute | solution.py:397
  208.5 0.0 collective-permute-done.17
  208.5 3.5 %conditional.2 = (bf16[576,1024]{1,0:T(8,128)(2,1)}, bf16[576,1024]{1,0:T(8,128)(2,1)}) conditional(s32[]{:T(128)} %bitcast.11, (bf16[576,1024]{1,0:T(8,128)(2,1)}, bf16[576,1024]{1,0:T(8,128)(2,1)}) %tuple.66, (bf16[576,1024]{1,0:T(8,128)(2,1)}, bf16[576,1024]{1,0:T(8,128)(2,1)}) %tuple.66, ...), branch_computations={%region_3.4_spmd, %region_4.5_spmd, %region_5.6_spmd, %region_6.7_... | conditional | bytes 9437280 | solution.py:407
  208.5 1.7 collective-permute-start
  210.2 1.8 collective-permute-start.1
  212.0 3.4 %place.1 = bf16[1152,1536]{1,0:T(8,128)(2,1)} custom-call(s32[1]{0:T(128)} %bitcast.10.source_ref, bf16[1152,256]{1,0:T(8,128)(2,1)S(1)} %copy-done.2, bf16[1152,256]{1,0:T(8,128)(2,1)S(1)} %collective-permute-done.31.refs_1_, bf16[1152,256]{1,0:T(8,128)(2,1)S(1)} %copy-done.1, bf16[1152,256]{1,0:T(8,128)(2,1)S(1)} %collective-permute-done.32.refs_3_, ...), custom_call_target="tpu_custom_call" | custom-call | bytes 7077888 | tf_op jit(solution)/shard_map/place/pallas_call | solution.py:261
  (17 shorter events, 0.0 us)
Async XLA Ops:
  51.3 3.7 %collective-permute-start.28 = (bf16[384,2304]{1,0:T(8,128)(2,1)S(1)}, bf16[384,2304]{1,0:T(8,128)(2,1)S(1)}, u32[]{:S(2)}, u32[]{:S(2)}) collective-permute-start(bf16[384,2304]{1,0:T(8,128)(2,1)S(1)} %bitcast.14), channel_id=1, source_target_pairs={{0,16},{16,0},{1,17},{17,1},{2,18},{18,2},{3,19},{19,3},{4,20},{20... | collective-permute-start | bytes 5308424 | tf_op jit(solution)/shard_map/ppermute | solution.py:321
  73.6 2.6 %collective-permute-start.30 = (bf16[384,1152]{1,0:T(8,128)(2,1)}, bf16[384,1152]{1,0:T(8,128)(2,1)S(1)}, u32[]{:S(2)}, u32[]{:S(2)}) collective-permute-start(bf16[384,1152]{1,0:T(8,128)(2,1)} %get-tuple-element.107), channel_id=1, source_target_pairs={{0,16},{16,0},{1,17},{17,1},{2,18},{18,2},{3,19},{19,3},{4,20},{20... | collective-permute-start | bytes 2654216 | tf_op jit(solution)/shard_map/ppermute | solution.py:321
  78.6 52.5 %all-to-all-start.1 = ((bf16[16,24,1152]{2,1,0:T(8,128)(2,1)}), bf16[16,24,1152]{2,1,0:T(8,128)(2,1)}, u32[]{:S(2)}, u32[]{:S(2)}) async-start(bf16[16,24,1152]{2,1,0:T(8,128)(2,1)} %bitcast.8), calls=%async_computation.1 | async-start | bytes 1769472 | tf_op jit(solution)/shard_map/all_to_all | solution.py:368
  91.0 7.3 %copy-start.2 = (bf16[1152,256]{1,0:T(8,128)(2,1)S(1)}, bf16[1152,256]{1,0:T(8,128)(2,1)}, u32[]{:S(2)}) copy-start(bf16[1152,256]{1,0:T(8,128)(2,1)} %get-tuple-element.109.refs_0_) | copy-start | bytes 1769476
  91.0 7.8 %copy-start.3 = (s32[16]{0:T(128)S(1)}, s32[16]{0:T(128)}, u32[]{:S(2)}) copy-start(s32[16]{0:T(128)} %param.30) | copy-start | bytes 196
  91.0 7.8 %copy-start.4 = (pred[16]{0:T(512)(128)(4,1)S(1)}, pred[16]{0:T(512)(128)(4,1)}, u32[]{:S(2)}) copy-start(pred[16]{0:T(512)(128)(4,1)} %constant.32.clone) | copy-start | bytes 52
  91.0 11.0 %copy-start.6 = (s32[256]{0:T(256)S(1)}, s32[256]{0:T(256)}, u32[]{:S(2)}) copy-start(s32[256]{0:T(256)} %constant.31.clone) | copy-start | bytes 3076
  91.0 11.7 %copy-start.5 = (s32[256]{0:T(256)S(1)}, s32[256]{0:T(256)}, u32[]{:S(2)}) copy-start(s32[256]{0:T(256)} %constant.30.clone) | copy-start | bytes 3076
  91.0 42.3 %collective-permute-start.29 = (bf16[576,1024]{1,0:T(8,128)(2,1)}, bf16[576,1024]{1,0:T(8,128)(2,1)}, u32[]{:S(2)}, u32[]{:S(2)}) collective-permute-start(bf16[576,1024]{1,0:T(8,128)(2,1)} %shard_map.137.refs_7_), channel_id=1, source_target_pairs={{0,1},{1,0},{2,3},{3,2},{4,5},{5,4},{6,7},{7,6},{8,9},{9,8},{10,11... | collective-permute-start | bytes 3538952 | tf_op jit(solution)/shard_map/ppermute | solution.py:388
  95.8 116.1 %collective-permute-start.32 = (bf16[1152,256]{1,0:T(8,128)(2,1)}, bf16[1152,256]{1,0:T(8,128)(2,1)S(1)}, u32[]{:S(2)}, u32[]{:S(2)}) collective-permute-start(bf16[1152,256]{1,0:T(8,128)(2,1)} %shard_map.138.refs_2_), channel_id=1, source_target_pairs={{0,8},{1,9},{2,10},{3,11},{4,12},{5,13},{6,14},{7,15},{8,0},{9,1},... | collective-permute-start | bytes 1769480 | tf_op jit(solution)/shard_map/ppermute | solution.py:381
  98.3 113.7 %collective-permute-start.31 = (bf16[1152,256]{1,0:T(8,128)(2,1)S(1)}, bf16[1152,256]{1,0:T(8,128)(2,1)S(1)}, u32[]{:S(2)}, u32[]{:S(2)}) collective-permute-start(bf16[1152,256]{1,0:T(8,128)(2,1)S(1)} %copy-done.2), channel_id=1, source_target_pairs={{0,8},{1,9},{2,10},{3,11},{4,12},{5,13},{6,14},{7,15},{8,0},{9,1},... | collective-permute-start | bytes 1769480 | tf_op jit(solution)/shard_map/ppermute | solution.py:361
  105.2 106.7 %copy-start.1 = (bf16[1152,256]{1,0:T(8,128)(2,1)S(1)}, bf16[1152,256]{1,0:T(8,128)(2,1)}, u32[]{:S(2)}) copy-start(bf16[1152,256]{1,0:T(8,128)(2,1)} %shard_map.138.refs_2_) | copy-start | bytes 1769476
  111.4 100.6 %copy-start = (bf16[576,1024]{1,0:T(8,128)(2,1)S(1)}, bf16[576,1024]{1,0:T(8,128)(2,1)}, u32[]{:S(2)}) copy-start(bf16[576,1024]{1,0:T(8,128)(2,1)} %shard_map.137.refs_7_) | copy-start | bytes 3538948
  133.4 75.1 %collective-permute-start.16 = (bf16[576,1024]{1,0:T(8,128)(2,1)}, bf16[576,1024]{1,0:T(8,128)(2,1)}, u32[]{:S(2)}, u32[]{:S(2)}) collective-permute-start(bf16[576,1024]{1,0:T(8,128)(2,1)} %get-tuple-element.72), channel_id=1, source_target_pairs={{3,11},{11,3},{7,15},{15,7},{19,27},{27,19},{23,31},{31,23}} | collective-permute-start | bytes 3538952 | tf_op jit(solution)/shard_map/cond/branch_1_fun/ppermute | solution.py:397
  137.2 71.3 %collective-permute-start.17 = (bf16[576,1024]{1,0:T(8,128)(2,1)}, bf16[576,1024]{1,0:T(8,128)(2,1)}, u32[]{:S(2)}, u32[]{:S(2)}) collective-permute-start(bf16[576,1024]{1,0:T(8,128)(2,1)} %get-tuple-element.73), channel_id=1, source_target_pairs={{2,11},{10,3},{6,15},{14,7},{18,27},{26,19},{22,31},{30,23}} | collective-permute-start | bytes 3538952 | tf_op jit(solution)/shard_map/cond/branch_1_fun/ppermute | solution.py:398
  208.5 3.5 %collective-permute-start = (bf16[576,1024]{1,0:T(8,128)(2,1)}, bf16[576,1024]{1,0:T(8,128)(2,1)}, u32[]{:S(2)}, u32[]{:S(2)}) collective-permute-start(bf16[576,1024]{1,0:T(8,128)(2,1)} %get-tuple-element.56), channel_id=1, source_target_pairs={{0,8},{8,0},{1,9},{9,1},{16,24},{24,16},{17,25},{25,17}} | collective-permute-start | bytes 3538952 | tf_op jit(solution)/shard_map/cond/branch_0_fun/ppermute | solution.py:397
  210.2 1.8 collective-permute-start.1

commit v8 on v7

--- a/solution.py
+++ b/solution.py
@@ -46,7 +46,8 @@
     second_hat = (beta_two * unbias_two) * second_moment + (
         (1.0 - beta_two) * unbias_two
     ) * (weight_grad * weight_grad)
-    return (first_hat / (jnp.sqrt(second_hat) + adam_eps)).astype(bf16)
+    root = second_hat * lax.rsqrt(second_hat)
+    return (first_hat / (root + adam_eps)).astype(bf16)
 
 
 def pack_kernel(expert_count, capacity, ids_ref, gates_ref, x_ref, g_ref, rows_ref, where_ref):
@@ -94,51 +95,118 @@
     )(id_rows, gate_rows, tokens, out_grad)
 
 
+def pre_block(block, w_in, w_out):
+    width = block.shape[1] // 2
+    pre_act = mxu(block[:, :width], w_in, NN)
+    act_grad = mxu(block[:, width:], w_out, NT)
+    return (act_grad * gelu_slope(pre_act)).astype(bf16)
+
+
 def pre_tile(rows, w_in, w_out, pre_ref):
-    per, width = rows[0].shape[0], rows[0].shape[1] // 2
+    per = rows[0].shape[0]
     for b, block in enumerate(rows):
-        pre_act = mxu(block[:, :width], w_in, NN)
-        act_grad = mxu(block[:, width:], w_out, NT)
-        pre_ref[b * per : (b + 1) * per, :] = (act_grad * gelu_slope(pre_act)).astype(bf16)
-
-
-def first_kernel(blocks, *refs):
-    rows = refs[:blocks]
-    w_in_ref, w_out_ref, m_ref, v_ref, adam_ref, pre_ref, xt_ref = refs[blocks:]
-    width, per = m_ref.shape[0], rows[0].shape[0]
-    for b in range(blocks):
-        xt_ref[:, b * per : (b + 1) * per] = rows[b][:, :width].T
-    pre_tile(rows, w_in_ref[...], w_out_ref[...], pre_ref)
-    weight_grad = mxu(xt_ref[...], pre_ref[...], NN)
-    adam_ref[...] = adam_step(weight_grad, m_ref[...], v_ref[...])
-
-
-def first_step(rows, w_in, w_out, first_moment, second_moment, tile):
-    per, width = rows[0].shape[0], rows[0].shape[1] // 2
-    total = len(rows) * per
+        pre_ref[b * per : (b + 1) * per, :] = pre_block(block, w_in, w_out)
+
+
+def own_kernel(rows_ref, w_in_ref, w_out_ref, pre_ref, xt_ref):
+    xt_ref[...] = rows_ref[:, : xt_ref.shape[0]].T
+    pre_ref[...] = pre_block(rows_ref, w_in_ref[...], w_out_ref[...])
+
+
+def own_step(rows, w_in, w_out, tile):
+    per, width = rows.shape[0], rows.shape[1] // 2
     corner = lambda i: (0, 0)
-    columns = pl.BlockSpec((width, tile), corner)
+    return pl.pallas_call(
+        own_kernel,
+        grid=(1,),
+        in_specs=[
+            pl.BlockSpec(rows.shape, corner),
+            pl.BlockSpec((width, tile), corner),
+            pl.BlockSpec((tile, width), corner),
+        ],
+        out_specs=[pl.BlockSpec((per, tile), corner), pl.BlockSpec((width, per), corner)],
+        out_shape=[
+            jax.ShapeDtypeStruct((per, tile), bf16),
+            jax.ShapeDtypeStruct((width, per), bf16),
+        ],
+        compiler_params=pltpu.CompilerParams(vmem_limit_bytes=48 * MIB),
+        cost_estimate=pl.CostEstimate(
+            flops=4 * per * width * tile, bytes_accessed=4 * tile * width, transcendentals=0
+        ),
+        name="own_step",
+    )(rows, w_in, w_out)
+
+
+def first_kernel(others, *refs):
+    rows = refs[:others]
+    pre_own, xt_own, w_in_ref, w_out_ref, m_ref, v_ref, adam_ref, pre_ref, xt_ref = refs[
+        others : others + 9
+    ]
+    m_buf, v_buf, pre_buf, xt_buf, sems = refs[others + 9 :]
+    width, tile = m_buf.shape
+    per = xt_own.shape[1]
+    gets = [
+        pltpu.make_async_copy(array.at[:, pl.ds(0, tile)], buf, sems.at[n])
+        for n, (array, buf) in enumerate(((m_ref, m_buf), (v_ref, v_buf)))
+    ]
+    for get in gets:
+        get.start()
+    xt_buf[:, :per] = xt_own[...]
+    pre_buf[:per, :] = pre_own[...]
+    for b in range(others):
+        part = slice((b + 1) * per, (b + 2) * per)
+        xt_buf[:, part] = rows[b][:, :width].T
+        pre_buf[part, :] = pre_block(rows[b], w_in_ref[...], w_out_ref[...])
+    puts = [
+        pltpu.make_async_copy(xt_buf, xt_ref, sems.at[2]),
+        pltpu.make_async_copy(pre_buf, pre_ref, sems.at[3]),
+    ]
+    for put in puts:
+        put.start()
+    weight_grad = mxu(xt_buf[...], pre_buf[...], NN)
+    for get in gets:
+        get.wait()
+    adam_ref[...] = adam_step(weight_grad, m_buf[...], v_buf[...])
+    for put in puts:
+        put.wait()
+
+
+def first_step(rows, pre_own, xt_own, w_in, w_out, first_moment, second_moment, tile):
+    width, per = xt_own.shape
+    total = (len(rows) + 1) * per
+    corner = lambda i: (0, 0)
+    anywhere = pl.BlockSpec(memory_space=pl.ANY)
     return pl.pallas_call(
         functools.partial(first_kernel, len(rows)),
         grid=(1,),
         in_specs=[pl.BlockSpec(r.shape, corner) for r in rows]
-        + [columns, pl.BlockSpec((tile, width), corner), columns, columns],
-        out_specs=[
-            columns,
-            pl.BlockSpec((total, tile), corner),
-            pl.BlockSpec((width, total), corner),
-        ],
+        + [
+            pl.BlockSpec((per, tile), corner),
+            pl.BlockSpec((width, per), corner),
+            pl.BlockSpec((width, tile), corner),
+            pl.BlockSpec((tile, width), corner),
+            anywhere,
+            anywhere,
+        ],
+        out_specs=[pl.BlockSpec((width, tile), corner), anywhere, anywhere],
         out_shape=[
             jax.ShapeDtypeStruct((width, tile), bf16),
             jax.ShapeDtypeStruct((total, tile), bf16),
             jax.ShapeDtypeStruct((width, total), bf16),
+        ],
+        scratch_shapes=[
+            pltpu.VMEM((width, tile), f32),
+            pltpu.VMEM((width, tile), f32),
+            pltpu.VMEM((total, tile), bf16),
+            pltpu.VMEM((width, total), bf16),
+            pltpu.SemaphoreType.DMA((4,)),
         ],
         compiler_params=pltpu.CompilerParams(vmem_limit_bytes=56 * MIB),
         cost_estimate=pl.CostEstimate(
             flops=6 * total * width * tile, bytes_accessed=14 * tile * width, transcendentals=0
         ),
         name="first_step",
-    )(*rows, w_in, w_out, first_moment, second_moment)
+    )(*rows, pre_own, xt_own, w_in, w_out, first_moment, second_moment)
 
 
 def rest_kernel(blocks, *refs):
@@ -355,8 +423,12 @@
     route = [(e, e ^ half) for e in range(expert_count)]
     across = [(e, e ^ 1) for e in range(expert_count)]
 
+    pre_own, xt_own = own_step(all_rows[0], w_in[0], w_out[0], tile)
+    if dp_count == 2:
+        pre_own = pltpu.with_memory_space_constraint(pre_own, pltpu.VMEM)
+        xt_own = pltpu.with_memory_space_constraint(xt_own, pltpu.VMEM)
     first, pre_first, x_t = first_step(
-        all_rows, w_in[0], w_out[0], first_moment[0], second_moment[0], tile
+        all_rows[1:], pre_own, xt_own, w_in[0], w_out[0], first_moment[0], second_moment[0], tile
     )
     first_got = lax.ppermute(first, "expert", route)
     pieces = [(0, 0, width, tile, [first, first_got])]

time: 216 us -> 217 us (level)
  transfers between devices with their start and end apart: 10 -> 10, of which waited for: 4 -> 5; matrix products, arithmetic and copies ran while one was open for 1% -> 1% of each run, Pallas kernels for 9% -> 9%
where the time goes in v8:
time: 217 us; the launch traced here: 216 us
  waiting for transfers between devices  94.9 us (44%)
  blocking collectives  47.6 us (22%)
  Pallas kernels  45.9 us (21%)
  starting transfers between devices  18.5 us (9%)
  between operations  5.08 us (2%)
  other arithmetic  3.08 us (1%)
    ppermute x2, waiting for transfers between devices, run(): lax.ppermute(near, 'expert', pairs)  70 us
    all_to_all x1, blocking collectives, shards(): lax.all_to_all(rows.reshape(expert_count, capacity, 2 * width), 'expert',...  47.6 us
    all_to_all x1, waiting for transfers between devices, shards(): lax.all_to_all(total.astype(bf16).reshape(expert_count, capacity, width),...  20.6 us
    pallas_call x3, Pallas kernels, adam_block(): pl.pallas_call(adam_kernel, grid=(tiles,), in_specs=[pl.BlockSpec((rows,...  15.8 us
    pallas_call x1, Pallas kernels, rest_step(): pl.pallas_call(functools.partial(rest_kernel, len(rows)), grid=(tiles,),...  13.2 us
    all_to_all x1, starting transfers between devices, shards(): lax.all_to_all(total.astype(bf16).reshape(expert_count, capacity, width),...  6.27 us
    pallas_call x1, Pallas kernels, first_step(): pl.pallas_call(functools.partial(first_kernel, len(rows)), grid=(1,), in_...  6.1 us
    ppermute x2, starting transfers between devices, run(): lax.ppermute(near, 'expert', pairs)  5.42 us
  transfers between devices with their start and end apart: 10, of which 5 were waited for; matrix products, arithmetic and copies ran while one was open for 1% of the time, Pallas kernels for 9%

profile of v8, /device:TPU:6, one launch (start us, length us, event | category | flops | bytes accessed | tf_op | source)
XLA Modules:
  0.0 216.2 jit_solution(9660856330320915574)
XLA Ops:
  0.6 3.1 %pack_rows.1 = (bf16[384,2304]{1,0:T(8,128)(2,1)}, s32[2,128]{1,0:T(2,128)}) custom-call(s32[2,128]{1,0:T(2,128)} %bitcast.34, f32[2,128]{1,0:T(2,128)} %bitcast.35, bf16[128,1152]{1,0:T(8,128)(2,1)} %x_ref.1, bf16[128,1152]{1,0:T(8,128)(2,1)} %g_ref.1), custom_call_target="tpu_custom_call" | custom-call | tf_op jit(solution)/shard_map/pack_rows/pallas_call | solution.py:88
  3.7 47.6 %all_to_all.10 = bf16[16,24,2304]{2,1,0:T(8,128)(2,1)S(1)} all-to-all(bf16[16,24,2304]{2,1,0:T(8,128)(2,1)} %bitcast.33), channel_id=1, replica_groups=mesh['dp'=2,'expert'=16] {'expert'}, dimensions={0} | all-to-all | bytes 3538944 | tf_op jit(solution)/shard_map/all_to_all | solution.py:409
  51.3 2.0 own_step.1
  53.3 1.6 collective-permute-done.28.refs_0_.refs_1_
  55.0 6.1 %first_step.1 = (bf16[1152,256]{1,0:T(8,128)(2,1)}, bf16[768,256]{1,0:T(8,128)(2,1)}, bf16[1152,768]{1,0:T(8,128)(2,1)}) custom-call(bf16[384,2304]{1,0:T(8,128)(2,1)S(1)} %collective-permute-done.28.refs_0_.refs_1_, bf16[384,256]{1,0:T(8,128)(2,1)S(1)} %get-tuple-element.104.refs_1_, bf16[1152,384]{1,0:T(8,128)(2,1)S(1)} %get-tuple-element.105.refs_2_, ...), custom_call_target="tpu_custom_call" | custom-call | flops 1358954496 | bytes 4128768 | tf_op jit(solution)/shard_map/first_step/pallas_call | solution.py:179
  61.1 13.2 %rest_step.1 = (bf16[768,1280]{1,0:T(8,128)(2,1)}, bf16[384,1152]{1,0:T(8,128)(2,1)}, bf16[384,1152]{1,0:T(8,128)(2,1)}) custom-call(bf16[384,2304]{1,0:T(8,128)(2,1)S(1)} %bitcast.16, bf16[384,2304]{1,0:T(8,128)(2,1)S(1)} %collective-permute-done.28.refs_0_.refs_1_, bf16[768,256]{1,0:T(8,128)(2,1)} %get-tuple-element.107.refs_2_, ...), custom_call_target="tpu_custom_call" | custom-call | flops 6794772480 | bytes 5898240 | tf_op jit(solution)/shard_map/rest_step/pallas_call | solution.py:238
  74.3 0.2 collective-permute-start.30
  74.5 2.5 %collective-permute-done.30 = bf16[384,1152]{1,0:T(8,128)(2,1)S(1)} collective-permute-done((bf16[384,1152]{1,0:T(8,128)(2,1)}, bf16[384,1152]{1,0:T(8,128)(2,1)S(1)}, u32[]{:S(2)}, u32[]{:S(2)}) %collective-permute-start.30) | collective-permute-done | bytes 884768 | tf_op jit(solution)/shard_map/ppermute | solution.py:389
  76.9 2.4 %add_convert_fusion = bf16[384,1152]{1,0:T(8,128)(2,1)} fusion(bf16[384,1152]{1,0:T(8,128)(2,1)S(1)} %collective-permute-done.30, bf16[384,1152]{1,0:T(8,128)(2,1)} %get-tuple-element.110), kind=kLoop, calls=%fused_computation | loop fusion | flops 1769472 | bytes 2654208 | tf_op jit(solution)/shard_map/convert_element_type | solution.py:441
  79.3 6.3 %all-to-all-start.1 = ((bf16[16,24,1152]{2,1,0:T(8,128)(2,1)}), bf16[16,24,1152]{2,1,0:T(8,128)(2,1)}, u32[]{:S(2)}, u32[]{:S(2)}) async-start(bf16[16,24,1152]{2,1,0:T(8,128)(2,1)} %bitcast.8), calls=%async_computation.1 | async-start | bytes 1769472 | tf_op jit(solution)/shard_map/all_to_all | solution.py:440
  85.6 5.8 %shard_map.137.refs_7_ = bf16[576,1024]{1,0:T(8,128)(2,1)} custom-call(bf16[1152,768]{1,0:T(8,128)(2,1)} %get-tuple-element.106.xt_ref, bf16[768,1280]{1,0:T(8,128)(2,1)} %get-tuple-element.108.pre_ref, f32[1152,1536]{1,0:T(8,128)} %bitcast.18, f32[1152,1536]{1,0:T(8,128)} %bitcast.22), custom_call_target="tpu_custom_call" | custom-call | flops 905969664 | bytes 5898240 | tf_op jit(solution)/shard_map/pallas_call | solution.py:272
  91.4 0.0 copy-start.6
  91.5 0.0 copy-start.5
  91.5 0.6 collective-permute-start.29
  92.1 4.0 %shard_map.138.refs_2_ = bf16[1152,256]{1,0:T(8,128)(2,1)} custom-call(bf16[1152,768]{1,0:T(8,128)(2,1)} %get-tuple-element.106.xt_ref, bf16[768,1280]{1,0:T(8,128)(2,1)} %get-tuple-element.108.pre_ref, f32[1152,1536]{1,0:T(8,128)} %bitcast.19, f32[1152,1536]{1,0:T(8,128)} %bitcast.23), custom_call_target="tpu_custom_call" | custom-call | flops 452984832 | bytes 2949120 | tf_op jit(solution)/shard_map/pallas_call | solution.py:272
  96.1 2.4 %collective-permute-start.32 = (bf16[1152,256]{1,0:T(8,128)(2,1)}, bf16[1152,256]{1,0:T(8,128)(2,1)S(1)}, u32[]{:S(2)}, u32[]{:S(2)}) collective-permute-start(bf16[1152,256]{1,0:T(8,128)(2,1)} %shard_map.138.refs_2_), channel_id=1, source_target_pairs={{0,8},{1,9},{2,10},{3,11},{4,12},{5,13},{6,14},{7,15},{8,0},{9,1},... | collective-permute-start | bytes 1769480 | tf_op jit(solution)/shard_map/ppermute | solution.py:453
  98.5 0.5 collective-permute-start.31
  99.0 0.7 fusion.2
  102.2 0.6 dynamic_slice.7
  102.8 0.6 dynamic_slice.6
  105.2 5.9 %shard_map.136.refs_4_ = bf16[576,1024]{1,0:T(8,128)(2,1)} custom-call(bf16[1152,768]{1,0:T(8,128)(2,1)} %get-tuple-element.106.xt_ref, bf16[768,1280]{1,0:T(8,128)(2,1)} %get-tuple-element.108.pre_ref, f32[1152,1536]{1,0:T(8,128)} %bitcast.20, f32[1152,1536]{1,0:T(8,128)} %bitcast.24), custom_call_target="tpu_custom_call" | custom-call | flops 905969664 | bytes 5898240 | tf_op jit(solution)/shard_map/pallas_call | solution.py:272
  111.2 20.6 %all-to-all-done.1 = bf16[16,24,1152]{2,1,0:T(8,128)(2,1)} async-done(((bf16[16,24,1152]{2,1,0:T(8,128)(2,1)}), bf16[16,24,1152]{2,1,0:T(8,128)(2,1)}, u32[]{:S(2)}, u32[]{:S(2)}) %all-to-all-start.1) | async-done | bytes 884768 | tf_op jit(solution)/shard_map/all_to_all | solution.py:440
  131.8 2.3 %combine_rows.1 = bf16[128,1152]{1,0:T(8,128)(2,1)} custom-call(s32[2,128]{1,0:T(2,128)} %get-tuple-element.109.where_ref, bf16[384,1152]{1,0:T(8,128)(2,1)} %bitcast.9.back_ref), custom_call_target="tpu_custom_call" | custom-call | tf_op jit(solution)/shard_map/combine_rows/pallas_call | solution.py:380
  134.1 75.1 %conditional.3 = (bf16[576,1024]{1,0:T(8,128)(2,1)}, bf16[576,1024]{1,0:T(8,128)(2,1)}) conditional(s32[]{:T(128)} %bitcast.12, (bf16[576,1024]{1,0:T(8,128)(2,1)}, bf16[576,1024]{1,0:T(8,128)(2,1)}) %tuple.66, (bf16[576,1024]{1,0:T(8,128)(2,1)}, bf16[576,1024]{1,0:T(8,128)(2,1)}) %tuple.66, ...), branch_computations={%region_10.11_spmd, %region_11.12_spmd, %region_12.13_spmd, %regio... | conditional | bytes 9437280 | solution.py:479
  134.1 3.7 %collective-permute-start.16 = (bf16[576,1024]{1,0:T(8,128)(2,1)}, bf16[576,1024]{1,0:T(8,128)(2,1)}, u32[]{:S(2)}, u32[]{:S(2)}) collective-permute-start(bf16[576,1024]{1,0:T(8,128)(2,1)} %get-tuple-element.72), channel_id=1, source_target_pairs={{3,11},{11,3},{7,15},{15,7},{19,27},{27,19},{23,31},{31,23}} | collective-permute-start | bytes 3538952 | tf_op jit(solution)/shard_map/cond/branch_1_fun/ppermute | solution.py:469
  137.8 1.3 collective-permute-start.17
  139.1 70.0 %collective-permute-done.16 = bf16[576,1024]{1,0:T(8,128)(2,1)} collective-permute-done((bf16[576,1024]{1,0:T(8,128)(2,1)}, bf16[576,1024]{1,0:T(8,128)(2,1)}, u32[]{:S(2)}, u32[]{:S(2)}) %collective-permute-start.16) | collective-permute-done | bytes 1179680 | tf_op jit(solution)/shard_map/cond/branch_1_fun/ppermute | solution.py:469
  209.2 0.1 collective-permute-done.17
  209.2 3.4 %conditional.2 = (bf16[576,1024]{1,0:T(8,128)(2,1)}, bf16[576,1024]{1,0:T(8,128)(2,1)}) conditional(s32[]{:T(128)} %bitcast.11, (bf16[576,1024]{1,0:T(8,128)(2,1)}, bf16[576,1024]{1,0:T(8,128)(2,1)}) %tuple.66, (bf16[576,1024]{1,0:T(8,128)(2,1)}, bf16[576,1024]{1,0:T(8,128)(2,1)}) %tuple.66, ...), branch_computations={%region_3.4_spmd, %region_4.5_spmd, %region_5.6_spmd, %region_6.7_... | conditional | bytes 9437280 | solution.py:479
  209.2 1.7 collective-permute-start
  210.9 1.8 collective-permute-start.1
  212.7 3.4 %place.1 = bf16[1152,1536]{1,0:T(8,128)(2,1)} custom-call(s32[1]{0:T(128)} %bitcast.10.source_ref, bf16[1152,256]{1,0:T(8,128)(2,1)S(1)} %copy-done.2, bf16[1152,256]{1,0:T(8,128)(2,1)S(1)} %collective-permute-done.31.refs_1_, bf16[1152,256]{1,0:T(8,128)(2,1)S(1)} %copy-done.1, bf16[1152,256]{1,0:T(8,128)(2,1)S(1)} %collective-permute-done.32.refs_3_, ...), custom_call_target="tpu_custom_call" | custom-call | bytes 7077888 | tf_op jit(solution)/shard_map/place/pallas_call | solution.py:329
  (18 shorter events, 0.0 us)
Async XLA Ops:
  51.3 3.7 %collective-permute-start.28 = (bf16[384,2304]{1,0:T(8,128)(2,1)S(1)}, bf16[384,2304]{1,0:T(8,128)(2,1)S(1)}, u32[]{:S(2)}, u32[]{:S(2)}) collective-permute-start(bf16[384,2304]{1,0:T(8,128)(2,1)S(1)} %bitcast.14), channel_id=1, source_target_pairs={{0,16},{16,0},{1,17},{17,1},{2,18},{18,2},{3,19},{19,3},{4,20},{20... | collective-permute-start | bytes 5308424 | tf_op jit(solution)/shard_map/ppermute | solution.py:389
  74.3 2.6 %collective-permute-start.30 = (bf16[384,1152]{1,0:T(8,128)(2,1)}, bf16[384,1152]{1,0:T(8,128)(2,1)S(1)}, u32[]{:S(2)}, u32[]{:S(2)}) collective-permute-start(bf16[384,1152]{1,0:T(8,128)(2,1)} %get-tuple-element.111), channel_id=1, source_target_pairs={{0,16},{16,0},{1,17},{17,1},{2,18},{18,2},{3,19},{19,3},{4,20},{20... | collective-permute-start | bytes 2654216 | tf_op jit(solution)/shard_map/ppermute | solution.py:389
  79.3 52.5 %all-to-all-start.1 = ((bf16[16,24,1152]{2,1,0:T(8,128)(2,1)}), bf16[16,24,1152]{2,1,0:T(8,128)(2,1)}, u32[]{:S(2)}, u32[]{:S(2)}) async-start(bf16[16,24,1152]{2,1,0:T(8,128)(2,1)} %bitcast.8), calls=%async_computation.1 | async-start | bytes 1769472 | tf_op jit(solution)/shard_map/all_to_all | solution.py:440
  91.4 7.1 %copy-start.2 = (bf16[1152,256]{1,0:T(8,128)(2,1)S(1)}, bf16[1152,256]{1,0:T(8,128)(2,1)}, u32[]{:S(2)}) copy-start(bf16[1152,256]{1,0:T(8,128)(2,1)} %get-tuple-element.113.refs_0_) | copy-start | bytes 1769476
  91.4 7.6 %copy-start.3 = (s32[16]{0:T(128)S(1)}, s32[16]{0:T(128)}, u32[]{:S(2)}) copy-start(s32[16]{0:T(128)} %param.30) | copy-start | bytes 196
  91.4 7.6 %copy-start.4 = (pred[16]{0:T(512)(128)(4,1)S(1)}, pred[16]{0:T(512)(128)(4,1)}, u32[]{:S(2)}) copy-start(pred[16]{0:T(512)(128)(4,1)} %constant.32.clone) | copy-start | bytes 52
  91.4 10.8 %copy-start.6 = (s32[256]{0:T(256)S(1)}, s32[256]{0:T(256)}, u32[]{:S(2)}) copy-start(s32[256]{0:T(256)} %constant.31.clone) | copy-start | bytes 3076
  91.5 11.4 %copy-start.5 = (s32[256]{0:T(256)S(1)}, s32[256]{0:T(256)}, u32[]{:S(2)}) copy-start(s32[256]{0:T(256)} %constant.30.clone) | copy-start | bytes 3076
  91.5 42.6 %collective-permute-start.29 = (bf16[576,1024]{1,0:T(8,128)(2,1)}, bf16[576,1024]{1,0:T(8,128)(2,1)}, u32[]{:S(2)}, u32[]{:S(2)}) collective-permute-start(bf16[576,1024]{1,0:T(8,128)(2,1)} %shard_map.137.refs_7_), channel_id=1, source_target_pairs={{0,1},{1,0},{2,3},{3,2},{4,5},{5,4},{6,7},{7,6},{8,9},{9,8},{10,11... | collective-permute-start | bytes 3538952 | tf_op jit(solution)/shard_map/ppermute | solution.py:460
  96.1 116.6 %collective-permute-start.32 = (bf16[1152,256]{1,0:T(8,128)(2,1)}, bf16[1152,256]{1,0:T(8,128)(2,1)S(1)}, u32[]{:S(2)}, u32[]{:S(2)}) collective-permute-start(bf16[1152,256]{1,0:T(8,128)(2,1)} %shard_map.138.refs_2_), channel_id=1, source_target_pairs={{0,8},{1,9},{2,10},{3,11},{4,12},{5,13},{6,14},{7,15},{8,0},{9,1},... | collective-permute-start | bytes 1769480 | tf_op jit(solution)/shard_map/ppermute | solution.py:453
  98.5 114.2 %collective-permute-start.31 = (bf16[1152,256]{1,0:T(8,128)(2,1)S(1)}, bf16[1152,256]{1,0:T(8,128)(2,1)S(1)}, u32[]{:S(2)}, u32[]{:S(2)}) collective-permute-start(bf16[1152,256]{1,0:T(8,128)(2,1)S(1)} %copy-done.2), channel_id=1, source_target_pairs={{0,8},{1,9},{2,10},{3,11},{4,12},{5,13},{6,14},{7,15},{8,0},{9,1},... | collective-permute-start | bytes 1769480 | tf_op jit(solution)/shard_map/ppermute | solution.py:433
  105.2 107.5 %copy-start.1 = (bf16[1152,256]{1,0:T(8,128)(2,1)S(1)}, bf16[1152,256]{1,0:T(8,128)(2,1)}, u32[]{:S(2)}) copy-start(bf16[1152,256]{1,0:T(8,128)(2,1)} %shard_map.138.refs_2_) | copy-start | bytes 1769476
  111.2 101.5 %copy-start = (bf16[576,1024]{1,0:T(8,128)(2,1)S(1)}, bf16[576,1024]{1,0:T(8,128)(2,1)}, u32[]{:S(2)}) copy-start(bf16[576,1024]{1,0:T(8,128)(2,1)} %shard_map.137.refs_7_) | copy-start | bytes 3538948
  134.1 75.1 %collective-permute-start.16 = (bf16[576,1024]{1,0:T(8,128)(2,1)}, bf16[576,1024]{1,0:T(8,128)(2,1)}, u32[]{:S(2)}, u32[]{:S(2)}) collective-permute-start(bf16[576,1024]{1,0:T(8,128)(2,1)} %get-tuple-element.72), channel_id=1, source_target_pairs={{3,11},{11,3},{7,15},{15,7},{19,27},{27,19},{23,31},{31,23}} | collective-permute-start | bytes 3538952 | tf_op jit(solution)/shard_map/cond/branch_1_fun/ppermute | solution.py:469
  137.8 71.4 %collective-permute-start.17 = (bf16[576,1024]{1,0:T(8,128)(2,1)}, bf16[576,1024]{1,0:T(8,128)(2,1)}, u32[]{:S(2)}, u32[]{:S(2)}) collective-permute-start(bf16[576,1024]{1,0:T(8,128)(2,1)} %get-tuple-element.73), channel_id=1, source_target_pairs={{2,11},{10,3},{6,15},{14,7},{18,27},{26,19},{22,31},{30,23}} | collective-permute-start | bytes 3538952 | tf_op jit(solution)/shard_map/cond/branch_1_fun/ppermute | solution.py:470
  209.2 3.4 %collective-permute-start = (bf16[576,1024]{1,0:T(8,128)(2,1)}, bf16[576,1024]{1,0:T(8,128)(2,1)}, u32[]{:S(2)}, u32[]{:S(2)}) collective-permute-start(bf16[576,1024]{1,0:T(8,128)(2,1)} %get-tuple-element.56), channel_id=1, source_target_pairs={{0,8},{8,0},{1,9},{9,1},{16,24},{24,16},{17,25},{25,17}} | collective-permute-start | bytes 3538952 | tf_op jit(solution)/shard_map/cond/branch_0_fun/ppermute | solution.py:469
  210.9 1.8 collective-permute-start.1

commit v9 on v8

--- a/solution.py
+++ b/solution.py
@@ -108,26 +108,36 @@
         pre_ref[b * per : (b + 1) * per, :] = pre_block(block, w_in, w_out)
 
 
-def own_kernel(rows_ref, w_in_ref, w_out_ref, pre_ref, xt_ref):
+def own_kernel(rows_ref, w_in_ref, w_out_ref, pre_ref, xt_ref, w_in_buf, w_out_buf, sems):
+    tile = pre_ref.shape[1]
+    gets = [
+        pltpu.make_async_copy(w_in_ref.at[:, pl.ds(0, tile)], w_in_buf, sems.at[0]),
+        pltpu.make_async_copy(w_out_ref.at[pl.ds(0, tile), :], w_out_buf, sems.at[1]),
+    ]
+    for get in gets:
+        get.start()
     xt_ref[...] = rows_ref[:, : xt_ref.shape[0]].T
-    pre_ref[...] = pre_block(rows_ref, w_in_ref[...], w_out_ref[...])
+    for get in gets:
+        get.wait()
+    pre_ref[...] = pre_block(rows_ref, w_in_buf[...], w_out_buf[...])
 
 
 def own_step(rows, w_in, w_out, tile):
     per, width = rows.shape[0], rows.shape[1] // 2
-    corner = lambda i: (0, 0)
+    vmem = pl.BlockSpec(memory_space=pltpu.VMEM)
+    anywhere = pl.BlockSpec(memory_space=pl.ANY)
     return pl.pallas_call(
         own_kernel,
-        grid=(1,),
-        in_specs=[
-            pl.BlockSpec(rows.shape, corner),
-            pl.BlockSpec((width, tile), corner),
-            pl.BlockSpec((tile, width), corner),
-        ],
-        out_specs=[pl.BlockSpec((per, tile), corner), pl.BlockSpec((width, per), corner)],
+        in_specs=[vmem, anywhere, anywhere],
+        out_specs=[vmem, vmem],
         out_shape=[
             jax.ShapeDtypeStruct((per, tile), bf16),
             jax.ShapeDtypeStruct((width, per), bf16),
+        ],
+        scratch_shapes=[
+            pltpu.VMEM((width, tile), bf16),
+            pltpu.VMEM((tile, width), bf16),
+            pltpu.SemaphoreType.DMA((2,)),
         ],
         compiler_params=pltpu.CompilerParams(vmem_limit_bytes=48 * MIB),
         cost_estimate=pl.CostEstimate(
@@ -142,29 +152,35 @@
     pre_own, xt_own, w_in_ref, w_out_ref, m_ref, v_ref, adam_ref, pre_ref, xt_ref = refs[
         others : others + 9
     ]
-    m_buf, v_buf, pre_buf, xt_buf, sems = refs[others + 9 :]
+    w_in_buf, w_out_buf, m_buf, v_buf, pre_buf, xt_buf, sems = refs[others + 9 :]
     width, tile = m_buf.shape
     per = xt_own.shape[1]
     gets = [
-        pltpu.make_async_copy(array.at[:, pl.ds(0, tile)], buf, sems.at[n])
-        for n, (array, buf) in enumerate(((m_ref, m_buf), (v_ref, v_buf)))
+        pltpu.make_async_copy(w_in_ref.at[:, pl.ds(0, tile)], w_in_buf, sems.at[0]),
+        pltpu.make_async_copy(w_out_ref.at[pl.ds(0, tile), :], w_out_buf, sems.at[1]),
+        pltpu.make_async_copy(m_ref.at[:, pl.ds(0, tile)], m_buf, sems.at[2]),
+        pltpu.make_async_copy(v_ref.at[:, pl.ds(0, tile)], v_buf, sems.at[3]),
     ]
     for get in gets:
         get.start()
     xt_buf[:, :per] = xt_own[...]
     pre_buf[:per, :] = pre_own[...]
     for b in range(others):
-        part = slice((b + 1) * per, (b + 2) * per)
-        xt_buf[:, part] = rows[b][:, :width].T
-        pre_buf[part, :] = pre_block(rows[b], w_in_ref[...], w_out_ref[...])
+        xt_buf[:, (b + 1) * per : (b + 2) * per] = rows[b][:, :width].T
+    for get in gets[:2]:
+        get.wait()
+    for b in range(others):
+        pre_buf[(b + 1) * per : (b + 2) * per, :] = pre_block(
+            rows[b], w_in_buf[...], w_out_buf[...]
+        )
     puts = [
-        pltpu.make_async_copy(xt_buf, xt_ref, sems.at[2]),
-        pltpu.make_async_copy(pre_buf, pre_ref, sems.at[3]),
+        pltpu.make_async_copy(xt_buf, xt_ref, sems.at[4]),
+        pltpu.make_async_copy(pre_buf, pre_ref, sems.at[5]),
     ]
     for put in puts:
         put.start()
     weight_grad = mxu(xt_buf[...], pre_buf[...], NN)
-    for get in gets:
+    for get in gets[2:]:
         get.wait()
     adam_ref[...] = adam_step(weight_grad, m_buf[...], v_buf[...])
     for put in puts:
@@ -174,32 +190,25 @@
 def first_step(rows, pre_own, xt_own, w_in, w_out, first_moment, second_moment, tile):
     width, per = xt_own.shape
     total = (len(rows) + 1) * per
-    corner = lambda i: (0, 0)
+    vmem = pl.BlockSpec(memory_space=pltpu.VMEM)
     anywhere = pl.BlockSpec(memory_space=pl.ANY)
     return pl.pallas_call(
         functools.partial(first_kernel, len(rows)),
-        grid=(1,),
-        in_specs=[pl.BlockSpec(r.shape, corner) for r in rows]
-        + [
-            pl.BlockSpec((per, tile), corner),
-            pl.BlockSpec((width, per), corner),
-            pl.BlockSpec((width, tile), corner),
-            pl.BlockSpec((tile, width), corner),
-            anywhere,
-            anywhere,
-        ],
-        out_specs=[pl.BlockSpec((width, tile), corner), anywhere, anywhere],
+        in_specs=[vmem] * (len(rows) + 2) + [anywhere] * 4,
+        out_specs=[vmem, anywhere, anywhere],
         out_shape=[
             jax.ShapeDtypeStruct((width, tile), bf16),
             jax.ShapeDtypeStruct((total, tile), bf16),
             jax.ShapeDtypeStruct((width, total), bf16),
         ],
         scratch_shapes=[
+            pltpu.VMEM((width, tile), bf16),
+            pltpu.VMEM((tile, width), bf16),
             pltpu.VMEM((width, tile), f32),
             pltpu.VMEM((width, tile), f32),
             pltpu.VMEM((total, tile), bf16),
             pltpu.VMEM((width, total), bf16),
-            pltpu.SemaphoreType.DMA((4,)),
+            pltpu.SemaphoreType.DMA((6,)),
         ],
         compiler_params=pltpu.CompilerParams(vmem_limit_bytes=56 * MIB),
         cost_estimate=pl.CostEstimate(

time: 217 us -> 215 us (level)
  transfers between devices with their start and end apart: 10 -> 10, of which waited for: 5 -> 4; matrix products, arithmetic and copies ran while one was open for 1% -> 1% of each run, Pallas kernels for 9% -> 9%
where the time goes in v9:
time: 215 us; the launch traced here: 214 us
  waiting for transfers between devices  94.8 us (44%)
  blocking collectives  47.6 us (22%)
  Pallas kernels  44 us (20%)
  starting transfers between devices  18.5 us (9%)
  between operations  5.08 us (2%)
  other arithmetic  3.08 us (1%)
    ppermute x2, waiting for transfers between devices, run(): lax.ppermute(near, 'expert', pairs)  70 us
    all_to_all x1, blocking collectives, shards(): lax.all_to_all(rows.reshape(expert_count, capacity, 2 * width), 'expert',...  47.6 us
    all_to_all x1, waiting for transfers between devices, shards(): lax.all_to_all(total.astype(bf16).reshape(expert_count, capacity, width),...  20.6 us
    pallas_call x3, Pallas kernels, adam_block(): pl.pallas_call(adam_kernel, grid=(tiles,), in_specs=[pl.BlockSpec((rows,...  15.8 us
    pallas_call x1, Pallas kernels, rest_step(): pl.pallas_call(functools.partial(rest_kernel, len(rows)), grid=(tiles,),...  13.2 us
    all_to_all x1, starting transfers between devices, shards(): lax.all_to_all(total.astype(bf16).reshape(expert_count, capacity, width),...  6.27 us
    ppermute x2, starting transfers between devices, run(): lax.ppermute(near, 'expert', pairs)  5.44 us
  transfers between devices with their start and end apart: 10, of which 4 were waited for; matrix products, arithmetic and copies ran while one was open for 1% of the time, Pallas kernels for 9%

profile of v9, /device:TPU:6, one launch (start us, length us, event | category | flops | bytes accessed | tf_op | source)
XLA Modules:
  0.0 214.2 jit_solution(17113229015231591172)
XLA Ops:
  0.6 3.1 %pack_rows.1 = (bf16[384,2304]{1,0:T(8,128)(2,1)}, s32[2,128]{1,0:T(2,128)}) custom-call(s32[2,128]{1,0:T(2,128)} %bitcast.34, f32[2,128]{1,0:T(2,128)} %bitcast.35, bf16[128,1152]{1,0:T(8,128)(2,1)} %x_ref.1, bf16[128,1152]{1,0:T(8,128)(2,1)} %g_ref.1), custom_call_target="tpu_custom_call" | custom-call | tf_op jit(solution)/shard_map/pack_rows/pallas_call | solution.py:88
  3.7 47.6 %all_to_all.10 = bf16[16,24,2304]{2,1,0:T(8,128)(2,1)S(1)} all-to-all(bf16[16,24,2304]{2,1,0:T(8,128)(2,1)} %bitcast.33), channel_id=1, replica_groups=mesh['dp'=2,'expert'=16] {'expert'}, dimensions={0} | all-to-all | bytes 3538944 | tf_op jit(solution)/shard_map/all_to_all | solution.py:418
  51.3 2.0 own_step.1
  53.3 1.6 collective-permute-done.28.refs_0_.refs_1_
  55.0 4.2 %first_step.1 = (bf16[1152,256]{1,0:T(8,128)(2,1)}, bf16[768,256]{1,0:T(8,128)(2,1)}, bf16[1152,768]{1,0:T(8,128)(2,1)}) custom-call(bf16[384,2304]{1,0:T(8,128)(2,1)S(1)} %collective-permute-done.28.refs_0_.refs_1_, bf16[384,256]{1,0:T(8,128)(2,1)S(1)} %get-tuple-element.104.refs_1_, bf16[1152,384]{1,0:T(8,128)(2,1)S(1)} %get-tuple-element.105.refs_2_, ...), custom_call_target="tpu_custom_call" | custom-call | flops 1358954496 | bytes 4128768 | tf_op jit(solution)/shard_map/first_step/pallas_call | solution.py:195
  59.1 13.2 %rest_step.1 = (bf16[768,1280]{1,0:T(8,128)(2,1)}, bf16[384,1152]{1,0:T(8,128)(2,1)}, bf16[384,1152]{1,0:T(8,128)(2,1)}) custom-call(bf16[384,2304]{1,0:T(8,128)(2,1)S(1)} %bitcast.16, bf16[384,2304]{1,0:T(8,128)(2,1)S(1)} %collective-permute-done.28.refs_0_.refs_1_, bf16[768,256]{1,0:T(8,128)(2,1)} %get-tuple-element.107.refs_2_, ...), custom_call_target="tpu_custom_call" | custom-call | flops 6794772480 | bytes 5898240 | tf_op jit(solution)/shard_map/rest_step/pallas_call | solution.py:247
  72.4 0.1 collective-permute-start.30
  72.5 2.5 %collective-permute-done.30 = bf16[384,1152]{1,0:T(8,128)(2,1)S(1)} collective-permute-done((bf16[384,1152]{1,0:T(8,128)(2,1)}, bf16[384,1152]{1,0:T(8,128)(2,1)S(1)}, u32[]{:S(2)}, u32[]{:S(2)}) %collective-permute-start.30) | collective-permute-done | bytes 884768 | tf_op jit(solution)/shard_map/ppermute | solution.py:398
  75.0 2.4 %add_convert_fusion = bf16[384,1152]{1,0:T(8,128)(2,1)} fusion(bf16[384,1152]{1,0:T(8,128)(2,1)S(1)} %collective-permute-done.30, bf16[384,1152]{1,0:T(8,128)(2,1)} %get-tuple-element.110), kind=kLoop, calls=%fused_computation | loop fusion | flops 1769472 | bytes 2654208 | tf_op jit(solution)/shard_map/convert_element_type | solution.py:450
  77.4 6.3 %all-to-all-start.1 = ((bf16[16,24,1152]{2,1,0:T(8,128)(2,1)}), bf16[16,24,1152]{2,1,0:T(8,128)(2,1)}, u32[]{:S(2)}, u32[]{:S(2)}) async-start(bf16[16,24,1152]{2,1,0:T(8,128)(2,1)} %bitcast.8), calls=%async_computation.1 | async-start | bytes 1769472 | tf_op jit(solution)/shard_map/all_to_all | solution.py:449
  83.7 5.8 %shard_map.137.refs_7_ = bf16[576,1024]{1,0:T(8,128)(2,1)} custom-call(bf16[1152,768]{1,0:T(8,128)(2,1)} %get-tuple-element.106.xt_ref, bf16[768,1280]{1,0:T(8,128)(2,1)} %get-tuple-element.108.pre_ref, f32[1152,1536]{1,0:T(8,128)} %bitcast.18, f32[1152,1536]{1,0:T(8,128)} %bitcast.22), custom_call_target="tpu_custom_call" | custom-call | flops 905969664 | bytes 5898240 | tf_op jit(solution)/shard_map/pallas_call | solution.py:281
  89.5 0.0 copy-start.6
  89.5 0.0 copy-start.5
  89.5 0.6 collective-permute-start.29
  90.2 4.0 %shard_map.138.refs_2_ = bf16[1152,256]{1,0:T(8,128)(2,1)} custom-call(bf16[1152,768]{1,0:T(8,128)(2,1)} %get-tuple-element.106.xt_ref, bf16[768,1280]{1,0:T(8,128)(2,1)} %get-tuple-element.108.pre_ref, f32[1152,1536]{1,0:T(8,128)} %bitcast.19, f32[1152,1536]{1,0:T(8,128)} %bitcast.23), custom_call_target="tpu_custom_call" | custom-call | flops 452984832 | bytes 2949120 | tf_op jit(solution)/shard_map/pallas_call | solution.py:281
  94.2 2.4 %collective-permute-start.32 = (bf16[1152,256]{1,0:T(8,128)(2,1)}, bf16[1152,256]{1,0:T(8,128)(2,1)S(1)}, u32[]{:S(2)}, u32[]{:S(2)}) collective-permute-start(bf16[1152,256]{1,0:T(8,128)(2,1)} %shard_map.138.refs_2_), channel_id=1, source_target_pairs={{0,8},{1,9},{2,10},{3,11},{4,12},{5,13},{6,14},{7,15},{8,0},{9,1},... | collective-permute-start | bytes 1769480 | tf_op jit(solution)/shard_map/ppermute | solution.py:462
  96.6 0.5 collective-permute-start.31
  97.1 0.7 fusion.2
  100.3 0.6 dynamic_slice.7
  100.9 0.6 dynamic_slice.6
  103.3 5.9 %shard_map.136.refs_4_ = bf16[576,1024]{1,0:T(8,128)(2,1)} custom-call(bf16[1152,768]{1,0:T(8,128)(2,1)} %get-tuple-element.106.xt_ref, bf16[768,1280]{1,0:T(8,128)(2,1)} %get-tuple-element.108.pre_ref, f32[1152,1536]{1,0:T(8,128)} %bitcast.20, f32[1152,1536]{1,0:T(8,128)} %bitcast.24), custom_call_target="tpu_custom_call" | custom-call | flops 905969664 | bytes 5898240 | tf_op jit(solution)/shard_map/pallas_call | solution.py:281
  109.3 20.6 %all-to-all-done.1 = bf16[16,24,1152]{2,1,0:T(8,128)(2,1)} async-done(((bf16[16,24,1152]{2,1,0:T(8,128)(2,1)}), bf16[16,24,1152]{2,1,0:T(8,128)(2,1)}, u32[]{:S(2)}, u32[]{:S(2)}) %all-to-all-start.1) | async-done | bytes 884768 | tf_op jit(solution)/shard_map/all_to_all | solution.py:449
  129.9 2.3 %combine_rows.1 = bf16[128,1152]{1,0:T(8,128)(2,1)} custom-call(s32[2,128]{1,0:T(2,128)} %get-tuple-element.109.where_ref, bf16[384,1152]{1,0:T(8,128)(2,1)} %bitcast.9.back_ref), custom_call_target="tpu_custom_call" | custom-call | tf_op jit(solution)/shard_map/combine_rows/pallas_call | solution.py:389
  132.1 75.1 %conditional.3 = (bf16[576,1024]{1,0:T(8,128)(2,1)}, bf16[576,1024]{1,0:T(8,128)(2,1)}) conditional(s32[]{:T(128)} %bitcast.12, (bf16[576,1024]{1,0:T(8,128)(2,1)}, bf16[576,1024]{1,0:T(8,128)(2,1)}) %tuple.66, (bf16[576,1024]{1,0:T(8,128)(2,1)}, bf16[576,1024]{1,0:T(8,128)(2,1)}) %tuple.66, ...), branch_computations={%region_10.11_spmd, %region_11.12_spmd, %region_12.13_spmd, %regio... | conditional | bytes 9437280 | solution.py:488
  132.1 3.8 %collective-permute-start.16 = (bf16[576,1024]{1,0:T(8,128)(2,1)}, bf16[576,1024]{1,0:T(8,128)(2,1)}, u32[]{:S(2)}, u32[]{:S(2)}) collective-permute-start(bf16[576,1024]{1,0:T(8,128)(2,1)} %get-tuple-element.72), channel_id=1, source_target_pairs={{3,11},{11,3},{7,15},{15,7},{19,27},{27,19},{23,31},{31,23}} | collective-permute-start | bytes 3538952 | tf_op jit(solution)/shard_map/cond/branch_1_fun/ppermute | solution.py:478
  135.9 1.3 collective-permute-start.17
  137.2 70.0 %collective-permute-done.16 = bf16[576,1024]{1,0:T(8,128)(2,1)} collective-permute-done((bf16[576,1024]{1,0:T(8,128)(2,1)}, bf16[576,1024]{1,0:T(8,128)(2,1)}, u32[]{:S(2)}, u32[]{:S(2)}) %collective-permute-start.16) | collective-permute-done | bytes 1179680 | tf_op jit(solution)/shard_map/cond/branch_1_fun/ppermute | solution.py:478
  207.2 0.0 collective-permute-done.17
  207.3 3.4 %conditional.2 = (bf16[576,1024]{1,0:T(8,128)(2,1)}, bf16[576,1024]{1,0:T(8,128)(2,1)}) conditional(s32[]{:T(128)} %bitcast.11, (bf16[576,1024]{1,0:T(8,128)(2,1)}, bf16[576,1024]{1,0:T(8,128)(2,1)}) %tuple.66, (bf16[576,1024]{1,0:T(8,128)(2,1)}, bf16[576,1024]{1,0:T(8,128)(2,1)}) %tuple.66, ...), branch_computations={%region_3.4_spmd, %region_4.5_spmd, %region_5.6_spmd, %region_6.7_... | conditional | bytes 9437280 | solution.py:488
  207.3 1.7 collective-permute-start
  208.9 1.8 collective-permute-start.1
  210.8 3.4 %place.1 = bf16[1152,1536]{1,0:T(8,128)(2,1)} custom-call(s32[1]{0:T(128)} %bitcast.10.source_ref, bf16[1152,256]{1,0:T(8,128)(2,1)S(1)} %copy-done.2, bf16[1152,256]{1,0:T(8,128)(2,1)S(1)} %collective-permute-done.31.refs_1_, bf16[1152,256]{1,0:T(8,128)(2,1)S(1)} %copy-done.1, bf16[1152,256]{1,0:T(8,128)(2,1)S(1)} %collective-permute-done.32.refs_3_, ...), custom_call_target="tpu_custom_call" | custom-call | bytes 7077888 | tf_op jit(solution)/shard_map/place/pallas_call | solution.py:338
  (18 shorter events, 0.0 us)
Async XLA Ops:
  51.3 3.7 %collective-permute-start.28 = (bf16[384,2304]{1,0:T(8,128)(2,1)S(1)}, bf16[384,2304]{1,0:T(8,128)(2,1)S(1)}, u32[]{:S(2)}, u32[]{:S(2)}) collective-permute-start(bf16[384,2304]{1,0:T(8,128)(2,1)S(1)} %bitcast.14), channel_id=1, source_target_pairs={{0,16},{16,0},{1,17},{17,1},{2,18},{18,2},{3,19},{19,3},{4,20},{20... | collective-permute-start | bytes 5308424 | tf_op jit(solution)/shard_map/ppermute | solution.py:398
  72.4 2.6 %collective-permute-start.30 = (bf16[384,1152]{1,0:T(8,128)(2,1)}, bf16[384,1152]{1,0:T(8,128)(2,1)S(1)}, u32[]{:S(2)}, u32[]{:S(2)}) collective-permute-start(bf16[384,1152]{1,0:T(8,128)(2,1)} %get-tuple-element.111), channel_id=1, source_target_pairs={{0,16},{16,0},{1,17},{17,1},{2,18},{18,2},{3,19},{19,3},{4,20},{20... | collective-permute-start | bytes 2654216 | tf_op jit(solution)/shard_map/ppermute | solution.py:398
  77.4 52.5 %all-to-all-start.1 = ((bf16[16,24,1152]{2,1,0:T(8,128)(2,1)}), bf16[16,24,1152]{2,1,0:T(8,128)(2,1)}, u32[]{:S(2)}, u32[]{:S(2)}) async-start(bf16[16,24,1152]{2,1,0:T(8,128)(2,1)} %bitcast.8), calls=%async_computation.1 | async-start | bytes 1769472 | tf_op jit(solution)/shard_map/all_to_all | solution.py:449
  89.5 7.1 %copy-start.2 = (bf16[1152,256]{1,0:T(8,128)(2,1)S(1)}, bf16[1152,256]{1,0:T(8,128)(2,1)}, u32[]{:S(2)}) copy-start(bf16[1152,256]{1,0:T(8,128)(2,1)} %get-tuple-element.113.refs_0_) | copy-start | bytes 1769476
  89.5 7.6 %copy-start.3 = (s32[16]{0:T(128)S(1)}, s32[16]{0:T(128)}, u32[]{:S(2)}) copy-start(s32[16]{0:T(128)} %param.30) | copy-start | bytes 196
  89.5 7.6 %copy-start.4 = (pred[16]{0:T(512)(128)(4,1)S(1)}, pred[16]{0:T(512)(128)(4,1)}, u32[]{:S(2)}) copy-start(pred[16]{0:T(512)(128)(4,1)} %constant.32.clone) | copy-start | bytes 52
  89.5 10.8 %copy-start.6 = (s32[256]{0:T(256)S(1)}, s32[256]{0:T(256)}, u32[]{:S(2)}) copy-start(s32[256]{0:T(256)} %constant.31.clone) | copy-start | bytes 3076
  89.5 11.4 %copy-start.5 = (s32[256]{0:T(256)S(1)}, s32[256]{0:T(256)}, u32[]{:S(2)}) copy-start(s32[256]{0:T(256)} %constant.30.clone) | copy-start | bytes 3076
  89.5 42.6 %collective-permute-start.29 = (bf16[576,1024]{1,0:T(8,128)(2,1)}, bf16[576,1024]{1,0:T(8,128)(2,1)}, u32[]{:S(2)}, u32[]{:S(2)}) collective-permute-start(bf16[576,1024]{1,0:T(8,128)(2,1)} %shard_map.137.refs_7_), channel_id=1, source_target_pairs={{0,1},{1,0},{2,3},{3,2},{4,5},{5,4},{6,7},{7,6},{8,9},{9,8},{10,11... | collective-permute-start | bytes 3538952 | tf_op jit(solution)/shard_map/ppermute | solution.py:469
  94.2 116.6 %collective-permute-start.32 = (bf16[1152,256]{1,0:T(8,128)(2,1)}, bf16[1152,256]{1,0:T(8,128)(2,1)S(1)}, u32[]{:S(2)}, u32[]{:S(2)}) collective-permute-start(bf16[1152,256]{1,0:T(8,128)(2,1)} %shard_map.138.refs_2_), channel_id=1, source_target_pairs={{0,8},{1,9},{2,10},{3,11},{4,12},{5,13},{6,14},{7,15},{8,0},{9,1},... | collective-permute-start | bytes 1769480 | tf_op jit(solution)/shard_map/ppermute | solution.py:462
  96.6 114.1 %collective-permute-start.31 = (bf16[1152,256]{1,0:T(8,128)(2,1)S(1)}, bf16[1152,256]{1,0:T(8,128)(2,1)S(1)}, u32[]{:S(2)}, u32[]{:S(2)}) collective-permute-start(bf16[1152,256]{1,0:T(8,128)(2,1)S(1)} %copy-done.2), channel_id=1, source_target_pairs={{0,8},{1,9},{2,10},{3,11},{4,12},{5,13},{6,14},{7,15},{8,0},{9,1},... | collective-permute-start | bytes 1769480 | tf_op jit(solution)/shard_map/ppermute | solution.py:442
  103.3 107.4 %copy-start.1 = (bf16[1152,256]{1,0:T(8,128)(2,1)S(1)}, bf16[1152,256]{1,0:T(8,128)(2,1)}, u32[]{:S(2)}) copy-start(bf16[1152,256]{1,0:T(8,128)(2,1)} %shard_map.138.refs_2_) | copy-start | bytes 1769476
  109.3 101.5 %copy-start = (bf16[576,1024]{1,0:T(8,128)(2,1)S(1)}, bf16[576,1024]{1,0:T(8,128)(2,1)}, u32[]{:S(2)}) copy-start(bf16[576,1024]{1,0:T(8,128)(2,1)} %shard_map.137.refs_7_) | copy-start | bytes 3538948
  132.1 75.1 %collective-permute-start.16 = (bf16[576,1024]{1,0:T(8,128)(2,1)}, bf16[576,1024]{1,0:T(8,128)(2,1)}, u32[]{:S(2)}, u32[]{:S(2)}) collective-permute-start(bf16[576,1024]{1,0:T(8,128)(2,1)} %get-tuple-element.72), channel_id=1, source_target_pairs={{3,11},{11,3},{7,15},{15,7},{19,27},{27,19},{23,31},{31,23}} | collective-permute-start | bytes 3538952 | tf_op jit(solution)/shard_map/cond/branch_1_fun/ppermute | solution.py:478
  135.9 71.4 %collective-permute-start.17 = (bf16[576,1024]{1,0:T(8,128)(2,1)}, bf16[576,1024]{1,0:T(8,128)(2,1)}, u32[]{:S(2)}, u32[]{:S(2)}) collective-permute-start(bf16[576,1024]{1,0:T(8,128)(2,1)} %get-tuple-element.73), channel_id=1, source_target_pairs={{2,11},{10,3},{6,15},{14,7},{18,27},{26,19},{22,31},{30,23}} | collective-permute-start | bytes 3538952 | tf_op jit(solution)/shard_map/cond/branch_1_fun/ppermute | solution.py:479
  207.3 3.4 %collective-permute-start = (bf16[576,1024]{1,0:T(8,128)(2,1)}, bf16[576,1024]{1,0:T(8,128)(2,1)}, u32[]{:S(2)}, u32[]{:S(2)}) collective-permute-start(bf16[576,1024]{1,0:T(8,128)(2,1)} %get-tuple-element.56), channel_id=1, source_target_pairs={{0,8},{8,0},{1,9},{9,1},{16,24},{24,16},{17,25},{25,17}} | collective-permute-start | bytes 3538952 | tf_op jit(solution)/shard_map/cond/branch_0_fun/ppermute | solution.py:478
  208.9 1.8 collective-permute-start.1

commit v10 on v9

--- a/solution.py
+++ b/solution.py
@@ -377,20 +377,38 @@
     return switches
 
 
-def combine_kernel(where_ref, back_ref, out_ref):
-    slots, tok_count = back_ref.shape[0], out_ref.shape[0]
-    row = lax.broadcasted_iota(jnp.int32, (slots, tok_count), 0)
-    pick = (row == where_ref[0:1, :]) | (row == where_ref[1:2, :])
-    pick = jnp.where(pick, 1.0, 0.0).astype(bf16)
-    out_ref[...] = mxu(pick, back_ref[...], TN).astype(bf16)
-
-
-def combine_rows(where_to, returned, tok_count):
-    return pl.pallas_call(
-        combine_kernel,
-        out_shape=jax.ShapeDtypeStruct((tok_count, returned.shape[1]), bf16),
+def combine_kernel(capacity, half, upper_ref, where_ref, mirror_ref, back_ref, own_ref, sum_ref):
+    slots, tok_count = back_ref.shape[0], own_ref.shape[0]
+    row = lax.broadcasted_iota(jnp.int32, (slots, tok_count), 0).astype(f32)
+    block = jnp.floor((row + 0.5) * (1.0 / capacity))
+    expert = jnp.floor(block * 0.5)
+    side = block - 2.0 * expert
+    upper = upper_ref[0].astype(f32)
+    place_of = (expert + half * upper) * capacity + (row - block * capacity)
+    for ref, out, wanted in ((where_ref, own_ref, upper), (mirror_ref, sum_ref, 1.0 - upper)):
+        first, second = ref[0:1, :].astype(f32), ref[1:2, :].astype(f32)
+        hit = ((place_of == first) | (place_of == second)) & (side == wanted)
+        pick = jnp.where(hit, 1.0, 0.0).astype(bf16)
+        out[...] = mxu(pick, back_ref[...], TN).astype(out.dtype)
+
+
+def combine_rows(upper, where_to, mirror_to, returned, tok_count, capacity, half):
+    width = returned.shape[1]
+    vmem = pl.BlockSpec(memory_space=pltpu.VMEM)
+    return pl.pallas_call(
+        functools.partial(combine_kernel, capacity, half),
+        in_specs=[pl.BlockSpec(memory_space=pltpu.SMEM), vmem, vmem, vmem],
+        out_shape=(
+            jax.ShapeDtypeStruct((tok_count, width), bf16),
+            jax.ShapeDtypeStruct((tok_count, width), bf16),
+        ),
+        cost_estimate=pl.CostEstimate(
+            flops=4 * tok_count * returned.shape[0] * width,
+            bytes_accessed=2 * returned.size + 6 * tok_count * width,
+            transcendentals=0,
+        ),
         name="combine_rows",
-    )(where_to, returned)
+    )(upper, where_to, mirror_to, returned)
 
 
 def dp_shift(block, apart):
@@ -446,15 +464,21 @@
     total = parts[0].astype(f32)
     for d in range(1, dp_count):
         total = total + dp_shift(parts[d], d).astype(f32)
+    total = total.astype(bf16).reshape(2, half, capacity, width).transpose(1, 0, 2, 3)
     returned = lax.all_to_all(
-        total.astype(bf16).reshape(expert_count, capacity, width),
+        total.reshape(half, 2 * capacity, width),
         "expert",
         split_axis=0,
         concat_axis=0,
+        axis_index_groups=[list(range(half)), list(range(half, expert_count))],
         tiled=True,
     ).reshape(slots, width)
-
-    x_grad = combine_rows(where_to, returned, tok_count)
+    upper = (own_index >= half).astype(jnp.int32).reshape(1)
+    mirror_to = lax.ppermute(where_to, "expert", route)
+    own_sum, mirror_sum = combine_rows(
+        upper, where_to, mirror_to, returned, tok_count, capacity, half
+    )
+    other_sum = lax.ppermute(mirror_sum, "expert", route)
     switches = swap_plans(half) if tiles > 2 else []
     direct = 1 if switches else tiles - 1
     moments = (first_moment[0], second_moment[0])
@@ -481,7 +505,7 @@
 
             return run
 
-        near, lent, x_grad = lax.optimization_barrier((near, lent, x_grad))
+        near, lent, own_sum = lax.optimization_barrier((near, lent, own_sum))
         near_all, far_all = [near], [far]
         for n, (plans, table) in enumerate(switches):
             choice = jnp.asarray(table, jnp.int32)[moved_mask]
@@ -491,6 +515,7 @@
             members = {e for plan in plans for p in plan for e in (p, p ^ half)}
             here = jnp.asarray([e in members for e in range(expert_count)])
             group += jnp.sum(jnp.where(here & (lane_ids == own_index), n, 0))
+        far_all[-1], own_sum = lax.optimization_barrier((far_all[-1], own_sum))
         wide = left * tile
         pieces.append((0, at * tile, width // 2, wide, near_all))
         pieces.append((width // 2, at * tile, width // 2, wide, far_all))
@@ -502,6 +527,7 @@
         for at in range(0, high, step):
             cut.append((row, col, at, min(step, high - at), wide, arrays))
     adam_out = place(source, cut, width, inner)
+    x_grad = (own_sum.astype(f32) + other_sum.astype(f32)).astype(bf16)
     return (x_grad, adam_out[None])
 
 

time: 215 us -> 232 us (1.079)
  the two profiles are of different devices: /device:TPU:6 before, /device:TPU:7 now
where the time goes in v10:
time: 232 us
  waiting for transfers between devices  110 us (47%)
  blocking collectives  46.3 us (20%)
  Pallas kernels  44.2 us (19%)
  starting transfers between devices  19.6 us (8%)
  between operations  4.95 us (2%)
  other arithmetic  3.76 us (2%)
  local copies, waits for them, and re-layouts  3.22 us (1%)
    ppermute x1, waiting for transfers between devices, shards(): mirror_to = lax.ppermute(where_to, 'expert', route)  50.7 us
    ppermute x2, waiting for transfers between devices, run(): lax.ppermute(near, 'expert', pairs)  48.9 us
    all_to_all x1, blocking collectives, shards(): lax.all_to_all(rows.reshape(expert_count, capacity, 2 * width), 'expert',...  46.3 us
    pallas_call x3, Pallas kernels, adam_block(): pl.pallas_call(adam_kernel, grid=(tiles,), in_specs=[pl.BlockSpec((rows,...  15.9 us
    pallas_call x1, Pallas kernels, rest_step(): pl.pallas_call(functools.partial(rest_kernel, len(rows)), grid=(tiles,),...  13.2 us
    ppermute x2, waiting for transfers between devices, run(): lax.ppermute(lent, 'expert', skew)  6.58 us
    ppermute x2, starting transfers between devices, run(): lax.ppermute(near, 'expert', pairs)  6.05 us
    all_to_all x1, starting transfers between devices, shards(): lax.all_to_all(total.reshape(half, 2 * capacity, width), 'expert', split_...  5.39 us
  transfers between devices with their start and end apart: 12, of which 5 were waited for; matrix products, arithmetic and copies ran while one was open for 1% of the time, Pallas kernels for 10%

profile of v10, /device:TPU:7, one launch (start us, length us, event | category | flops | bytes accessed | tf_op | source)
XLA Modules:
  0.0 231.7 jit_solution(119520985441314106)
XLA Ops:
  0.6 3.1 %pack_rows.1 = (bf16[384,2304]{1,0:T(8,128)(2,1)}, s32[2,128]{1,0:T(2,128)}) custom-call(s32[2,128]{1,0:T(2,128)} %bitcast.40, f32[2,128]{1,0:T(2,128)} %bitcast.41, bf16[128,1152]{1,0:T(8,128)(2,1)} %x_ref.1, bf16[128,1152]{1,0:T(8,128)(2,1)} %g_ref.1), custom_call_target="tpu_custom_call" | custom-call | tf_op jit(solution)/shard_map/pack_rows/pallas_call | solution.py:88
  3.7 46.3 %all_to_all.10 = bf16[16,24,2304]{2,1,0:T(8,128)(2,1)S(1)} all-to-all(bf16[16,24,2304]{2,1,0:T(8,128)(2,1)} %bitcast.39), channel_id=1, replica_groups=mesh['dp'=2,'expert'=16] {'expert'}, dimensions={0} | all-to-all | bytes 3538944 | tf_op jit(solution)/shard_map/all_to_all | solution.py:436
  50.0 2.0 collective-permute-start.28
  52.0 2.0 own_step.1
  54.0 1.3 collective-permute-done.28.refs_0_.refs_1_
  55.3 4.1 %first_step.1 = (bf16[1152,256]{1,0:T(8,128)(2,1)}, bf16[768,256]{1,0:T(8,128)(2,1)}, bf16[1152,768]{1,0:T(8,128)(2,1)}) custom-call(bf16[384,2304]{1,0:T(8,128)(2,1)S(1)} %collective-permute-done.28.refs_0_.refs_1_, bf16[384,256]{1,0:T(8,128)(2,1)S(1)} %get-tuple-element.108.refs_1_, bf16[1152,384]{1,0:T(8,128)(2,1)S(1)} %get-tuple-element.109.refs_2_, ...), custom_call_target="tpu_custom_call" | custom-call | flops 1358954496 | bytes 4128768 | tf_op jit(solution)/shard_map/first_step/pallas_call | solution.py:195
  59.4 13.2 %rest_step.1 = (bf16[768,1280]{1,0:T(8,128)(2,1)}, bf16[384,1152]{1,0:T(8,128)(2,1)}, bf16[384,1152]{1,0:T(8,128)(2,1)}) custom-call(bf16[384,2304]{1,0:T(8,128)(2,1)S(1)} %bitcast.20, bf16[384,2304]{1,0:T(8,128)(2,1)S(1)} %collective-permute-done.28.refs_0_.refs_1_, bf16[768,256]{1,0:T(8,128)(2,1)} %get-tuple-element.111.refs_2_, ...), custom_call_target="tpu_custom_call" | custom-call | flops 6794772480 | bytes 5898240 | tf_op jit(solution)/shard_map/rest_step/pallas_call | solution.py:247
  72.6 0.4 collective-permute-start.31
  73.0 2.3 collective-permute-done.31
  75.2 1.4 add_convert_fusion
  76.6 1.0 copy.14
  77.6 5.4 %all-to-all-start.1 = ((bf16[8,48,1152]{2,1,0:T(8,128)(2,1)}), bf16[8,48,1152]{2,1,0:T(8,128)(2,1)S(1)}, u32[]{:S(2)}, u32[]{:S(2)}) async-start(bf16[8,48,1152]{2,1,0:T(8,128)(2,1)} %bitcast.12), calls=%async_computation.1 | async-start | bytes 1769472 | tf_op jit(solution)/shard_map/all_to_all | solution.py:468
  83.0 5.9 %shard_map.137.refs_7_ = bf16[576,1024]{1,0:T(8,128)(2,1)} custom-call(bf16[1152,768]{1,0:T(8,128)(2,1)} %get-tuple-element.110.xt_ref, bf16[768,1280]{1,0:T(8,128)(2,1)} %get-tuple-element.112.pre_ref, f32[1152,1536]{1,0:T(8,128)} %bitcast.22, f32[1152,1536]{1,0:T(8,128)} %bitcast.26), custom_call_target="tpu_custom_call" | custom-call | flops 905969664 | bytes 5898240 | tf_op jit(solution)/shard_map/pallas_call | solution.py:281
  89.3 4.0 %shard_map.138.refs_2_ = bf16[1152,256]{1,0:T(8,128)(2,1)} custom-call(bf16[1152,768]{1,0:T(8,128)(2,1)} %get-tuple-element.110.xt_ref, bf16[768,1280]{1,0:T(8,128)(2,1)} %get-tuple-element.112.pre_ref, f32[1152,1536]{1,0:T(8,128)} %bitcast.23, f32[1152,1536]{1,0:T(8,128)} %bitcast.27), custom_call_target="tpu_custom_call" | custom-call | flops 452984832 | bytes 2949120 | tf_op jit(solution)/shard_map/pallas_call | solution.py:281
  93.3 2.3 collective-permute-start.34
  95.7 50.7 %collective-permute-done.30.mirror_ref = s32[2,128]{1,0:T(2,128)S(1)} collective-permute-done((s32[2,128]{1,0:T(2,128)S(1)}, s32[2,128]{1,0:T(2,128)S(1)}, u32[]{:S(2)}, u32[]{:S(2)}) %collective-permute-start.30) | collective-permute-done | bytes 1056 | tf_op jit(solution)/shard_map/ppermute | solution.py:477
  146.4 0.6 copy-done.6
  147.4 2.5 %combine_rows.1 = (bf16[128,1152]{1,0:T(8,128)(2,1)}, bf16[128,1152]{1,0:T(8,128)(2,1)}) custom-call(s32[1]{0:T(128)} %bitcast.9.upper_ref, s32[2,128]{1,0:T(2,128)} %get-tuple-element.113.where_ref, s32[2,128]{1,0:T(2,128)} %copy-done.6, bf16[384,1152]{1,0:T(8,128)(2,1)} %bitcast.37), custom_call_target="tpu_custom_call" | custom-call | flops 226492416 | bytes 1769472 | tf_op jit(solution)/shard_map/combine_rows/pallas_call | solution.py:398
  149.9 0.6 fusion.1
  152.8 0.7 dynamic_slice.6
  153.5 0.6 dynamic_slice.7
  156.0 6.0 %shard_map.136.refs_4_ = bf16[576,1024]{1,0:T(8,128)(2,1)} custom-call(bf16[1152,768]{1,0:T(8,128)(2,1)} %get-tuple-element.110.xt_ref, bf16[768,1280]{1,0:T(8,128)(2,1)} %get-tuple-element.112.pre_ref, f32[1152,1536]{1,0:T(8,128)} %bitcast.24, f32[1152,1536]{1,0:T(8,128)} %bitcast.28), custom_call_target="tpu_custom_call" | custom-call | flops 905969664 | bytes 5898240 | tf_op jit(solution)/shard_map/pallas_call | solution.py:281
  162.0 61.0 %conditional.2 = (bf16[576,1024]{1,0:T(8,128)(2,1)}, bf16[576,1024]{1,0:T(8,128)(2,1)}) conditional(s32[]{:T(128)} %bitcast, (bf16[576,1024]{1,0:T(8,128)(2,1)}, bf16[576,1024]{1,0:T(8,128)(2,1)}) %tuple.67, (bf16[576,1024]{1,0:T(8,128)(2,1)}, bf16[576,1024]{1,0:T(8,128)(2,1)}) %tuple.67, ...), branch_computations={%region_1.2_spmd, %region_2.3_spmd, %region_3.4_spmd, %region_4.5_... | conditional | bytes 9437280 | solution.py:512
  162.0 4.3 %collective-permute-start.2 = (bf16[576,1024]{1,0:T(8,128)(2,1)}, bf16[576,1024]{1,0:T(8,128)(2,1)}, u32[]{:S(2)}, u32[]{:S(2)}) collective-permute-start(bf16[576,1024]{1,0:T(8,128)(2,1)} %get-tuple-element.58), channel_id=1, source_target_pairs={{3,11},{11,3},{7,15},{15,7},{19,27},{27,19},{23,31},{31,23}} | collective-permute-start | bytes 3538952 | tf_op jit(solution)/shard_map/cond/branch_1_fun/ppermute | solution.py:502
  166.3 1.3 collective-permute-start.3
  167.6 48.9 %collective-permute-done.2 = bf16[576,1024]{1,0:T(8,128)(2,1)} collective-permute-done((bf16[576,1024]{1,0:T(8,128)(2,1)}, bf16[576,1024]{1,0:T(8,128)(2,1)}, u32[]{:S(2)}, u32[]{:S(2)}) %collective-permute-start.2) | collective-permute-done | bytes 1179680 | tf_op jit(solution)/shard_map/cond/branch_1_fun/ppermute | solution.py:502
  216.4 6.6 %collective-permute-done.3 = bf16[576,1024]{1,0:T(8,128)(2,1)} collective-permute-done((bf16[576,1024]{1,0:T(8,128)(2,1)}, bf16[576,1024]{1,0:T(8,128)(2,1)}, u32[]{:S(2)}, u32[]{:S(2)}) %collective-permute-start.3) | collective-permute-done | bytes 1179680 | tf_op jit(solution)/shard_map/cond/branch_1_fun/ppermute | solution.py:503
  223.0 3.5 %conditional.3 = (bf16[576,1024]{1,0:T(8,128)(2,1)}, bf16[576,1024]{1,0:T(8,128)(2,1)}) conditional(s32[]{:T(128)} %bitcast.15, (bf16[576,1024]{1,0:T(8,128)(2,1)}, bf16[576,1024]{1,0:T(8,128)(2,1)}) %tuple.67, (bf16[576,1024]{1,0:T(8,128)(2,1)}, bf16[576,1024]{1,0:T(8,128)(2,1)}) %tuple.67, ...), branch_computations={%region_10.11_spmd, %region_11.12_spmd, %region_12.13_spmd, %regio... | conditional | bytes 9437280 | solution.py:512
  223.0 1.8 collective-permute-start.14
  224.8 1.7 collective-permute-start.15
  226.5 3.4 %place.1 = bf16[1152,1536]{1,0:T(8,128)(2,1)} custom-call(s32[1]{0:T(128)} %bitcast.14.source_ref, bf16[1152,256]{1,0:T(8,128)(2,1)S(1)} %copy-done.2, bf16[1152,256]{1,0:T(8,128)(2,1)S(1)} %collective-permute-done.33.refs_1_, bf16[1152,256]{1,0:T(8,128)(2,1)S(1)} %copy-done.1, bf16[1152,256]{1,0:T(8,128)(2,1)S(1)} %collective-permute-done.34.refs_3_, ...), custom_call_target="tpu_custom_call" | custom-call | bytes 7077888 | tf_op jit(solution)/shard_map/place/pallas_call | solution.py:338
  230.0 1.7 add_convert_fusion.1
  (32 shorter events, 1.0 us)
Async XLA Ops:
  50.0 5.3 %collective-permute-start.28 = (bf16[384,2304]{1,0:T(8,128)(2,1)S(1)}, bf16[384,2304]{1,0:T(8,128)(2,1)S(1)}, u32[]{:S(2)}, u32[]{:S(2)}) collective-permute-start(bf16[384,2304]{1,0:T(8,128)(2,1)S(1)} %bitcast.18), channel_id=1, source_target_pairs={{0,16},{16,0},{1,17},{17,1},{2,18},{18,2},{3,19},{19,3},{4,20},{20... | collective-permute-start | bytes 5308424 | tf_op jit(solution)/shard_map/ppermute | solution.py:416
  72.6 2.7 %collective-permute-start.31 = (bf16[384,1152]{1,0:T(8,128)(2,1)}, bf16[384,1152]{1,0:T(8,128)(2,1)S(1)}, u32[]{:S(2)}, u32[]{:S(2)}) collective-permute-start(bf16[384,1152]{1,0:T(8,128)(2,1)} %get-tuple-element.115), channel_id=1, source_target_pairs={{0,16},{16,0},{1,17},{17,1},{2,18},{18,2},{3,19},{19,3},{4,20},{20... | collective-permute-start | bytes 2654216 | tf_op jit(solution)/shard_map/ppermute | solution.py:416
  77.6 68.8 %all-to-all-start.1 = ((bf16[8,48,1152]{2,1,0:T(8,128)(2,1)}), bf16[8,48,1152]{2,1,0:T(8,128)(2,1)S(1)}, u32[]{:S(2)}, u32[]{:S(2)}) async-start(bf16[8,48,1152]{2,1,0:T(8,128)(2,1)} %bitcast.12), calls=%async_computation.1 | async-start | bytes 1769472 | tf_op jit(solution)/shard_map/all_to_all | solution.py:468
  88.9 4.4 %copy-start.2 = (bf16[1152,256]{1,0:T(8,128)(2,1)S(1)}, bf16[1152,256]{1,0:T(8,128)(2,1)}, u32[]{:S(2)}) copy-start(bf16[1152,256]{1,0:T(8,128)(2,1)} %get-tuple-element.123.refs_0_) | copy-start | bytes 1769476
  88.9 6.7 %copy-start.5 = (s32[2,128]{1,0:T(2,128)S(1)}, s32[2,128]{1,0:T(2,128)}, u32[]{:S(2)}) copy-start(s32[2,128]{1,0:T(2,128)} %get-tuple-element.113.where_ref) | copy-start | bytes 3076
  88.9 61.0 %copy-start.7 = (s32[16]{0:T(128)S(1)}, s32[16]{0:T(128)}, u32[]{:S(2)}) copy-start(s32[16]{0:T(128)} %param.30) | copy-start | bytes 196
  88.9 61.0 %copy-start.8 = (pred[16]{0:T(512)(128)(4,1)S(1)}, pred[16]{0:T(512)(128)(4,1)}, u32[]{:S(2)}) copy-start(pred[16]{0:T(512)(128)(4,1)} %constant.33.clone) | copy-start | bytes 52
  88.9 63.9 %copy-start.10 = (s32[256]{0:T(256)S(1)}, s32[256]{0:T(256)}, u32[]{:S(2)}) copy-start(s32[256]{0:T(256)} %constant.32.clone) | copy-start | bytes 3076
  88.9 64.6 %copy-start.9 = (s32[256]{0:T(256)S(1)}, s32[256]{0:T(256)}, u32[]{:S(2)}) copy-start(s32[256]{0:T(256)} %constant.31.clone) | copy-start | bytes 3076
  88.9 73.1 %collective-permute-start.29 = (bf16[576,1024]{1,0:T(8,128)(2,1)}, bf16[576,1024]{1,0:T(8,128)(2,1)}, u32[]{:S(2)}, u32[]{:S(2)}) collective-permute-start(bf16[576,1024]{1,0:T(8,128)(2,1)} %shard_map.137.refs_7_), channel_id=1, source_target_pairs={{0,1},{1,0},{2,3},{3,2},{4,5},{5,4},{6,7},{7,6},{8,9},{9,8},{10,11... | collective-permute-start | bytes 3538952 | tf_op jit(solution)/shard_map/ppermute | solution.py:493
  93.2 133.3 %collective-permute-start.33 = (bf16[1152,256]{1,0:T(8,128)(2,1)S(1)}, bf16[1152,256]{1,0:T(8,128)(2,1)S(1)}, u32[]{:S(2)}, u32[]{:S(2)}) collective-permute-start(bf16[1152,256]{1,0:T(8,128)(2,1)S(1)} %copy-done.2), channel_id=1, source_target_pairs={{0,8},{1,9},{2,10},{3,11},{4,12},{5,13},{6,14},{7,15},{8,0},{9,1},... | collective-permute-start | bytes 1769480 | tf_op jit(solution)/shard_map/ppermute | solution.py:460
  93.3 133.2 %collective-permute-start.34 = (bf16[1152,256]{1,0:T(8,128)(2,1)}, bf16[1152,256]{1,0:T(8,128)(2,1)S(1)}, u32[]{:S(2)}, u32[]{:S(2)}) collective-permute-start(bf16[1152,256]{1,0:T(8,128)(2,1)} %shard_map.138.refs_2_), channel_id=1, source_target_pairs={{0,8},{1,9},{2,10},{3,11},{4,12},{5,13},{6,14},{7,15},{8,0},{9,1},... | collective-permute-start | bytes 1769480 | tf_op jit(solution)/shard_map/ppermute | solution.py:486
  95.6 50.8 %collective-permute-start.30 = (s32[2,128]{1,0:T(2,128)S(1)}, s32[2,128]{1,0:T(2,128)S(1)}, u32[]{:S(2)}, u32[]{:S(2)}) collective-permute-start(s32[2,128]{1,0:T(2,128)S(1)} %copy-done.5), channel_id=1, source_target_pairs={{0,8},{1,9},{2,10},{3,11},{4,12},{5,13},{6,14},{7,15},{8,0},{9,1},... | collective-permute-start | bytes 3080 | tf_op jit(solution)/shard_map/ppermute | solution.py:477
  146.4 0.6 copy-start.6
  146.4 0.9 copy-start.3
  149.9 80.1 %collective-permute-start.32 = (bf16[128,1152]{1,0:T(8,128)(2,1)}, bf16[128,1152]{1,0:T(8,128)(2,1)}, u32[]{:S(2)}, u32[]{:S(2)}) collective-permute-start(bf16[128,1152]{1,0:T(8,128)(2,1)} %get-tuple-element.122), channel_id=1, source_target_pairs={{0,8},{1,9},{2,10},{3,11},{4,12},{5,13},{6,14},{7,15},{8,0},{9,1},... | collective-permute-start | bytes 884744 | tf_op jit(solution)/shard_map/ppermute | solution.py:481
  156.0 70.6 %copy-start = (bf16[576,1024]{1,0:T(8,128)(2,1)S(1)}, bf16[576,1024]{1,0:T(8,128)(2,1)}, u32[]{:S(2)}) copy-start(bf16[576,1024]{1,0:T(8,128)(2,1)} %shard_map.137.refs_7_) | copy-start | bytes 3538948
  156.0 70.6 %copy-start.1 = (bf16[1152,256]{1,0:T(8,128)(2,1)S(1)}, bf16[1152,256]{1,0:T(8,128)(2,1)}, u32[]{:S(2)}) copy-start(bf16[1152,256]{1,0:T(8,128)(2,1)} %shard_map.138.refs_2_) | copy-start | bytes 1769476
  162.0 54.4 %collective-permute-start.2 = (bf16[576,1024]{1,0:T(8,128)(2,1)}, bf16[576,1024]{1,0:T(8,128)(2,1)}, u32[]{:S(2)}, u32[]{:S(2)}) collective-permute-start(bf16[576,1024]{1,0:T(8,128)(2,1)} %get-tuple-element.58), channel_id=1, source_target_pairs={{3,11},{11,3},{7,15},{15,7},{19,27},{27,19},{23,31},{31,23}} | collective-permute-start | bytes 3538952 | tf_op jit(solution)/shard_map/cond/branch_1_fun/ppermute | solution.py:502
  166.3 56.8 %collective-permute-start.3 = (bf16[576,1024]{1,0:T(8,128)(2,1)}, bf16[576,1024]{1,0:T(8,128)(2,1)}, u32[]{:S(2)}, u32[]{:S(2)}) collective-permute-start(bf16[576,1024]{1,0:T(8,128)(2,1)} %get-tuple-element.59), channel_id=1, source_target_pairs={{2,11},{10,3},{6,15},{14,7},{18,27},{26,19},{22,31},{30,23}} | collective-permute-start | bytes 3538952 | tf_op jit(solution)/shard_map/cond/branch_1_fun/ppermute | solution.py:503
  223.0 3.5 %collective-permute-start.14 = (bf16[576,1024]{1,0:T(8,128)(2,1)}, bf16[576,1024]{1,0:T(8,128)(2,1)}, u32[]{:S(2)}, u32[]{:S(2)}) collective-permute-start(bf16[576,1024]{1,0:T(8,128)(2,1)} %get-tuple-element.70), channel_id=1, source_target_pairs={{0,8},{8,0},{1,9},{9,1},{16,24},{24,16},{17,25},{25,17}} | collective-permute-start | bytes 3538952 | tf_op jit(solution)/shard_map/cond/branch_0_fun/ppermute | solution.py:502
  224.8 1.7 collective-permute-start.15
  226.5 3.5 %copy-start.4 = (bf16[128,1152]{1,0:T(8,128)(2,1)S(1)}, bf16[128,1152]{1,0:T(8,128)(2,1)}, u32[]{:S(2)}) copy-start(bf16[128,1152]{1,0:T(8,128)(2,1)} %get-tuple-element.121) | copy-start | bytes 884740
